TPU v7x, 512 devices: a whole 4x8x8 slice. The times are simulated.
512 devices in a mesh: ex: 64 (over y, z_hi, core), feat: 8 (over x, z_lo).
Axes of the slice: x: 4, y: 8, z: 8 (z_hi: 4, z_lo: 2; z = z_hi * 2 + z_lo), core: 2. Of those that a mesh axis runs over, the one named last changes fastest.
Arguments:
- proj_inputs: bfloat16 [2, 2048, 24, 2048], P(None, 'ex', None, 'feat'), may hold values from -6 to 6
- out_cotangent: bfloat16 [2, 2048, 24, 4096], P(None, 'ex', None, 'feat'), may hold values from -200 to 200
- seq_lengths: int32 [2048], P('ex'), may hold values from 6 to 24, as said below
- frozen_adapter: bfloat16 [2, 128, 2048], P(None, None, 'feat'), may hold values from -0.125 to 0.125
- left_factor: bfloat16 [2, 512, 4096], P(None, None, 'feat'), may hold values from -0.09375 to 0.09375
- right_factor: bfloat16 [2, 128, 16], replicated, may hold values from -0.5 to 0.5
- valid_grads: bfloat16 [256, 8192], P('ex', 'feat'), may hold values from -200 to 200
Outputs:
- scores: float32 [2048, 256], P('ex')
Inputs may be any that keep to these rules, and one draw needn't show every extreme that they name: Tokens at positions below seq_lengths are live; in every aligned block of 32 examples one example has all 24 tokens live and one has the fewest allowed.
All inputs are finite; a program needn't handle non-finite values.
Results may differ from a plain program's by a relative error of at most 0.0037.
Values may be sent and summed in bfloat16 or wider, within the bound.
No kernel may reach another device: no remote copies, remote signals or barrier semaphores. Data moves between devices by JAX's collectives and lax.ppermute only.
A program may use at most 64 MiB of HBM per device.

v0:
```python
import math

import jax
import jax.numpy as jnp
from jax import lax
from jax.sharding import PartitionSpec as P


def body(
    proj_inputs, out_cotangent, seq_lengths, frozen_adapter, left_factor, right_factor, valid_grads
):
    highest = lax.Precision.HIGHEST
    layer_count, example_count, token_count, _ = proj_inputs.shape
    feat_count = lax.axis_size("feat")
    proj_count = right_factor.shape[2]
    owned_rows = left_factor.shape[1] // feat_count
    position = jnp.arange(token_count, dtype=jnp.int32)
    live_tokens = (position[None, :] < seq_lengths[:, None]).astype(jnp.float32)
    adapted = jnp.einsum(
        "lesh,lrh->lesr", proj_inputs, frozen_adapter, preferred_element_type=jnp.float32
    )
    right_wide = right_factor.astype(jnp.float32)
    adapted = lax.psum(adapted, "feat")
    right_rows = jnp.einsum("lesr,lrb->lesb", adapted, right_wide, precision=highest)
    right_rows = (right_rows * live_tokens[None, :, :, None]).astype(jnp.bfloat16)
    flat_cotan = out_cotangent.reshape(
        layer_count, example_count * token_count, out_cotangent.shape[3]
    )
    term = jnp.einsum("lkd,ltd->klt", left_factor, flat_cotan, preferred_element_type=jnp.float32)
    left_rows = lax.psum_scatter(
        term.reshape(lax.axis_size("feat") * owned_rows, layer_count * example_count * token_count),
        "feat",
        scatter_dimension=0,
        tiled=True,
    )
    own_rows = left_rows.shape[0]
    left_rows = left_rows.reshape(own_rows, layer_count, example_count, token_count)
    projected = jnp.einsum(
        "kles,lesb->ekb", left_rows, right_rows.astype(jnp.float32), precision=highest
    )
    projected = projected.reshape(example_count, own_rows * proj_count)
    train_squares = jnp.sum(projected * projected, axis=1)
    rounded = projected.astype(jnp.bfloat16)
    scaling = math.sqrt(valid_grads.shape[1] * feat_count)
    valid_wide = valid_grads.astype(jnp.float32)
    valid_squares = jnp.sum(valid_wide * valid_wide, axis=1)
    products = jnp.einsum(
        "ek,vk->ev",
        lax.all_gather(rounded, "ex", axis=0, tiled=True),
        valid_grads,
        preferred_element_type=jnp.float32,
    )
    products, valid_squares, train_squares = lax.psum(
        (products, valid_squares, train_squares), "feat"
    )
    products = products / jnp.sqrt(valid_squares + 1e-06)[None, :]
    products = lax.all_to_all(products, "ex", split_axis=0, concat_axis=1, tiled=True)
    return scaling * products / jnp.sqrt(train_squares + 1e-06)[:, None]


def solution(mesh):
    return jax.shard_map(
        body,
        mesh=mesh,
        in_specs=(
            P(None, "ex", None, "feat"),
            P(None, "ex", None, "feat"),
            P("ex"),
            P(None, None, "feat"),
            P(None, None, "feat"),
            P(),
            P("ex", "feat"),
        ),
        out_specs=P("ex", None),
        check_vma=False,
    )
```

profile of v0, /device:TPU:1, one launch (start us, length us, event | category | flops | bytes accessed | tf_op | source)
XLA Modules:
  0.0 342.0 jit_solution(11740228024214441054)
XLA Ops:
  6.5 0.0 copy-start
  6.5 2.5 fusion.3
  9.1 0.0 all-reduce.3.cloned.1.call-update
  9.1 0.0 reduce-scatter.4.cloned.1.call-start
  9.2 2.7 fusion.7
  11.9 3.5 %copy.20 = f32[512,1536]{1,0:T(8,128)} copy(f32[512,1536]{0,1:T(8,128)} %bitcast.34) | data formatting | bytes 6291456
  15.4 0.0 reduce-scatter.4.cloned.1.call-update
  15.5 0.0 all-gather.2.cloned.1.call-start
  15.5 0.6 copy-done.4
  16.1 0.1 fusion.5
  16.2 83.7 %all-reduce.3.cloned.1.call-done = f32[2,32,24,128]{3,2,1,0:T(8,128)} async-done(((f32[2,32,24,128]{3,2,1,0:T(8,128)}), f32[2,32,24,128]{3,2,1,0:T(8,128)}) %all-reduce.3.cloned.1.call-update) | async-done | bytes 786448 | tf_op jit(solution)/shard_map/psum | solution.py:23
  99.8 3.2 fusion
  103.0 80.2 %reduce-scatter.4.cloned.1.call-done = f32[64,1536]{1,0:T(8,128)} async-done(((f32[512,1536]{1,0:T(8,128)}), f32[64,1536]{1,0:T(8,128)}) %reduce-scatter.4.cloned.1.call-update) | async-done | bytes 393232
  183.2 1.3 copy.21
  184.5 0.8 multiply_reduce_fusion
  185.3 0.3 copy.15
  185.6 0.8 copy.16
  186.3 0.0 all-gather.2.cloned.1.call-update
  186.4 0.1 multiply_reduce_fusion.1
  186.5 88.7 %all-gather.2.cloned.1.call-done = bf16[2048,1024]{1,0:T(8,128)(2,1)} async-done(((bf16[32,1024]{1,0:T(8,128)(2,1)}), bf16[2048,1024]{1,0:T(8,128)(2,1)}) %all-gather.2.cloned.1.call-update) | async-done | bytes 4194320 | tf_op jit(solution)/shard_map/all_gather | solution.py:49
  275.2 3.4 fusion.8
  278.6 28.1 %all-reduce = (f32[2048,4]{0,1:T(4,128)S(1)}, f32[4]{0:T(128)S(1)}, f32[32]{0:T(128)S(1)}) all-reduce(f32[2048,4]{0,1:T(4,128)S(1)} %fusion.8, f32[4]{0:T(128)S(1)} %multiply_reduce_fusion.1, f32[32]{0:T(128)S(1)} %get-tuple-element.8), channel_id=1, replica_groups=mesh['ex'=64,'feat'=8] {'feat'}, use_global_device_ids=true, to_apply=%region_2.0 | all-reduce | flops 8228 | bytes 65824 | tf_op jit(solution)/shard_map/psum | solution.py:53
  306.7 0.1 broadcast_divide_fusion.1
  306.7 0.1 all_to_all.10
  306.8 0.1 copy.29
  306.9 0.8 reshape.48
  307.7 13.9 %all-to-all-start = ((f32[64,1,128]{2,1,0:T(1,128)}), f32[64,1,128]{2,1,0:T(1,128)S(1)}, u32[]{:S(2)}, u32[]{:S(2)}) async-start(f32[64,1,128]{2,1,0:T(1,128)} %reshape.48), calls=%async_computation | async-start | bytes 65536 | tf_op jit(solution)/shard_map/all_to_all | solution.py:57
  321.7 11.7 %all-to-all-done = f32[64,1,128]{2,1,0:T(1,128)S(1)} async-done(((f32[64,1,128]{2,1,0:T(1,128)}), f32[64,1,128]{2,1,0:T(1,128)S(1)}, u32[]{:S(2)}, u32[]{:S(2)}) %all-to-all-start) | async-done | bytes 32800 | tf_op jit(solution)/shard_map/all_to_all | solution.py:57
  333.4 0.5 broadcast.25
  333.9 0.7 reduce.1
  334.6 0.1 reshape.49
  334.8 0.7 copy.18
  (13 shorter events, 0.1 us)
Async XLA Ops:
  6.5 2.6 copy-start
  6.5 2.6 copy-start.1
  6.5 93.3 %all-reduce.3.cloned.1.call-start = ((), (), s32[]{:S(2)}) async-start(), calls=%async_computation.2 | async-start | bytes 1572864 | tf_op jit(solution)/shard_map/psum | solution.py:23
  9.1 174.1 %reduce-scatter.4.cloned.1.call-start = ((), (), s32[]{:S(2)}) async-start(), calls=%async_computation.4 | async-start | bytes 3538944
  15.4 0.7 copy-start.4
  15.4 84.4 %copy-start.3 = (bf16[2,128,16]{1,2,0:T(8,128)(2,1)S(1)}, bf16[2,128,16]{1,2,0:T(8,128)(2,1)}, u32[]{:S(2)}) copy-start(bf16[2,128,16]{1,2,0:T(8,128)(2,1)} %param.12) | copy-start | bytes 24580
  15.4 170.9 %copy-start.2 = (bf16[4,1024]{1,0:T(4,128)(2,1)S(1)}, bf16[4,1024]{1,0:T(4,128)(2,1)}, u32[]{:S(2)}) copy-start(bf16[4,1024]{1,0:T(4,128)(2,1)} %param.13) | copy-start | bytes 24580
  15.5 259.8 %all-gather.2.cloned.1.call-start = ((), (), s32[]{:S(2)}) async-start(), calls=%async_computation.3 | async-start | bytes 4259840 | tf_op jit(solution)/shard_map/all_gather | solution.py:49
  307.7 25.7 %all-to-all-start = ((f32[64,1,128]{2,1,0:T(1,128)}), f32[64,1,128]{2,1,0:T(1,128)S(1)}, u32[]{:S(2)}, u32[]{:S(2)}) async-start(f32[64,1,128]{2,1,0:T(1,128)} %reshape.48), calls=%async_computation | async-start | bytes 65536 | tf_op jit(solution)/shard_map/all_to_all | solution.py:57
Sparse Core Ops, SparseCore 0:
  10.3 89.4 all-reduce.2
  102.7 80.5 reduce-scatter.3
  186.5 88.6 all-gather.1
where the time goes:
time: 342 us
  waiting for transfers between devices  264 us (77%)
  blocking collectives  28.1 us (8%)
  starting transfers between devices  14 us (4%)
  between operations  13.2 us (4%)
  matrix products  12.6 us (4%)
  local copies, waits for them, and re-layouts  8.7 us (3%)
    all_gather x1, waiting for transfers between devices, body(): lax.all_gather(rounded, 'ex', axis=0, tiled=True)  88.7 us
    psum x1, waiting for transfers between devices, body(): adapted = lax.psum(adapted, 'feat')  83.7 us
    unnamed x4, waiting for transfers between devices  80.3 us
    psum x1, blocking collectives, body(): lax.psum((products, valid_squares, train_squares), 'feat')  28.1 us
    all_to_all x1, starting transfers between devices, body(): lax.all_to_all(products, 'ex', split_axis=0, concat_axis=1, tiled=True)  13.9 us
    all_to_all x1, waiting for transfers between devices, body(): lax.all_to_all(products, 'ex', split_axis=0, concat_axis=1, tiled=True)  11.7 us
  transfers between devices with their start and end apart: 4, of which 4 were waited for; matrix products, arithmetic and copies ran while one was open for 3% of the time, Pallas kernels for 0%

commit v1 on v0

v1 whole, which is shorter than its diff:
```python
import math

import jax
import jax.numpy as jnp
from jax import lax
from jax.experimental import pallas as pl
from jax.experimental.pallas import tpu as pltpu
from jax.sharding import PartitionSpec as P

F32 = jnp.float32
BF16 = jnp.bfloat16
GROUP = 4
NT = (((1,), (1,)), ((), ()))
NN = (((1,), (0,)), ((), ()))
TN = (((0,), (0,)), ((), ()))


def dot(a, b, dims):
    return lax.dot_general(a, b, dims, preferred_element_type=F32)


def split(x):
    high = x.astype(BF16)
    return high, (x - high.astype(F32)).astype(BF16)


def call(kernel, out_shape, flops, bytes_accessed, name, scratch=(), smem=0, args=()):
    specs = [pl.BlockSpec(memory_space=pltpu.SMEM)] * smem
    specs += [pl.BlockSpec(memory_space=pltpu.VMEM)] * (len(args) - smem)
    return pl.pallas_call(
        kernel,
        out_shape=out_shape,
        in_specs=specs,
        out_specs=jax.tree.map(lambda _: pl.BlockSpec(memory_space=pltpu.VMEM), out_shape),
        scratch_shapes=list(scratch),
        cost_estimate=pl.CostEstimate(flops=flops, bytes_accessed=bytes_accessed, transcendentals=0),
        name=name,
    )(*args)


def right_kernel(x_ref, a_ref, r_ref, out_ref):
    peers = out_ref.shape[0]
    layers = x_ref.shape[0]
    proj = r_ref.shape[2]
    for l in range(layers):
        mix = dot(r_ref[l], a_ref[l], TN)
        high, low = split(mix)
        both = jnp.concatenate([high, low], axis=0)
        rows = dot(both, x_ref[l], NT)
        rows = (rows[:proj] + rows[proj:]).astype(BF16)
        for p in range(peers):
            out_ref[p, l * proj:(l + 1) * proj, :] = rows


def left_kernel(c_ref, l_ref, high_ref, low_ref):
    layers, tokens, _ = c_ref.shape
    step = 256
    for l in range(layers):
        for t in range(0, tokens, step):
            high, low = split(dot(c_ref[l, t:t + step, :], l_ref[l], NT))
            high_ref[l, t:t + step, :] = high
            low_ref[l, t:t + step, :] = low


def project_kernel(seq_ref, rr_ref, high_ref, low_ref, out_ref):
    peers, two_proj, tokens = rr_ref.shape
    layers, _, kl = high_ref.shape
    proj = two_proj // layers
    half = proj // 2
    owned = kl // peers
    examples = seq_ref.shape[0]
    seq = tokens // examples
    span = GROUP * seq
    width = 2 * 128
    total = rr_ref[0].astype(F32)
    for p in range(1, peers):
        total = total + rr_ref[p].astype(F32)
    first = total[:proj]
    second = total[proj:]
    lane = lax.broadcasted_iota(jnp.int32, (proj, width), 1)
    out_lane = lax.broadcasted_iota(jnp.int32, (GROUP * half, 128), 1)
    for g in range(examples // GROUP):
        x0 = first if g == 0 else pltpu.roll(first, (tokens - g * span) % tokens, 1)
        x1 = pltpu.roll(second, (tokens + span - g * span) % tokens, 1)
        x0, x1 = x0[:, :width], x1[:, :width]
        blocks = []
        for i in range(GROUP):
            start = i * seq
            stop = start + seq_ref[g * GROUP + i]
            mask0 = (lane >= start) & (lane < stop)
            mask1 = (lane >= start + span) & (lane < stop + span)
            blocks.append(jnp.where(mask0, x0, jnp.where(mask1, x1, 0.0)))
        spread = jnp.concatenate(blocks, axis=0)
        high, low = split(spread)
        both = jnp.concatenate([high, low], axis=0)[:, :layers * span]
        high = high[:, :layers * span]
        t = g * span
        left_high = jnp.concatenate([high_ref[l, t:t + span, :] for l in range(layers)], axis=0)
        left_low = jnp.concatenate([low_ref[l, t:t + span, :] for l in range(layers)], axis=0)
        rows = GROUP * proj
        part = dot(both, left_high, NN)
        part = part[:rows] + part[rows:] + dot(high, left_low, NN)
        part = part.reshape(GROUP, 2, half, kl)
        even = part[:, 0].reshape(GROUP * half, kl)
        odd = part[:, 1].reshape(GROUP * half, kl)
        for p in range(peers):
            tile = (p * owned) // 128 * 128
            e = even[:, tile:tile + 128]
            o = odd[:, tile:tile + 128]
            if (p * owned) % 128 == 0:
                o = pltpu.roll(o, 64, 1)
            else:
                e = pltpu.roll(e, 64, 1)
            both_k = jnp.where(out_lane < 64, e, o)
            r = g * GROUP * half
            out_ref[p, r:r + GROUP * half, :] = both_k.astype(BF16)


def product_kernel(part_ref, valid_ref, squares_ref, out_ref, sum_ref):
    peers, rows, _ = part_ref.shape
    valid_count = valid_ref.shape[0]
    examples = rows // 8
    total = part_ref[0].astype(F32)
    for p in range(1, peers):
        total = total + part_ref[p].astype(F32)
    sum_ref[...] = total
    squares = jnp.sum((total * total).reshape(examples, 8, 128), axis=1)
    squares = jnp.sum(squares, axis=1, keepdims=True)
    row = lax.broadcasted_iota(jnp.int32, (examples, valid_count), 0)
    column = lax.broadcasted_iota(jnp.int32, (examples, valid_count), 1)
    train = jnp.sum(jnp.where(row == column, squares, 0.0), axis=0, keepdims=True)
    acc = jnp.zeros((2 * examples, valid_count), F32)
    for b in range(8):
        block = sum_ref[pl.ds(b, examples, stride=8), :]
        high, low = split(block)
        both = jnp.concatenate([high, low], axis=0)
        acc = acc + dot(both, valid_ref[:, b * 128:(b + 1) * 128], NT)
    products = acc[:examples] + acc[examples:]
    tail_row = lax.broadcasted_iota(jnp.int32, (8, valid_count), 0)
    tail = jnp.where(tail_row == 0, squares_ref[...], jnp.where(tail_row == 1, train, 0.0))
    for p in range(peers):
        out_ref[p, :examples, :] = products
        out_ref[p, examples:, :] = tail


def score_kernel(scaling, part_ref, out_ref):
    peers = part_ref.shape[0]
    examples, valid_count = out_ref.shape
    total = part_ref[0]
    for p in range(1, peers):
        total = total + part_ref[p]
    products = total[:examples]
    valid = jnp.sqrt(total[examples:examples + 1] + 1e-06)
    row = lax.broadcasted_iota(jnp.int32, (examples, valid_count), 0)
    column = lax.broadcasted_iota(jnp.int32, (examples, valid_count), 1)
    train = jnp.where(row == column, total[examples + 1:examples + 2], 0.0)
    train = jnp.sqrt(jnp.sum(train, axis=1, keepdims=True) + 1e-06)
    out_ref[...] = scaling * products / (train * valid)


def body(proj_inputs, out_cotangent, seq_lengths, frozen_adapter, left_factor, right_factor, valid_grads):
    layers, examples, seq, inputs = proj_inputs.shape
    width = out_cotangent.shape[3]
    peers = lax.axis_size("feat")
    groups = lax.axis_size("ex")
    proj = right_factor.shape[2]
    kl = left_factor.shape[1]
    tokens = examples * seq
    owned = kl // peers
    valid_count = valid_grads.shape[0] * groups
    scaling = math.sqrt(kl * proj)

    own_valid = valid_grads.reshape(-1, owned, 2, 8).transpose(0, 3, 2, 1).reshape(1, -1, owned * proj)
    own_valid = jnp.broadcast_to(own_valid, (groups,) + own_valid.shape[1:])
    valid = lax.all_to_all(own_valid, "ex", 0, 0, tiled=True).reshape(valid_count, owned * proj)
    valid_wide = valid.astype(F32)
    valid_squares = jnp.sum(valid_wide * valid_wide, axis=1)[None, :]

    right_parts = call(
        right_kernel,
        jax.ShapeDtypeStruct((peers, layers * proj, tokens), BF16),
        2 * layers * tokens * inputs * 256,
        proj_inputs.size * 2,
        "right_rows",
        args=(proj_inputs.reshape(layers, tokens, inputs), frozen_adapter, right_factor),
    )
    right_parts = lax.all_to_all(right_parts, "feat", 0, 0, tiled=True)

    left_shape = jax.ShapeDtypeStruct((layers, tokens, kl), BF16)
    left_high, left_low = call(
        left_kernel,
        (left_shape, left_shape),
        2 * layers * tokens * width * kl,
        (out_cotangent.size + left_factor.size) * 2 + layers * tokens * kl * 4,
        "left_rows",
        args=(out_cotangent.reshape(layers, tokens, width), left_factor),
    )
    parts = call(
        project_kernel,
        jax.ShapeDtypeStruct((peers, examples * 8, 128), BF16),
        2 * layers * tokens * kl * 256,
        layers * tokens * kl * 4,
        "project",
        smem=1,
        args=(seq_lengths, right_parts, left_high, left_low),
    )
    parts = lax.all_to_all(parts, "feat", 0, 0, tiled=True)
    products = call(
        product_kernel,
        jax.ShapeDtypeStruct((peers, examples + 8, valid_count), F32),
        4 * examples * valid_count * owned * proj,
        parts.size * 2 + valid.size * 2,
        "products",
        scratch=(pltpu.VMEM((examples * 8, 128), F32),),
        args=(parts, valid, valid_squares),
    )
    products = lax.all_to_all(products, "feat", 0, 0, tiled=True)

    def score(part_ref, out_ref):
        score_kernel(scaling, part_ref, out_ref)

    return call(
        score,
        jax.ShapeDtypeStruct((examples, valid_count), F32),
        examples * valid_count * 16,
        products.size * 4,
        "scores",
        args=(products,),
    )


def solution(mesh):
    return jax.shard_map(
        body,
        mesh=mesh,
        in_specs=(
            P(None, "ex", None, "feat"),
            P(None, "ex", None, "feat"),
            P("ex"),
            P(None, None, "feat"),
            P(None, None, "feat"),
            P(),
            P("ex", "feat"),
        ),
        out_specs=P("ex", None),
        check_vma=False,
    )
```

time: 342 us -> 86.2 us (0.25)
  waiting for transfers between devices: 264 us -> 26.3 us
  blocking collectives: 28.1 us -> 11.2 us
  Pallas kernels: 0 us -> 14.5 us
  starting transfers between devices: 14 us -> 28.2 us
  between operations: 13.2 us -> 0.04 us
  matrix products: 12.6 us -> 0 us
  local copies, waits for them, and re-layouts: 8.7 us -> 5.13 us
    all_gather x1 -> x0, waiting for transfers between devices: 88.7 us -> none  [body(): lax.all_gather(rounded, 'ex', axis=0, tiled=True)]
    psum x1 -> x0, waiting for transfers between devices: 83.7 us -> none  [body(): adapted = lax.psum(adapted, 'feat')]
    unnamed x4 -> x0, waiting for transfers between devices: 80.3 us -> none
    psum x1 -> x0, blocking collectives: 28.1 us -> none  [body(): lax.psum((products, valid_squares, train_squares), 'feat')]
    all_to_all x1 -> x3, waiting for transfers between devices: 11.7 us -> 26.3 us  [the longest x1 11.6 us: body(): lax.all_to_all(own_valid, 'ex', 0, 0, tiled=True)]
    pallas_call x0 -> x5, Pallas kernels: none -> 14.5 us  [call(): pl.pallas_call(kernel, out_shape=out_shape, in_specs=specs, out_specs=jax...]
    all_to_all x1 -> x3, starting transfers between devices: 13.9 us -> 28.2 us  [the longest x1 18 us: body(): lax.all_to_all(own_valid, 'ex', 0, 0, tiled=True)]
    dot_general x5 -> x0, matrix products: 12.6 us -> none  [the longest x1 3.37 us: body(): jnp.einsum('ek,vk->ev', lax.all_gather(rounded, 'ex', axis=0, tiled=True)...]
  transfers between devices with their start and end apart: 4 -> 3, of which waited for: 4 -> 3; matrix products, arithmetic and copies ran while one was open for 3% -> 3% of each run, Pallas kernels for 0% -> 9%
where the time goes in v1:
time: 86.2 us; the launch traced here: 85.6 us
  starting transfers between devices  28.2 us (33%)
  waiting for transfers between devices  26.3 us (31%)
  Pallas kernels  14.5 us (17%)
  blocking collectives  11.2 us (13%)
  local copies, waits for them, and re-layouts  5.13 us (6%)
    all_to_all x1, starting transfers between devices, body(): lax.all_to_all(own_valid, 'ex', 0, 0, tiled=True)  18 us
    pallas_call x5, Pallas kernels, call(): pl.pallas_call(kernel, out_shape=out_shape, in_specs=specs, out_specs=jax...  14.5 us
    all_to_all x1, waiting for transfers between devices, body(): lax.all_to_all(own_valid, 'ex', 0, 0, tiled=True)  11.6 us
    all_to_all x1, blocking collectives, body(): products = lax.all_to_all(products, 'feat', 0, 0, tiled=True)  11.2 us
    all_to_all x1, waiting for transfers between devices, body(): parts = lax.all_to_all(parts, 'feat', 0, 0, tiled=True)  8.18 us
    all_to_all x1, starting transfers between devices, body(): right_parts = lax.all_to_all(right_parts, 'feat', 0, 0, tiled=True)  6.65 us
    all_to_all x1, waiting for transfers between devices, body(): right_parts = lax.all_to_all(right_parts, 'feat', 0, 0, tiled=True)  6.45 us
    all_to_all x1, starting transfers between devices, body(): parts = lax.all_to_all(parts, 'feat', 0, 0, tiled=True)  3.49 us
  transfers between devices with their start and end apart: 3, of which 3 were waited for; matrix products, arithmetic and copies ran while one was open for 3% of the time, Pallas kernels for 9%

profile of v1, /device:TPU:1, one launch (start us, length us, event | category | flops | bytes accessed | tf_op | source)
XLA Modules:
  0.0 85.6 jit_solution(1463239065538387392)
XLA Ops:
  0.0 0.0 copy-start.2
  0.0 1.4 %copy.9.r_ref = bf16[2,128,16]{2,1,0:T(8,128)(2,1)} copy(bf16[2,128,16]{1,2,0:T(8,128)(2,1)} %param.12) | data formatting | bytes 16384 | tf_op args[5]
  1.4 2.5 %right_rows.1 = bf16[8,32,768]{2,1,0:T(8,128)(2,1)} custom-call(bf16[2,768,256]{2,1,0:T(8,128)(2,1)} %bitcast.3, bf16[2,128,256]{2,1,0:T(8,128)(2,1)} %a_ref.1, bf16[2,128,16]{2,1,0:T(8,128)(2,1)} %copy.9.r_ref), custom_call_target="tpu_custom_call" | custom-call | flops 201326592 | bytes 786432 | tf_op jit(solution)/shard_map/right_rows/pallas_call | solution.py:30
  3.9 6.6 %all-to-all-start = ((bf16[8,32,768]{2,1,0:T(8,128)(2,1)}), bf16[8,32,768]{2,1,0:T(8,128)(2,1)S(1)}, u32[]{:S(2)}, u32[]{:S(2)}) async-start(bf16[8,32,768]{2,1,0:T(8,128)(2,1)} %right_rows.1), calls=%async_computation | async-start | bytes 786432 | tf_op jit(solution)/shard_map/all_to_all | solution.py:187
  10.5 0.0 copy-done.2
  10.6 0.2 reshape.18
  10.7 0.1 copy.10
  10.8 0.1 broadcast_in_dim.10
  10.9 6.4 %all-to-all-done.rr_ref = bf16[8,32,768]{2,1,0:T(8,128)(2,1)S(1)} async-done(((bf16[8,32,768]{2,1,0:T(8,128)(2,1)}), bf16[8,32,768]{2,1,0:T(8,128)(2,1)S(1)}, u32[]{:S(2)}, u32[]{:S(2)}) %all-to-all-start) | async-done | bytes 393248 | tf_op jit(solution)/shard_map/all_to_all | solution.py:187
  17.4 0.0 copy-start.1
  17.4 0.9 %broadcast_in_dim.11 = bf16[64,4,1024]{2,1,0:T(4,128)(2,1)} broadcast(bf16[4,1024]{1,0:T(4,128)(2,1)S(1)} %broadcast_in_dim.10), dimensions={1,2} | broadcast | bytes 532480 | tf_op jit(solution)/shard_map/broadcast_in_dim | solution.py:174
  18.3 18.0 %all-to-all-start.2 = ((bf16[64,4,1024]{2,1,0:T(4,128)(2,1)}), bf16[64,4,1024]{2,1,0:T(4,128)(2,1)S(1)}, u32[]{:S(2)}, u32[]{:S(2)}) async-start(bf16[64,4,1024]{2,1,0:T(4,128)(2,1)} %broadcast_in_dim.11), calls=%async_computation.2 | async-start | bytes 1048576 | tf_op jit(solution)/shard_map/all_to_all | solution.py:175
  36.4 4.4 %left_rows.1 = (bf16[2,768,512]{2,1,0:T(8,128)(2,1)}, bf16[2,768,512]{2,1,0:T(8,128)(2,1)}) custom-call(bf16[2,768,512]{2,1,0:T(8,128)(2,1)} %bitcast.5, bf16[2,512,512]{2,1,0:T(8,128)(2,1)} %l_ref.1), custom_call_target="tpu_custom_call" | custom-call | flops 805306368 | bytes 5767168 | tf_op jit(solution)/shard_map/left_rows/pallas_call | solution.py:30
  40.7 0.0 copy-done.1
  40.7 3.7 %project.1 = bf16[8,256,128]{2,1,0:T(8,128)(2,1)} custom-call(s32[32]{0:T(128)} %seq_ref.1, bf16[8,32,768]{2,1,0:T(8,128)(2,1)} %copy-done.1, bf16[2,768,512]{2,1,0:T(8,128)(2,1)} %get-tuple-element.7.high_ref, bf16[2,768,512]{2,1,0:T(8,128)(2,1)} %get-tuple-element.8.low_ref), custom_call_target="tpu_custom_call" | custom-call | flops 402653184 | bytes 3145728 | tf_op jit(solution)/shard_map/project/pallas_call | solution.py:30
  44.4 11.6 %all-to-all-done.2 = bf16[64,4,1024]{2,1,0:T(4,128)(2,1)S(1)} async-done(((bf16[64,4,1024]{2,1,0:T(4,128)(2,1)}), bf16[64,4,1024]{2,1,0:T(4,128)(2,1)S(1)}, u32[]{:S(2)}, u32[]{:S(2)}) %all-to-all-start.2) | async-done | bytes 524320 | tf_op jit(solution)/shard_map/all_to_all | solution.py:175
  56.0 3.5 %all-to-all-start.1 = ((bf16[8,256,128]{2,1,0:T(8,128)(2,1)}), bf16[8,256,128]{2,1,0:T(8,128)(2,1)S(1)}, u32[]{:S(2)}, u32[]{:S(2)}) async-start(bf16[8,256,128]{2,1,0:T(8,128)(2,1)} %project.1), calls=%async_computation.1 | async-start | bytes 1048576 | tf_op jit(solution)/shard_map/all_to_all | solution.py:207
  59.5 0.3 multiply_reduce_fusion
  59.9 0.7 broadcast_in_dim.12.squares_ref
  60.5 0.9 %reshape.19.valid_ref = bf16[256,1024]{1,0:T(8,128)(2,1)} reshape(bf16[64,4,1024]{2,1,0:T(4,128)(2,1)S(1)} %all-to-all-done.2) | data formatting | bytes 1048576 | tf_op jit(solution)/shard_map/reshape | solution.py:175
  61.4 8.2 %all-to-all-done.1.part_ref = bf16[8,256,128]{2,1,0:T(8,128)(2,1)S(1)} async-done(((bf16[8,256,128]{2,1,0:T(8,128)(2,1)}), bf16[8,256,128]{2,1,0:T(8,128)(2,1)S(1)}, u32[]{:S(2)}, u32[]{:S(2)}) %all-to-all-start.1) | async-done | bytes 524320 | tf_op jit(solution)/shard_map/all_to_all | solution.py:207
  69.6 0.0 copy-start
  69.6 0.8 copy-done
  70.4 2.3 %products.1 = f32[8,40,256]{2,1,0:T(8,128)} custom-call(bf16[8,256,128]{2,1,0:T(8,128)(2,1)} %copy-done, bf16[256,1024]{1,0:T(8,128)(2,1)} %reshape.19.valid_ref, f32[1,256]{1,0:T(1,128)} %broadcast_in_dim.12.squares_ref), custom_call_target="tpu_custom_call" | custom-call | flops 33554432 | bytes 1048576 | tf_op jit(solution)/shard_map/products/pallas_call | solution.py:30
  72.7 11.2 %all_to_all.20.part_ref = f32[8,40,256]{2,1,0:T(8,128)} all-to-all(f32[8,40,256]{2,1,0:T(8,128)} %products.1), channel_id=1, replica_groups=mesh['ex'=64,'feat'=8] {'feat'}, dimensions={0} | all-to-all | bytes 655360 | tf_op jit(solution)/shard_map/all_to_all | solution.py:217
  83.9 1.7 %scores.1 = f32[32,256]{1,0:T(8,128)} custom-call(f32[8,40,256]{2,1,0:T(8,128)} %all_to_all.20.part_ref), custom_call_target="tpu_custom_call" | custom-call | flops 131072 | bytes 327680 | tf_op jit(solution)/shard_map/scores/pallas_call | solution.py:30
Async XLA Ops:
  0.0 10.5 %copy-start.2 = (bf16[4,1024]{1,0:T(4,128)(2,1)S(1)}, bf16[4,1024]{1,0:T(4,128)(2,1)}, u32[]{:S(2)}) copy-start(bf16[4,1024]{1,0:T(4,128)(2,1)} %param.13) | copy-start | bytes 24580
  3.9 13.5 %all-to-all-start = ((bf16[8,32,768]{2,1,0:T(8,128)(2,1)}), bf16[8,32,768]{2,1,0:T(8,128)(2,1)S(1)}, u32[]{:S(2)}, u32[]{:S(2)}) async-start(bf16[8,32,768]{2,1,0:T(8,128)(2,1)} %right_rows.1), calls=%async_computation | async-start | bytes 786432 | tf_op jit(solution)/shard_map/all_to_all | solution.py:187
  17.4 23.3 %copy-start.1 = (bf16[8,32,768]{2,1,0:T(8,128)(2,1)}, bf16[8,32,768]{2,1,0:T(8,128)(2,1)S(1)}, u32[]{:S(2)}) copy-start(bf16[8,32,768]{2,1,0:T(8,128)(2,1)S(1)} %all-to-all-done.rr_ref) | copy-start | bytes 1179652
  18.3 37.7 %all-to-all-start.2 = ((bf16[64,4,1024]{2,1,0:T(4,128)(2,1)}), bf16[64,4,1024]{2,1,0:T(4,128)(2,1)S(1)}, u32[]{:S(2)}, u32[]{:S(2)}) async-start(bf16[64,4,1024]{2,1,0:T(4,128)(2,1)} %broadcast_in_dim.11), calls=%async_computation.2 | async-start | bytes 1048576 | tf_op jit(solution)/shard_map/all_to_all | solution.py:175
  56.0 13.6 %all-to-all-start.1 = ((bf16[8,256,128]{2,1,0:T(8,128)(2,1)}), bf16[8,256,128]{2,1,0:T(8,128)(2,1)S(1)}, u32[]{:S(2)}, u32[]{:S(2)}) async-start(bf16[8,256,128]{2,1,0:T(8,128)(2,1)} %project.1), calls=%async_computation.1 | async-start | bytes 1048576 | tf_op jit(solution)/shard_map/all_to_all | solution.py:207
  69.6 0.8 copy-start

commit v2 on v1

--- a/solution.py
+++ b/solution.py
@@ -9,6 +9,7 @@
 
 F32 = jnp.float32
 BF16 = jnp.bfloat16
+VMEM_LIMIT = 24 << 20
 GROUP = 4
 NT = (((1,), (1,)), ((), ()))
 NN = (((1,), (0,)), ((), ()))
@@ -22,6 +23,10 @@
 def split(x):
     high = x.astype(BF16)
     return high, (x - high.astype(F32)).astype(BF16)
+
+
+def on_chip(x):
+    return pltpu.with_memory_space_constraint(x, pltpu.VMEM)
 
 
 def call(kernel, out_shape, flops, bytes_accessed, name, scratch=(), smem=0, args=()):
@@ -31,9 +36,12 @@
         kernel,
         out_shape=out_shape,
         in_specs=specs,
-        out_specs=jax.tree.map(lambda _: pl.BlockSpec(memory_space=pltpu.VMEM), out_shape),
+        out_specs=jax.tree.map(
+            lambda _: pl.BlockSpec(memory_space=pltpu.VMEM), out_shape, is_leaf=lambda x: hasattr(x, "shape")
+        ),
         scratch_shapes=list(scratch),
         cost_estimate=pl.CostEstimate(flops=flops, bytes_accessed=bytes_accessed, transcendentals=0),
+        compiler_params=pltpu.CompilerParams(vmem_limit_bytes=VMEM_LIMIT),
         name=name,
     )(*args)
 
@@ -41,9 +49,9 @@
 def right_kernel(x_ref, a_ref, r_ref, out_ref):
     peers = out_ref.shape[0]
     layers = x_ref.shape[0]
-    proj = r_ref.shape[2]
+    proj = r_ref.shape[1]
     for l in range(layers):
-        mix = dot(r_ref[l], a_ref[l], TN)
+        mix = dot(r_ref[l], a_ref[l], NN)
         high, low = split(mix)
         both = jnp.concatenate([high, low], axis=0)
         rows = dot(both, x_ref[l], NT)
@@ -116,7 +124,7 @@
             out_ref[p, r:r + GROUP * half, :] = both_k.astype(BF16)
 
 
-def product_kernel(part_ref, valid_ref, squares_ref, out_ref, sum_ref):
+def product_kernel(part_ref, valid_ref, out_ref, sum_ref):
     peers, rows, _ = part_ref.shape
     valid_count = valid_ref.shape[0]
     examples = rows // 8
@@ -130,14 +138,18 @@
     column = lax.broadcasted_iota(jnp.int32, (examples, valid_count), 1)
     train = jnp.sum(jnp.where(row == column, squares, 0.0), axis=0, keepdims=True)
     acc = jnp.zeros((2 * examples, valid_count), F32)
+    valid_squares = jnp.zeros((valid_count, 128), F32)
     for b in range(8):
         block = sum_ref[pl.ds(b, examples, stride=8), :]
         high, low = split(block)
         both = jnp.concatenate([high, low], axis=0)
-        acc = acc + dot(both, valid_ref[:, b * 128:(b + 1) * 128], NT)
+        valid = valid_ref[:, b * 128:(b + 1) * 128]
+        valid_squares = valid_squares + valid * valid
+        acc = acc + dot(both, valid.astype(BF16), NT)
     products = acc[:examples] + acc[examples:]
+    valid_squares = jnp.sum(valid_squares.T, axis=0, keepdims=True)
     tail_row = lax.broadcasted_iota(jnp.int32, (8, valid_count), 0)
-    tail = jnp.where(tail_row == 0, squares_ref[...], jnp.where(tail_row == 1, train, 0.0))
+    tail = jnp.where(tail_row == 0, valid_squares, jnp.where(tail_row == 1, train, 0.0))
     for p in range(peers):
         out_ref[p, :examples, :] = products
         out_ref[p, examples:, :] = tail
@@ -171,22 +183,19 @@
     scaling = math.sqrt(kl * proj)
 
     own_valid = valid_grads.reshape(-1, owned, 2, 8).transpose(0, 3, 2, 1).reshape(1, -1, owned * proj)
-    own_valid = jnp.broadcast_to(own_valid, (groups,) + own_valid.shape[1:])
-    valid = lax.all_to_all(own_valid, "ex", 0, 0, tiled=True).reshape(valid_count, owned * proj)
-    valid_wide = valid.astype(F32)
-    valid_squares = jnp.sum(valid_wide * valid_wide, axis=1)[None, :]
+    valid = lax.all_gather(lax.optimization_barrier(own_valid.astype(F32))[0], "ex", axis=0, tiled=True)
 
     right_parts = call(
         right_kernel,
-        jax.ShapeDtypeStruct((peers, layers * proj, tokens), BF16),
+        pltpu.VMEM((peers, layers * proj, tokens), BF16),
         2 * layers * tokens * inputs * 256,
         proj_inputs.size * 2,
         "right_rows",
-        args=(proj_inputs.reshape(layers, tokens, inputs), frozen_adapter, right_factor),
+        args=(proj_inputs.reshape(layers, tokens, inputs), frozen_adapter, right_factor.swapaxes(1, 2)),
     )
     right_parts = lax.all_to_all(right_parts, "feat", 0, 0, tiled=True)
 
-    left_shape = jax.ShapeDtypeStruct((layers, tokens, kl), BF16)
+    left_shape = pltpu.VMEM((layers, tokens, kl), BF16)
     left_high, left_low = call(
         left_kernel,
         (left_shape, left_shape),
@@ -197,22 +206,22 @@
     )
     parts = call(
         project_kernel,
-        jax.ShapeDtypeStruct((peers, examples * 8, 128), BF16),
+        pltpu.VMEM((peers, examples * 8, 128), BF16),
         2 * layers * tokens * kl * 256,
         layers * tokens * kl * 4,
         "project",
         smem=1,
-        args=(seq_lengths, right_parts, left_high, left_low),
+        args=(seq_lengths, on_chip(right_parts), on_chip(left_high), on_chip(left_low)),
     )
     parts = lax.all_to_all(parts, "feat", 0, 0, tiled=True)
     products = call(
         product_kernel,
-        jax.ShapeDtypeStruct((peers, examples + 8, valid_count), F32),
+        pltpu.VMEM((peers, examples + 8, valid_count), F32),
         4 * examples * valid_count * owned * proj,
         parts.size * 2 + valid.size * 2,
         "products",
         scratch=(pltpu.VMEM((examples * 8, 128), F32),),
-        args=(parts, valid, valid_squares),
+        args=(on_chip(parts), on_chip(valid)),
     )
     products = lax.all_to_all(products, "feat", 0, 0, tiled=True)
 
@@ -225,7 +234,7 @@
         examples * valid_count * 16,
         products.size * 4,
         "scores",
-        args=(products,),
+        args=(on_chip(products),),
     )
 
 

time: 86.2 us -> 121 us (1.40)
  waiting for transfers between devices: 26.3 us -> 71.3 us
  starting transfers between devices: 28.2 us -> 10.1 us
  between operations: 0.04 us -> 13.5 us
  Pallas kernels: 14.5 us -> 5.63 us
  local copies, waits for them, and re-layouts: 5.13 us -> 8.74 us
    all_gather x0 -> x1, waiting for transfers between devices: none -> 68.1 us  [body(): lax.all_gather(lax.optimization_barrier(own_valid.astype(F32))[0], 'ex',...]
    all_to_all x1 -> x0, starting transfers between devices: 18 us -> none  [body(): lax.all_to_all(own_valid, 'ex', 0, 0, tiled=True)]
    all_to_all x1 -> x0, waiting for transfers between devices: 11.6 us -> none  [body(): lax.all_to_all(own_valid, 'ex', 0, 0, tiled=True)]
    pallas_call x5, Pallas kernels: 14.5 us -> 5.63 us  [call(): pl.pallas_call(kernel, out_shape=out_shape, in_specs=specs, out_specs=jax...]
    all_to_all x1, waiting for transfers between devices: 8.18 us -> 0.01 us  [body(): parts = lax.all_to_all(parts, 'feat', 0, 0, tiled=True)]
    unnamed x7 -> x13, local copies, waits for them, and re-layouts: 2.23 us -> 6.79 us
    all_to_all x1, waiting for transfers between devices: 6.45 us -> 3.16 us  [body(): right_parts = lax.all_to_all(right_parts, 'feat', 0, 0, tiled=True)]
    broadcast_in_dim x3 -> x0, local copies, waits for them, and re-layouts: 1.71 us -> none  [the longest x2 1.04 us: body(): own_valid = jnp.broadcast_to(own_valid, (groups,) + own_valid.shape[1:])]
  transfers between devices with their start and end apart: 3 -> 3, of which waited for: 3 -> 2; matrix products, arithmetic and copies ran while one was open for 3% -> 1% of each run, Pallas kernels for 9% -> 4%
where the time goes in v2:
time: 121 us
  waiting for transfers between devices  71.3 us (59%)
  between operations  13.5 us (11%)
  blocking collectives  11.5 us (10%)
  starting transfers between devices  10.1 us (8%)
  local copies, waits for them, and re-layouts  8.74 us (7%)
  Pallas kernels  5.63 us (5%)
    all_gather x1, waiting for transfers between devices, body(): lax.all_gather(lax.optimization_barrier(own_valid.astype(F32))[0], 'ex',...  68.1 us
    all_to_all x1, blocking collectives, body(): products = lax.all_to_all(products, 'feat', 0, 0, tiled=True)  11.5 us
    unnamed x13, local copies, waits for them, and re-layouts  6.79 us
    all_to_all x1, starting transfers between devices, body(): right_parts = lax.all_to_all(right_parts, 'feat', 0, 0, tiled=True)  6.65 us
    pallas_call x5, Pallas kernels, call(): pl.pallas_call(kernel, out_shape=out_shape, in_specs=specs, out_specs=jax...  5.63 us
    all_to_all x1, starting transfers between devices, body(): parts = lax.all_to_all(parts, 'feat', 0, 0, tiled=True)  3.49 us
    all_to_all x1, waiting for transfers between devices, body(): right_parts = lax.all_to_all(right_parts, 'feat', 0, 0, tiled=True)  3.16 us
  transfers between devices with their start and end apart: 3, of which 2 were waited for; matrix products, arithmetic and copies ran while one was open for 1% of the time, Pallas kernels for 4%

profile of v2, /device:TPU:1, one launch (start us, length us, event | category | flops | bytes accessed | tf_op | source)
XLA Modules:
  0.0 120.7 jit_solution(480164219305655416)
XLA Ops:
  6.5 0.0 all-gather.3.cloned.1.call-start
  6.5 1.1 reshape.27
  7.6 0.1 copy.10
  7.7 0.1 reshape.26
  7.9 0.6 copy.11
  8.5 0.0 all-gather.3.cloned.1.call-update
  8.5 0.0 copy-start
  8.5 1.1 copy-done
  9.7 0.0 copy-start.1
  9.7 0.9 copy-done.1
  10.6 0.0 copy-start.2
  10.6 0.7 copy-done.2
  11.3 1.2 %right_rows.1 = bf16[8,32,768]{2,1,0:T(8,128)(2,1)} custom-call(bf16[2,768,256]{2,1,0:T(8,128)(2,1)S(1)} %bitcast.8, bf16[2,128,256]{2,1,0:T(8,128)(2,1)S(1)} %copy-done.1, bf16[2,16,128]{2,1,0:T(8,128)(2,1)S(1)} %bitcast.9), custom_call_target="tpu_custom_call" | custom-call | flops 201326592 | bytes 786432 | tf_op jit(solution)/shard_map/right_rows/pallas_call | solution.py:35
  12.5 6.6 %all-to-all-start = ((bf16[8,32,768]{2,1,0:T(8,128)(2,1)}), bf16[8,32,768]{2,1,0:T(8,128)(2,1)S(1)}, u32[]{:S(2)}, u32[]{:S(2)}) async-start(bf16[8,32,768]{2,1,0:T(8,128)(2,1)} %right_rows.1), calls=%async_computation | async-start | bytes 786432 | tf_op jit(solution)/shard_map/all_to_all | solution.py:196
  19.1 0.0 copy-start.3
  19.1 0.0 copy-start.4
  19.2 1.4 %copy-done.4 = bf16[2,32,24,512]{3,2,1,0:T(8,128)(2,1)S(1)} copy-done((bf16[2,32,24,512]{3,2,1,0:T(8,128)(2,1)S(1)}, bf16[2,32,24,512]{3,2,1,0:T(8,128)(2,1)}, u32[]{:S(2)}) %copy-start.4) | copy-done | bytes 1572888
  20.6 0.0 copy-start.5
  20.6 1.2 %copy-done.5 = bf16[2,512,512]{2,1,0:T(8,128)(2,1)S(1)} copy-done((bf16[2,512,512]{2,1,0:T(8,128)(2,1)S(1)}, bf16[2,512,512]{2,1,0:T(8,128)(2,1)}, u32[]{:S(2)}) %copy-start.5) | copy-done | bytes 1048600
  21.8 1.0 left_rows.1
  22.8 3.2 %all-to-all-done.rr_ref = bf16[8,32,768]{2,1,0:T(8,128)(2,1)S(1)} async-done(((bf16[8,32,768]{2,1,0:T(8,128)(2,1)}), bf16[8,32,768]{2,1,0:T(8,128)(2,1)S(1)}, u32[]{:S(2)}, u32[]{:S(2)}) %all-to-all-start) | async-done | bytes 393248 | tf_op jit(solution)/shard_map/all_to_all | solution.py:196
  26.0 0.0 copy-done.3
  26.0 2.3 %project.1 = bf16[8,256,128]{2,1,0:T(8,128)(2,1)} custom-call(s32[32]{0:T(128)S(1)} %copy-done.3, bf16[8,32,768]{2,1,0:T(8,128)(2,1)S(1)} %all-to-all-done.rr_ref, bf16[2,768,512]{2,1,0:T(8,128)(2,1)S(1)} %get-tuple-element.7.high_ref, bf16[2,768,512]{2,1,0:T(8,128)(2,1)S(1)} %get-tuple-element.8.low_ref), custom_call_target="tpu_custom_call" | custom-call | flops 402653184 | bytes 3145728 | tf_op jit(solution)/shard_map/project/pallas_call | solution.py:35
  28.2 3.5 %all-to-all-start.1 = ((bf16[8,256,128]{2,1,0:T(8,128)(2,1)}), bf16[8,256,128]{2,1,0:T(8,128)(2,1)S(1)}, u32[]{:S(2)}, u32[]{:S(2)}) async-start(bf16[8,256,128]{2,1,0:T(8,128)(2,1)} %project.1), calls=%async_computation.1 | async-start | bytes 1048576 | tf_op jit(solution)/shard_map/all_to_all | solution.py:216
  31.7 68.1 %all-gather.3.cloned.1.call-done = f32[1,256,1024]{2,0,1:T(1,128)} async-done(((f32[1,4,1024]{2,0,1:T(1,128)}), f32[1,256,1024]{2,0,1:T(1,128)}) %all-gather.3.cloned.1.call-update) | async-done | bytes 1048592 | tf_op jit(solution)/shard_map/all_gather | solution.py:186
  99.8 1.4 %copy.14 = f32[1,256,1024]{2,1,0:T(8,128)S(1)} copy(f32[1,256,1024]{2,0,1:T(1,128)} %all-gather.3.cloned.1.call-done) | data formatting | bytes 2097152
  101.3 0.0 all-to-all-done.1.part_ref
  101.3 0.4 products.1
  101.7 11.5 %all_to_all.15.part_ref = f32[8,40,256]{2,1,0:T(8,128)S(1)} all-to-all(f32[8,40,256]{2,1,0:T(8,128)S(1)} %products.1), channel_id=1, replica_groups=mesh['ex'=64,'feat'=8] {'feat'}, dimensions={0} | all-to-all | bytes 655360 | tf_op jit(solution)/shard_map/all_to_all | solution.py:226
  113.1 0.7 scores.1
Async XLA Ops:
  6.5 93.3 %all-gather.3.cloned.1.call-start = ((), (), s32[]{:S(2)}) async-start(), calls=%async_computation.3 | async-start | bytes 1064960 | tf_op jit(solution)/shard_map/all_gather | solution.py:186
  8.5 1.1 copy-start
  9.7 0.9 copy-start.1
  10.6 0.7 copy-start.2
  12.5 13.5 %all-to-all-start = ((bf16[8,32,768]{2,1,0:T(8,128)(2,1)}), bf16[8,32,768]{2,1,0:T(8,128)(2,1)S(1)}, u32[]{:S(2)}, u32[]{:S(2)}) async-start(bf16[8,32,768]{2,1,0:T(8,128)(2,1)} %right_rows.1), calls=%async_computation | async-start | bytes 786432 | tf_op jit(solution)/shard_map/all_to_all | solution.py:196
  19.1 6.8 %copy-start.3 = (s32[32]{0:T(128)S(1)}, s32[32]{0:T(128)}, u32[]{:S(2)}) copy-start(s32[32]{0:T(128)} %seq_ref.1) | copy-start | bytes 388
  19.1 1.4 %copy-start.4 = (bf16[2,32,24,512]{3,2,1,0:T(8,128)(2,1)S(1)}, bf16[2,32,24,512]{3,2,1,0:T(8,128)(2,1)}, u32[]{:S(2)}) copy-start(bf16[2,32,24,512]{3,2,1,0:T(8,128)(2,1)} %param.8) | copy-start | bytes 4718596
  20.6 1.2 %copy-start.5 = (bf16[2,512,512]{2,1,0:T(8,128)(2,1)S(1)}, bf16[2,512,512]{2,1,0:T(8,128)(2,1)}, u32[]{:S(2)}) copy-start(bf16[2,512,512]{2,1,0:T(8,128)(2,1)} %l_ref.1) | copy-start | bytes 3145732
  28.2 73.0 %all-to-all-start.1 = ((bf16[8,256,128]{2,1,0:T(8,128)(2,1)}), bf16[8,256,128]{2,1,0:T(8,128)(2,1)S(1)}, u32[]{:S(2)}, u32[]{:S(2)}) async-start(bf16[8,256,128]{2,1,0:T(8,128)(2,1)} %project.1), calls=%async_computation.1 | async-start | bytes 1048576 | tf_op jit(solution)/shard_map/all_to_all | solution.py:216
Sparse Core Ops, SparseCore 0:
  10.6 89.1 all-gather.2

commit v3 on v2

--- a/solution.py
+++ b/solution.py
@@ -7,13 +7,13 @@
 from jax.experimental.pallas import tpu as pltpu
 from jax.sharding import PartitionSpec as P
 
+
 F32 = jnp.float32
 BF16 = jnp.bfloat16
 VMEM_LIMIT = 24 << 20
 GROUP = 4
 NT = (((1,), (1,)), ((), ()))
 NN = (((1,), (0,)), ((), ()))
-TN = (((0,), (0,)), ((), ()))
 
 
 def dot(a, b, dims):
@@ -29,7 +29,11 @@
     return pltpu.with_memory_space_constraint(x, pltpu.VMEM)
 
 
-def call(kernel, out_shape, flops, bytes_accessed, name, scratch=(), smem=0, args=()):
+def off_chip(x):
+    return pltpu.with_memory_space_constraint(x, pltpu.HBM)
+
+
+def call(kernel, out_shape, flops, bytes_accessed, scratch=(), smem=0, args=()):
     specs = [pl.BlockSpec(memory_space=pltpu.SMEM)] * smem
     specs += [pl.BlockSpec(memory_space=pltpu.VMEM)] * (len(args) - smem)
     return pl.pallas_call(
@@ -42,7 +46,6 @@
         scratch_shapes=list(scratch),
         cost_estimate=pl.CostEstimate(flops=flops, bytes_accessed=bytes_accessed, transcendentals=0),
         compiler_params=pltpu.CompilerParams(vmem_limit_bytes=VMEM_LIMIT),
-        name=name,
     )(*args)
 
 
@@ -124,7 +127,25 @@
             out_ref[p, r:r + GROUP * half, :] = both_k.astype(BF16)
 
 
-def product_kernel(part_ref, valid_ref, out_ref, sum_ref):
+def valid_kernel(own_ref, held_ref, other_ref, out_ref, squares_ref):
+    half = held_ref.shape[0]
+    count = 2 * half
+    lane = lax.broadcasted_iota(jnp.int32, (8, count), 1)
+    relative = ((lane >> 7) & 1) | (((lane >> 6) & 1) << 1) | (((lane >> 5) & 1) << 2)
+    group = (relative ^ own_ref[0]) & 7
+    index = (((lane >> 2) & 7) << 5) | (group << 2) | (lane & 3)
+    row = lax.broadcasted_iota(jnp.int32, (count, count), 0)
+    order = (row == jnp.broadcast_to(index[:1], (count, count))).astype(F32).astype(BF16)
+    squares = jnp.zeros((count, 128), F32)
+    for b in range(8):
+        lanes = slice(b * 128, (b + 1) * 128)
+        rows = dot(order[:, :half], held_ref[:, lanes], NN) + dot(order[:, half:], other_ref[:, lanes], NN)
+        squares = squares + rows * rows
+        out_ref[:, lanes] = rows.astype(BF16)
+    squares_ref[...] = jnp.sum(squares.T, axis=0, keepdims=True)
+
+
+def product_kernel(part_ref, valid_ref, squares_ref, out_ref, sum_ref):
     peers, rows, _ = part_ref.shape
     valid_count = valid_ref.shape[0]
     examples = rows // 8
@@ -138,18 +159,14 @@
     column = lax.broadcasted_iota(jnp.int32, (examples, valid_count), 1)
     train = jnp.sum(jnp.where(row == column, squares, 0.0), axis=0, keepdims=True)
     acc = jnp.zeros((2 * examples, valid_count), F32)
-    valid_squares = jnp.zeros((valid_count, 128), F32)
     for b in range(8):
         block = sum_ref[pl.ds(b, examples, stride=8), :]
         high, low = split(block)
         both = jnp.concatenate([high, low], axis=0)
-        valid = valid_ref[:, b * 128:(b + 1) * 128]
-        valid_squares = valid_squares + valid * valid
-        acc = acc + dot(both, valid.astype(BF16), NT)
+        acc = acc + dot(both, valid_ref[:, b * 128:(b + 1) * 128], NT)
     products = acc[:examples] + acc[examples:]
-    valid_squares = jnp.sum(valid_squares.T, axis=0, keepdims=True)
     tail_row = lax.broadcasted_iota(jnp.int32, (8, valid_count), 0)
-    tail = jnp.where(tail_row == 0, valid_squares, jnp.where(tail_row == 1, train, 0.0))
+    tail = jnp.where(tail_row == 0, squares_ref[...], jnp.where(tail_row == 1, train, 0.0))
     for p in range(peers):
         out_ref[p, :examples, :] = products
         out_ref[p, examples:, :] = tail
@@ -170,7 +187,7 @@
     out_ref[...] = scaling * products / (train * valid)
 
 
-def body(proj_inputs, out_cotangent, seq_lengths, frozen_adapter, left_factor, right_factor, valid_grads):
+def scores_of(proj_inputs, out_cotangent, seq_lengths, frozen_adapter, left_factor, right_factor, valid_grads):
     layers, examples, seq, inputs = proj_inputs.shape
     width = out_cotangent.shape[3]
     peers = lax.axis_size("feat")
@@ -181,17 +198,37 @@
     owned = kl // peers
     valid_count = valid_grads.shape[0] * groups
     scaling = math.sqrt(kl * proj)
+    mesh_y = 8
+    inner = groups // mesh_y
 
     own_valid = valid_grads.reshape(-1, owned, 2, 8).transpose(0, 3, 2, 1).reshape(1, -1, owned * proj)
-    valid = lax.all_gather(lax.optimization_barrier(own_valid.astype(F32))[0], "ex", axis=0, tiled=True)
+    far = [[y * inner + j for y in range(mesh_y)] for j in range(inner)]
+    own_valid = jnp.broadcast_to(own_valid, (mesh_y,) + own_valid.shape[1:])
+    held = lax.all_to_all(own_valid, "ex", 0, 0, tiled=True, axis_index_groups=far)
+    held = held.reshape(-1, owned * proj)
+    for bit in (4, 2, 1):
+        other = lax.ppermute(held, "ex", [(i, i ^ bit) for i in range(groups)])
+        if bit > 1:
+            held = jnp.concatenate([held, other], axis=0)
+    own_group = jnp.full((1,), lax.axis_index("ex"), jnp.int32)
+    valid, valid_squares = call(
+        valid_kernel,
+        (
+            pltpu.VMEM((valid_count, owned * proj), BF16),
+            pltpu.VMEM((1, valid_count), F32),
+        ),
+        2 * valid_count * valid_count * owned * proj,
+        2 * valid_count * owned * proj * 2,
+        smem=1,
+        args=(own_group, on_chip(held), on_chip(other)),
+    )
 
     right_parts = call(
         right_kernel,
         pltpu.VMEM((peers, layers * proj, tokens), BF16),
         2 * layers * tokens * inputs * 256,
         proj_inputs.size * 2,
-        "right_rows",
-        args=(proj_inputs.reshape(layers, tokens, inputs), frozen_adapter, right_factor.swapaxes(1, 2)),
+        args=(off_chip(proj_inputs.reshape(layers, tokens, inputs)), off_chip(frozen_adapter), off_chip(right_factor.swapaxes(1, 2))),
     )
     right_parts = lax.all_to_all(right_parts, "feat", 0, 0, tiled=True)
 
@@ -201,15 +238,13 @@
         (left_shape, left_shape),
         2 * layers * tokens * width * kl,
         (out_cotangent.size + left_factor.size) * 2 + layers * tokens * kl * 4,
-        "left_rows",
-        args=(out_cotangent.reshape(layers, tokens, width), left_factor),
+        args=(off_chip(out_cotangent.reshape(layers, tokens, width)), off_chip(left_factor)),
     )
     parts = call(
         project_kernel,
         pltpu.VMEM((peers, examples * 8, 128), BF16),
         2 * layers * tokens * kl * 256,
         layers * tokens * kl * 4,
-        "project",
         smem=1,
         args=(seq_lengths, on_chip(right_parts), on_chip(left_high), on_chip(left_low)),
     )
@@ -219,9 +254,8 @@
         pltpu.VMEM((peers, examples + 8, valid_count), F32),
         4 * examples * valid_count * owned * proj,
         parts.size * 2 + valid.size * 2,
-        "products",
         scratch=(pltpu.VMEM((examples * 8, 128), F32),),
-        args=(on_chip(parts), on_chip(valid)),
+        args=(on_chip(parts), on_chip(valid), on_chip(valid_squares)),
     )
     products = lax.all_to_all(products, "feat", 0, 0, tiled=True)
 
@@ -233,14 +267,13 @@
         jax.ShapeDtypeStruct((examples, valid_count), F32),
         examples * valid_count * 16,
         products.size * 4,
-        "scores",
         args=(on_chip(products),),
     )
 
 
 def solution(mesh):
     return jax.shard_map(
-        body,
+        scores_of,
         mesh=mesh,
         in_specs=(
             P(None, "ex", None, "feat"),

time: 121 us -> 78.7 us (0.65)
  waiting for transfers between devices: 71.3 us -> 16.4 us
  starting transfers between devices: 10.1 us -> 40.1 us
  between operations: 13.5 us -> 0.12 us
  local copies, waits for them, and re-layouts: 8.74 us -> 1.07 us
  Pallas kernels: 5.63 us -> 8.97 us
    all_gather x1 -> x0, waiting for transfers between devices: 68.1 us -> none  [body(): lax.all_gather(lax.optimization_barrier(own_valid.astype(F32))[0], 'ex',...]
    ppermute x0 -> x3, starting transfers between devices: none -> 22 us  [scores_of(): other = lax.ppermute(held, 'ex', [(i, i ^ bit) for i in range(groups)])]
    all_to_all x2 -> x3, starting transfers between devices: 10.1 us -> 18.1 us  [the longest x1 7.94 us: scores_of(): lax.all_to_all(own_valid, 'ex', 0, 0, tiled=True, axis_index_groups=far)]
    ppermute x0 -> x3, waiting for transfers between devices: none -> 7.7 us  [scores_of(): other = lax.ppermute(held, 'ex', [(i, i ^ bit) for i in range(groups)])]
    unnamed x13 -> x6, local copies, waits for them, and re-layouts: 6.79 us -> 0.02 us
    all_to_all x2 -> x3, waiting for transfers between devices: 3.17 us -> 8.73 us  [the longest x1 6.45 us: scores_of(): right_parts = lax.all_to_all(right_parts, 'feat', 0, 0, tiled=True)]
    pallas_call x5 -> x6, Pallas kernels: 5.63 us -> 8.97 us  [call(): pl.pallas_call(kernel, out_shape=out_shape, in_specs=specs, out_specs=jax...]
    convert_element_type x3 -> x0, local copies, waits for them, and re-layouts: 1.32 us -> none  [body(): own_valid.astype(F32)]
  transfers between devices with their start and end apart: 3 -> 6, of which waited for: 2 -> 5; matrix products, arithmetic and copies ran while one was open for 1% -> 1% of each run, Pallas kernels for 4% -> 7%
where the time goes in v3:
time: 78.7 us; the launch traced here: 78.1 us
  starting transfers between devices  40.1 us (51%)
  waiting for transfers between devices  16.4 us (21%)
  blocking collectives  11.4 us (14%)
  Pallas kernels  8.97 us (11%)
  local copies, waits for them, and re-layouts  1.07 us (1%)
    ppermute x3, starting transfers between devices, scores_of(): other = lax.ppermute(held, 'ex', [(i, i ^ bit) for i in range(groups)])  22 us
    all_to_all x1, blocking collectives, scores_of(): products = lax.all_to_all(products, 'feat', 0, 0, tiled=True)  11.4 us
    pallas_call x6, Pallas kernels, call(): pl.pallas_call(kernel, out_shape=out_shape, in_specs=specs, out_specs=jax...  8.97 us
    all_to_all x1, starting transfers between devices, scores_of(): lax.all_to_all(own_valid, 'ex', 0, 0, tiled=True, axis_index_groups=far)  7.94 us
    ppermute x3, waiting for transfers between devices, scores_of(): other = lax.ppermute(held, 'ex', [(i, i ^ bit) for i in range(groups)])  7.7 us
    all_to_all x1, starting transfers between devices, scores_of(): right_parts = lax.all_to_all(right_parts, 'feat', 0, 0, tiled=True)  6.65 us
    all_to_all x1, waiting for transfers between devices, scores_of(): right_parts = lax.all_to_all(right_parts, 'feat', 0, 0, tiled=True)  6.45 us
    all_to_all x1, starting transfers between devices, scores_of(): parts = lax.all_to_all(parts, 'feat', 0, 0, tiled=True)  3.49 us
  transfers between devices with their start and end apart: 6, of which 5 were waited for; matrix products, arithmetic and copies ran while one was open for 1% of the time, Pallas kernels for 7%

profile of v3, /device:TPU:1, one launch (start us, length us, event | category | flops | bytes accessed | tf_op | source)
XLA Modules:
  0.0 78.1 jit_solution(16667555980390979456)
XLA Ops:
  0.0 0.0 copy-start.1
  0.0 2.4 %shard_map.73 = bf16[8,32,768]{2,1,0:T(8,128)(2,1)} custom-call(bf16[2,768,256]{2,1,0:T(8,128)(2,1)} %bitcast.5, bf16[2,128,256]{2,1,0:T(8,128)(2,1)} %a_ref.1, bf16[2,16,128]{2,1,0:T(8,128)(2,1)} %bitcast.7), custom_call_target="tpu_custom_call" | custom-call | flops 201326592 | bytes 786432 | tf_op jit(solution)/shard_map/pallas_call | solution.py:39
  2.4 6.6 %all-to-all-start = ((bf16[8,32,768]{2,1,0:T(8,128)(2,1)}), bf16[8,32,768]{2,1,0:T(8,128)(2,1)S(1)}, u32[]{:S(2)}, u32[]{:S(2)}) async-start(bf16[8,32,768]{2,1,0:T(8,128)(2,1)} %shard_map.73), calls=%async_computation | async-start | bytes 786432 | tf_op jit(solution)/shard_map/all_to_all | solution.py:233
  9.1 0.0 copy-done.1
  9.1 0.2 reshape.16
  9.3 0.1 copy.8
  9.4 0.1 broadcast_in_dim.11
  9.5 6.4 %all-to-all-done.rr_ref = bf16[8,32,768]{2,1,0:T(8,128)(2,1)S(1)} async-done(((bf16[8,32,768]{2,1,0:T(8,128)(2,1)}), bf16[8,32,768]{2,1,0:T(8,128)(2,1)S(1)}, u32[]{:S(2)}, u32[]{:S(2)}) %all-to-all-start) | async-done | bytes 393248 | tf_op jit(solution)/shard_map/all_to_all | solution.py:233
  15.9 0.6 broadcast_in_dim.12
  16.6 0.0 copy-start
  16.6 7.9 %all-to-all-start.2 = ((bf16[8,4,1024]{2,1,0:T(4,128)(2,1)}), bf16[8,4,1024]{2,1,0:T(4,128)(2,1)S(1)}, u32[]{:S(2)}, u32[]{:S(2)}) async-start(bf16[8,4,1024]{2,1,0:T(4,128)(2,1)} %broadcast_in_dim.12), calls=%async_computation.2 | async-start | bytes 131072 | tf_op jit(solution)/shard_map/all_to_all | solution.py:207
  24.5 2.7 %shard_map.74 = (bf16[2,768,512]{2,1,0:T(8,128)(2,1)S(1)}, bf16[2,768,512]{2,1,0:T(8,128)(2,1)S(1)}) custom-call(bf16[2,768,512]{2,1,0:T(8,128)(2,1)} %bitcast.8, bf16[2,512,512]{2,1,0:T(8,128)(2,1)} %l_ref.1), custom_call_target="tpu_custom_call" | custom-call | flops 805306368 | bytes 5767168 | tf_op jit(solution)/shard_map/pallas_call | solution.py:39
  27.2 0.0 copy-done
  27.2 2.2 %shard_map.75 = bf16[8,256,128]{2,1,0:T(8,128)(2,1)} custom-call(s32[32]{0:T(128)S(1)} %copy-done, bf16[8,32,768]{2,1,0:T(8,128)(2,1)S(1)} %all-to-all-done.rr_ref, bf16[2,768,512]{2,1,0:T(8,128)(2,1)S(1)} %get-tuple-element.9.high_ref, bf16[2,768,512]{2,1,0:T(8,128)(2,1)S(1)} %get-tuple-element.10.low_ref), custom_call_target="tpu_custom_call" | custom-call | flops 402653184 | bytes 3145728 | tf_op jit(solution)/shard_map/pallas_call | solution.py:39
  29.4 2.3 %all-to-all-done.2 = bf16[8,4,1024]{2,1,0:T(4,128)(2,1)S(1)} async-done(((bf16[8,4,1024]{2,1,0:T(4,128)(2,1)}), bf16[8,4,1024]{2,1,0:T(4,128)(2,1)S(1)}, u32[]{:S(2)}, u32[]{:S(2)}) %all-to-all-start.2) | async-done | bytes 65568 | tf_op jit(solution)/shard_map/all_to_all | solution.py:207
  31.7 3.5 %all-to-all-start.1 = ((bf16[8,256,128]{2,1,0:T(8,128)(2,1)}), bf16[8,256,128]{2,1,0:T(8,128)(2,1)S(1)}, u32[]{:S(2)}, u32[]{:S(2)}) async-start(bf16[8,256,128]{2,1,0:T(8,128)(2,1)} %shard_map.75), calls=%async_computation.1 | async-start | bytes 1048576 | tf_op jit(solution)/shard_map/all_to_all | solution.py:251
  35.3 9.7 %collective-permute-start = (bf16[32,1024]{1,0:T(8,128)(2,1)S(1)}, bf16[32,1024]{1,0:T(8,128)(2,1)S(1)}, u32[]{:S(2)}, u32[]{:S(2)}) collective-permute-start(bf16[32,1024]{1,0:T(8,128)(2,1)S(1)} %reshape.17), channel_id=1, source_target_pairs={{0,32},{8,40},{16,48},{24,56},{32,0},{40,8},{48,16},{56,24},{64,96... | collective-permute-start | bytes 196616 | tf_op jit(solution)/shard_map/ppermute | solution.py:210
  45.0 2.9 %collective-permute-done = bf16[32,1024]{1,0:T(8,128)(2,1)S(1)} collective-permute-done((bf16[32,1024]{1,0:T(8,128)(2,1)S(1)}, bf16[32,1024]{1,0:T(8,128)(2,1)S(1)}, u32[]{:S(2)}, u32[]{:S(2)}) %collective-permute-start) | collective-permute-done | bytes 65568 | tf_op jit(solution)/shard_map/ppermute | solution.py:210
  47.9 5.2 %collective-permute-start.1 = (bf16[64,1024]{1,0:T(8,128)(2,1)S(1)}, bf16[64,1024]{1,0:T(8,128)(2,1)S(1)}, u32[]{:S(2)}, u32[]{:S(2)}) collective-permute-start(bf16[64,1024]{1,0:T(8,128)(2,1)S(1)} %pad_maximum_fusion), channel_id=1, source_target_pairs={{0,16},{8,24},{16,0},{24,8},{32,48},{40,56},{48,32},{56,40},{64,80... | collective-permute-start | bytes 393224 | tf_op jit(solution)/shard_map/ppermute | solution.py:210
  53.1 3.7 %collective-permute-done.1 = bf16[64,1024]{1,0:T(8,128)(2,1)S(1)} collective-permute-done((bf16[64,1024]{1,0:T(8,128)(2,1)S(1)}, bf16[64,1024]{1,0:T(8,128)(2,1)S(1)}, u32[]{:S(2)}, u32[]{:S(2)}) %collective-permute-start.1) | collective-permute-done | bytes 131104 | tf_op jit(solution)/shard_map/ppermute | solution.py:210
  56.8 7.1 %collective-permute-start.2 = (bf16[128,1024]{1,0:T(8,128)(2,1)S(1)}, bf16[128,1024]{1,0:T(8,128)(2,1)S(1)}, u32[]{:S(2)}, u32[]{:S(2)}) collective-permute-start(bf16[128,1024]{1,0:T(8,128)(2,1)S(1)} %constant_dynamic-update-slice_fusion.held_ref), channel_id=1, source_target_pairs={{0,8},{8,0},{16,24},{24,16},{32,40},{40,32},{48,56},{56,48},{64,72... | collective-permute-start | bytes 786440 | tf_op jit(solution)/shard_map/ppermute | solution.py:210
  64.0 1.1 %collective-permute-done.2.other_ref = bf16[128,1024]{1,0:T(8,128)(2,1)S(1)} collective-permute-done((bf16[128,1024]{1,0:T(8,128)(2,1)S(1)}, bf16[128,1024]{1,0:T(8,128)(2,1)S(1)}, u32[]{:S(2)}, u32[]{:S(2)}) %collective-permute-start.2) | collective-permute-done | bytes 262176 | tf_op jit(solution)/shard_map/ppermute | solution.py:210
  65.1 0.5 shard_map.76
  65.6 0.0 all-to-all-done.1.part_ref
  65.6 0.4 shard_map.77
  66.0 11.4 %all_to_all.20.part_ref = f32[8,40,256]{2,1,0:T(8,128)S(1)} all-to-all(f32[8,40,256]{2,1,0:T(8,128)S(1)} %shard_map.77), channel_id=1, replica_groups=mesh['ex'=64,'feat'=8] {'feat'}, dimensions={0} | all-to-all | bytes 655360 | tf_op jit(solution)/shard_map/all_to_all | solution.py:260
  77.4 0.7 shard_map.78
  (5 shorter events, 0.1 us)
Async XLA Ops:
  0.0 9.1 %copy-start.1 = (bf16[4,1024]{1,0:T(4,128)(2,1)S(1)}, bf16[4,1024]{1,0:T(4,128)(2,1)}, u32[]{:S(2)}) copy-start(bf16[4,1024]{1,0:T(4,128)(2,1)} %param.13) | copy-start | bytes 24580
  2.4 13.5 %all-to-all-start = ((bf16[8,32,768]{2,1,0:T(8,128)(2,1)}), bf16[8,32,768]{2,1,0:T(8,128)(2,1)S(1)}, u32[]{:S(2)}, u32[]{:S(2)}) async-start(bf16[8,32,768]{2,1,0:T(8,128)(2,1)} %shard_map.73), calls=%async_computation | async-start | bytes 786432 | tf_op jit(solution)/shard_map/all_to_all | solution.py:233
  16.6 10.7 %copy-start = (s32[32]{0:T(128)S(1)}, s32[32]{0:T(128)}, u32[]{:S(2)}) copy-start(s32[32]{0:T(128)} %seq_ref.1) | copy-start | bytes 388
  16.6 15.2 %all-to-all-start.2 = ((bf16[8,4,1024]{2,1,0:T(4,128)(2,1)}), bf16[8,4,1024]{2,1,0:T(4,128)(2,1)S(1)}, u32[]{:S(2)}, u32[]{:S(2)}) async-start(bf16[8,4,1024]{2,1,0:T(4,128)(2,1)} %broadcast_in_dim.12), calls=%async_computation.2 | async-start | bytes 131072 | tf_op jit(solution)/shard_map/all_to_all | solution.py:207
  31.7 33.9 %all-to-all-start.1 = ((bf16[8,256,128]{2,1,0:T(8,128)(2,1)}), bf16[8,256,128]{2,1,0:T(8,128)(2,1)S(1)}, u32[]{:S(2)}, u32[]{:S(2)}) async-start(bf16[8,256,128]{2,1,0:T(8,128)(2,1)} %shard_map.75), calls=%async_computation.1 | async-start | bytes 1048576 | tf_op jit(solution)/shard_map/all_to_all | solution.py:251
  35.3 12.6 %collective-permute-start = (bf16[32,1024]{1,0:T(8,128)(2,1)S(1)}, bf16[32,1024]{1,0:T(8,128)(2,1)S(1)}, u32[]{:S(2)}, u32[]{:S(2)}) collective-permute-start(bf16[32,1024]{1,0:T(8,128)(2,1)S(1)} %reshape.17), channel_id=1, source_target_pairs={{0,32},{8,40},{16,48},{24,56},{32,0},{40,8},{48,16},{56,24},{64,96... | collective-permute-start | bytes 196616 | tf_op jit(solution)/shard_map/ppermute | solution.py:210
  47.9 9.0 %collective-permute-start.1 = (bf16[64,1024]{1,0:T(8,128)(2,1)S(1)}, bf16[64,1024]{1,0:T(8,128)(2,1)S(1)}, u32[]{:S(2)}, u32[]{:S(2)}) collective-permute-start(bf16[64,1024]{1,0:T(8,128)(2,1)S(1)} %pad_maximum_fusion), channel_id=1, source_target_pairs={{0,16},{8,24},{16,0},{24,8},{32,48},{40,56},{48,32},{56,40},{64,80... | collective-permute-start | bytes 393224 | tf_op jit(solution)/shard_map/ppermute | solution.py:210
  56.8 8.3 %collective-permute-start.2 = (bf16[128,1024]{1,0:T(8,128)(2,1)S(1)}, bf16[128,1024]{1,0:T(8,128)(2,1)S(1)}, u32[]{:S(2)}, u32[]{:S(2)}) collective-permute-start(bf16[128,1024]{1,0:T(8,128)(2,1)S(1)} %constant_dynamic-update-slice_fusion.held_ref), channel_id=1, source_target_pairs={{0,8},{8,0},{16,24},{24,16},{32,40},{40,32},{48,56},{56,48},{64,72... | collective-permute-start | bytes 786440 | tf_op jit(solution)/shard_map/ppermute | solution.py:210

commit v4 on v3

--- a/solution.py
+++ b/solution.py
@@ -11,6 +11,7 @@
 F32 = jnp.float32
 BF16 = jnp.bfloat16
 VMEM_LIMIT = 24 << 20
+LEFT_STEP = 256
 GROUP = 4
 NT = (((1,), (1,)), ((), ()))
 NN = (((1,), (0,)), ((), ()))
@@ -33,9 +34,13 @@
     return pltpu.with_memory_space_constraint(x, pltpu.HBM)
 
 
-def call(kernel, out_shape, flops, bytes_accessed, scratch=(), smem=0, args=()):
+def staged(arrays):
+    return tuple(pltpu.VMEM(x.shape, x.dtype) for x in arrays)
+
+
+def call(kernel, out_shape, flops, bytes_accessed, scratch=(), smem=0, args=(), hbm=False):
     specs = [pl.BlockSpec(memory_space=pltpu.SMEM)] * smem
-    specs += [pl.BlockSpec(memory_space=pltpu.VMEM)] * (len(args) - smem)
+    specs += [pl.BlockSpec(memory_space=pltpu.HBM if hbm else pltpu.VMEM)] * (len(args) - smem)
     return pl.pallas_call(
         kernel,
         out_shape=out_shape,
@@ -49,28 +54,50 @@
     )(*args)
 
 
-def right_kernel(x_ref, a_ref, r_ref, out_ref):
+def right_kernel(x_hbm, a_hbm, r_hbm, out_ref, x_ref, a_ref, r_ref, sems):
     peers = out_ref.shape[0]
     layers = x_ref.shape[0]
     proj = r_ref.shape[1]
+    small = [
+        pltpu.make_async_copy(r_hbm, r_ref, sems.at[0]),
+        pltpu.make_async_copy(a_hbm, a_ref, sems.at[1]),
+    ]
+    inputs = [pltpu.make_async_copy(x_hbm.at[l], x_ref.at[l], sems.at[2 + l]) for l in range(layers)]
+    for copy in small + inputs:
+        copy.start()
+    for copy in small:
+        copy.wait()
+    mixes = []
     for l in range(layers):
-        mix = dot(r_ref[l], a_ref[l], NN)
-        high, low = split(mix)
-        both = jnp.concatenate([high, low], axis=0)
-        rows = dot(both, x_ref[l], NT)
+        high, low = split(dot(r_ref[l], a_ref[l], NN))
+        mixes.append(jnp.concatenate([high, low], axis=0))
+    for l in range(layers):
+        inputs[l].wait()
+        rows = dot(mixes[l], x_ref[l], NT)
         rows = (rows[:proj] + rows[proj:]).astype(BF16)
         for p in range(peers):
             out_ref[p, l * proj:(l + 1) * proj, :] = rows
 
 
-def left_kernel(c_ref, l_ref, high_ref, low_ref):
+def left_kernel(c_hbm, l_hbm, high_ref, low_ref, c_ref, l_ref, sems):
     layers, tokens, _ = c_ref.shape
-    step = 256
+    step = LEFT_STEP
+    factors, pieces = [], []
     for l in range(layers):
+        factors.append(pltpu.make_async_copy(l_hbm.at[l], l_ref.at[l], sems.at[l]))
+        factors[-1].start()
         for t in range(0, tokens, step):
-            high, low = split(dot(c_ref[l, t:t + step, :], l_ref[l], NT))
-            high_ref[l, t:t + step, :] = high
-            low_ref[l, t:t + step, :] = low
+            rows = pl.ds(t, step)
+            copy = pltpu.make_async_copy(c_hbm.at[l, rows], c_ref.at[l, rows], sems.at[layers + len(pieces)])
+            copy.start()
+            pieces.append((l, t, copy))
+    for l, t, copy in pieces:
+        if t == 0:
+            factors[l].wait()
+        copy.wait()
+        high, low = split(dot(c_ref[l, t:t + step, :], l_ref[l], NT))
+        high_ref[l, t:t + step, :] = high
+        low_ref[l, t:t + step, :] = low
 
 
 def project_kernel(seq_ref, rr_ref, high_ref, low_ref, out_ref):
@@ -127,19 +154,26 @@
             out_ref[p, r:r + GROUP * half, :] = both_k.astype(BF16)
 
 
-def valid_kernel(own_ref, held_ref, other_ref, out_ref, squares_ref):
-    half = held_ref.shape[0]
+def join_kernel(*refs):
+    rows = refs[0].shape[0]
+    for n, ref in enumerate(refs[:-1]):
+        refs[-1][n * rows:(n + 1) * rows, :] = ref[...]
+
+
+def valid_kernel(own_ref, *refs):
+    pieces, other_ref, out_ref, squares_ref = refs[:-3], refs[-3], refs[-2], refs[-1]
+    half = other_ref.shape[0]
     count = 2 * half
     lane = lax.broadcasted_iota(jnp.int32, (8, count), 1)
-    relative = ((lane >> 7) & 1) | (((lane >> 6) & 1) << 1) | (((lane >> 5) & 1) << 2)
-    group = (relative ^ own_ref[0]) & 7
-    index = (((lane >> 2) & 7) << 5) | (group << 2) | (lane & 3)
+    group = (((lane >> 7) & 1) | (((lane >> 5) & 3) << 1)) ^ own_ref[0]
+    index = (((lane >> 2) & 7) << 5) | ((group & 7) << 2) | (lane & 3)
     row = lax.broadcasted_iota(jnp.int32, (count, count), 0)
     order = (row == jnp.broadcast_to(index[:1], (count, count))).astype(F32).astype(BF16)
     squares = jnp.zeros((count, 128), F32)
     for b in range(8):
         lanes = slice(b * 128, (b + 1) * 128)
-        rows = dot(order[:, :half], held_ref[:, lanes], NN) + dot(order[:, half:], other_ref[:, lanes], NN)
+        held = jnp.concatenate([ref[:, lanes] for ref in (*pieces, other_ref)], axis=0)
+        rows = dot(order, held, NN)
         squares = squares + rows * rows
         out_ref[:, lanes] = rows.astype(BF16)
     squares_ref[...] = jnp.sum(squares.T, axis=0, keepdims=True)
@@ -206,10 +240,18 @@
     own_valid = jnp.broadcast_to(own_valid, (mesh_y,) + own_valid.shape[1:])
     held = lax.all_to_all(own_valid, "ex", 0, 0, tiled=True, axis_index_groups=far)
     held = held.reshape(-1, owned * proj)
-    for bit in (4, 2, 1):
-        other = lax.ppermute(held, "ex", [(i, i ^ bit) for i in range(groups)])
-        if bit > 1:
-            held = jnp.concatenate([held, other], axis=0)
+    pieces = [held]
+    for bit in (2, 4, 6):
+        pieces.append(lax.ppermute(held, "ex", [(i, i ^ bit) for i in range(groups)]))
+    pieces = [on_chip(piece) for piece in pieces]
+    half = call(
+        join_kernel,
+        jax.ShapeDtypeStruct((valid_count // 2, owned * proj), BF16),
+        0,
+        2 * valid_count * owned * proj,
+        args=pieces,
+    )
+    other = lax.ppermute(half, "ex", [(i, i ^ 1) for i in range(groups)])
     own_group = jnp.full((1,), lax.axis_index("ex"), jnp.int32)
     valid, valid_squares = call(
         valid_kernel,
@@ -220,25 +262,31 @@
         2 * valid_count * valid_count * owned * proj,
         2 * valid_count * owned * proj * 2,
         smem=1,
-        args=(own_group, on_chip(held), on_chip(other)),
-    )
-
+        args=(own_group, *pieces, on_chip(other)),
+    )
+
+    right_in = (proj_inputs.reshape(layers, tokens, inputs), frozen_adapter, right_factor.swapaxes(1, 2))
     right_parts = call(
         right_kernel,
         pltpu.VMEM((peers, layers * proj, tokens), BF16),
         2 * layers * tokens * inputs * 256,
         proj_inputs.size * 2,
-        args=(off_chip(proj_inputs.reshape(layers, tokens, inputs)), off_chip(frozen_adapter), off_chip(right_factor.swapaxes(1, 2))),
+        scratch=(*staged(right_in), pltpu.SemaphoreType.DMA((2 + layers,))),
+        args=tuple(off_chip(x) for x in right_in),
+        hbm=True,
     )
     right_parts = lax.all_to_all(right_parts, "feat", 0, 0, tiled=True)
 
     left_shape = pltpu.VMEM((layers, tokens, kl), BF16)
+    left_in = (out_cotangent.reshape(layers, tokens, width), left_factor)
     left_high, left_low = call(
         left_kernel,
         (left_shape, left_shape),
         2 * layers * tokens * width * kl,
         (out_cotangent.size + left_factor.size) * 2 + layers * tokens * kl * 4,
-        args=(off_chip(out_cotangent.reshape(layers, tokens, width)), off_chip(left_factor)),
+        scratch=(*staged(left_in), pltpu.SemaphoreType.DMA((layers + layers * tokens // LEFT_STEP,))),
+        args=tuple(off_chip(x) for x in left_in),
+        hbm=True,
     )
     parts = call(
         project_kernel,

time: 78.7 us -> 79.5 us (1.010)
  blocking collectives: 11.4 us -> 13.2 us
  waiting for transfers between devices: 16.4 us -> 14.6 us
    all_to_all x1, blocking collectives: 11.4 us -> 13.2 us  [scores_of(): products = lax.all_to_all(products, 'feat', 0, 0, tiled=True)]
    ppermute x3 -> x4, waiting for transfers between devices: 7.7 us -> 6.37 us  [the longest x3 5.24 us: scores_of(): lax.ppermute(held, 'ex', [(i, i ^ bit) for i in range(groups)])]
    ppermute x3 -> x4, starting transfers between devices: 22 us -> 22.5 us  [the longest x3 15.7 us: scores_of(): lax.ppermute(held, 'ex', [(i, i ^ bit) for i in range(groups)])]
    pallas_call x6 -> x7, Pallas kernels: 8.97 us -> 9.41 us  [call(): pl.pallas_call(kernel, out_shape=out_shape, in_specs=specs, out_specs=jax...]
  transfers between devices with their start and end apart: 6 -> 7, of which waited for: 5 -> 5; matrix products, arithmetic and copies ran while one was open for 1% -> 0% of each run, Pallas kernels for 7% -> 7%
where the time goes in v4:
time: 79.5 us; the launch traced here: 79 us
  starting transfers between devices  40.6 us (51%)
  waiting for transfers between devices  14.6 us (18%)
  blocking collectives  13.2 us (17%)
  Pallas kernels  9.41 us (12%)
  local copies, waits for them, and re-layouts  1.03 us (1%)
    ppermute x3, starting transfers between devices, scores_of(): lax.ppermute(held, 'ex', [(i, i ^ bit) for i in range(groups)])  15.7 us
    all_to_all x1, blocking collectives, scores_of(): products = lax.all_to_all(products, 'feat', 0, 0, tiled=True)  13.2 us
    pallas_call x7, Pallas kernels, call(): pl.pallas_call(kernel, out_shape=out_shape, in_specs=specs, out_specs=jax...  9.41 us
    all_to_all x1, starting transfers between devices, scores_of(): lax.all_to_all(own_valid, 'ex', 0, 0, tiled=True, axis_index_groups=far)  7.93 us
    ppermute x1, starting transfers between devices, scores_of(): other = lax.ppermute(half, 'ex', [(i, i ^ 1) for i in range(groups)])  6.82 us
    all_to_all x1, starting transfers between devices, scores_of(): right_parts = lax.all_to_all(right_parts, 'feat', 0, 0, tiled=True)  6.66 us
    all_to_all x1, waiting for transfers between devices, scores_of(): right_parts = lax.all_to_all(right_parts, 'feat', 0, 0, tiled=True)  6.45 us
    ppermute x3, waiting for transfers between devices, scores_of(): lax.ppermute(held, 'ex', [(i, i ^ bit) for i in range(groups)])  5.24 us
  transfers between devices with their start and end apart: 7, of which 5 were waited for; matrix products, arithmetic and copies ran while one was open for 0% of the time, Pallas kernels for 7%

profile of v4, /device:TPU:1, one launch (start us, length us, event | category | flops | bytes accessed | tf_op | source)
XLA Modules:
  0.0 79.0 jit_solution(2570491951205117947)
XLA Ops:
  0.0 0.0 copy-start.1
  0.0 2.4 %shard_map.73 = bf16[8,32,768]{2,1,0:T(8,128)(2,1)} custom-call(bf16[2,768,256]{2,1,0:T(8,128)(2,1)} %bitcast.5, bf16[2,128,256]{2,1,0:T(8,128)(2,1)} %a_hbm.1, bf16[2,16,128]{2,1,0:T(8,128)(2,1)} %bitcast.7), custom_call_target="tpu_custom_call" | custom-call | flops 201326592 | bytes 786432 | tf_op jit(solution)/shard_map/pallas_call | solution.py:44
  2.4 6.7 %all-to-all-start = ((bf16[8,32,768]{2,1,0:T(8,128)(2,1)}), bf16[8,32,768]{2,1,0:T(8,128)(2,1)S(1)}, u32[]{:S(2)}, u32[]{:S(2)}) async-start(bf16[8,32,768]{2,1,0:T(8,128)(2,1)} %shard_map.73), calls=%async_computation | async-start | bytes 786432 | tf_op jit(solution)/shard_map/all_to_all | solution.py:278
  9.1 0.0 copy-done.1
  9.1 0.2 reshape.16
  9.3 0.1 copy.8
  9.4 0.1 broadcast_in_dim.11
  9.5 6.4 %all-to-all-done.rr_ref = bf16[8,32,768]{2,1,0:T(8,128)(2,1)S(1)} async-done(((bf16[8,32,768]{2,1,0:T(8,128)(2,1)}), bf16[8,32,768]{2,1,0:T(8,128)(2,1)S(1)}, u32[]{:S(2)}, u32[]{:S(2)}) %all-to-all-start) | async-done | bytes 393248 | tf_op jit(solution)/shard_map/all_to_all | solution.py:278
  15.9 0.6 broadcast_in_dim.12
  16.5 0.0 copy-start
  16.5 7.9 %all-to-all-start.2 = ((bf16[8,4,1024]{2,1,0:T(4,128)(2,1)}), bf16[8,4,1024]{2,1,0:T(4,128)(2,1)S(1)}, u32[]{:S(2)}, u32[]{:S(2)}) async-start(bf16[8,4,1024]{2,1,0:T(4,128)(2,1)} %broadcast_in_dim.12), calls=%async_computation.2 | async-start | bytes 131072 | tf_op jit(solution)/shard_map/all_to_all | solution.py:241
  24.5 3.2 %shard_map.74 = (bf16[2,768,512]{2,1,0:T(8,128)(2,1)S(1)}, bf16[2,768,512]{2,1,0:T(8,128)(2,1)S(1)}) custom-call(bf16[2,768,512]{2,1,0:T(8,128)(2,1)} %bitcast.8, bf16[2,512,512]{2,1,0:T(8,128)(2,1)} %l_hbm.1), custom_call_target="tpu_custom_call" | custom-call | flops 805306368 | bytes 5767168 | tf_op jit(solution)/shard_map/pallas_call | solution.py:44
  27.7 0.0 copy-done
  27.7 2.2 %shard_map.75 = bf16[8,256,128]{2,1,0:T(8,128)(2,1)} custom-call(s32[32]{0:T(128)S(1)} %copy-done, bf16[8,32,768]{2,1,0:T(8,128)(2,1)S(1)} %all-to-all-done.rr_ref, bf16[2,768,512]{2,1,0:T(8,128)(2,1)S(1)} %get-tuple-element.9.high_ref, bf16[2,768,512]{2,1,0:T(8,128)(2,1)S(1)} %get-tuple-element.10.low_ref), custom_call_target="tpu_custom_call" | custom-call | flops 402653184 | bytes 3145728 | tf_op jit(solution)/shard_map/pallas_call | solution.py:44
  29.9 1.8 %all-to-all-done.2 = bf16[8,4,1024]{2,1,0:T(4,128)(2,1)S(1)} async-done(((bf16[8,4,1024]{2,1,0:T(4,128)(2,1)}), bf16[8,4,1024]{2,1,0:T(4,128)(2,1)S(1)}, u32[]{:S(2)}, u32[]{:S(2)}) %all-to-all-start.2) | async-done | bytes 65568 | tf_op jit(solution)/shard_map/all_to_all | solution.py:241
  31.7 3.5 %all-to-all-start.1 = ((bf16[8,256,128]{2,1,0:T(8,128)(2,1)}), bf16[8,256,128]{2,1,0:T(8,128)(2,1)S(1)}, u32[]{:S(2)}, u32[]{:S(2)}) async-start(bf16[8,256,128]{2,1,0:T(8,128)(2,1)} %shard_map.75), calls=%async_computation.1 | async-start | bytes 1048576 | tf_op jit(solution)/shard_map/all_to_all | solution.py:299
  35.2 5.8 %collective-permute-start = (bf16[32,1024]{1,0:T(8,128)(2,1)S(1)}, bf16[32,1024]{1,0:T(8,128)(2,1)S(1)}, u32[]{:S(2)}, u32[]{:S(2)}) collective-permute-start(bf16[32,1024]{1,0:T(8,128)(2,1)S(1)} %reshape.17.refs_0_), channel_id=1, source_target_pairs={{0,16},{8,24},{16,0},{24,8},{32,48},{40,56},{48,32},{56,40},{64,80... | collective-permute-start | bytes 196616 | tf_op jit(solution)/shard_map/ppermute | solution.py:245
  41.0 7.9 %collective-permute-start.1 = (bf16[32,1024]{1,0:T(8,128)(2,1)S(1)}, bf16[32,1024]{1,0:T(8,128)(2,1)S(1)}, u32[]{:S(2)}, u32[]{:S(2)}) collective-permute-start(bf16[32,1024]{1,0:T(8,128)(2,1)S(1)} %reshape.17.refs_0_), channel_id=1, source_target_pairs={{0,32},{8,40},{16,48},{24,56},{32,0},{40,8},{48,16},{56,24},{64,96... | collective-permute-start | bytes 196616 | tf_op jit(solution)/shard_map/ppermute | solution.py:245
  49.0 1.9 %collective-permute-start.2 = (bf16[32,1024]{1,0:T(8,128)(2,1)S(1)}, bf16[32,1024]{1,0:T(8,128)(2,1)S(1)}, u32[]{:S(2)}, u32[]{:S(2)}) collective-permute-start(bf16[32,1024]{1,0:T(8,128)(2,1)S(1)} %reshape.17.refs_0_), channel_id=1, source_target_pairs={{0,48},{8,56},{16,32},{24,40},{32,16},{40,24},{48,0},{56,8},{64,11... | collective-permute-start | bytes 196616 | tf_op jit(solution)/shard_map/ppermute | solution.py:245
  50.9 0.0 collective-permute-done.refs_1_
  50.9 0.4 collective-permute-done.1.refs_2_
  51.3 4.8 %collective-permute-done.2.refs_3_ = bf16[32,1024]{1,0:T(8,128)(2,1)S(1)} collective-permute-done((bf16[32,1024]{1,0:T(8,128)(2,1)S(1)}, bf16[32,1024]{1,0:T(8,128)(2,1)S(1)}, u32[]{:S(2)}, u32[]{:S(2)}) %collective-permute-start.2) | collective-permute-done | bytes 65568 | tf_op jit(solution)/shard_map/ppermute | solution.py:245
  56.2 6.8 %collective-permute-start.3 = (bf16[128,1024]{1,0:T(8,128)(2,1)S(1)}, bf16[128,1024]{1,0:T(8,128)(2,1)S(1)}, u32[]{:S(2)}, u32[]{:S(2)}) collective-permute-start(bf16[128,1024]{1,0:T(8,128)(2,1)S(1)} %shard_map.76), channel_id=1, source_target_pairs={{0,8},{8,0},{16,24},{24,16},{32,40},{40,32},{48,56},{56,48},{64,72... | collective-permute-start | bytes 786440 | tf_op jit(solution)/shard_map/ppermute | solution.py:254
  63.0 1.1 %collective-permute-done.3.refs_4_ = bf16[128,1024]{1,0:T(8,128)(2,1)S(1)} collective-permute-done((bf16[128,1024]{1,0:T(8,128)(2,1)S(1)}, bf16[128,1024]{1,0:T(8,128)(2,1)S(1)}, u32[]{:S(2)}, u32[]{:S(2)}) %collective-permute-start.3) | collective-permute-done | bytes 262176 | tf_op jit(solution)/shard_map/ppermute | solution.py:254
  64.2 0.5 shard_map.77
  64.7 0.0 all-to-all-done.1.part_ref
  64.7 0.4 shard_map.78
  65.0 13.2 %all_to_all.20.part_ref = f32[8,40,256]{2,1,0:T(8,128)S(1)} all-to-all(f32[8,40,256]{2,1,0:T(8,128)S(1)} %shard_map.78), channel_id=1, replica_groups=mesh['ex'=64,'feat'=8] {'feat'}, dimensions={0} | all-to-all | bytes 655360 | tf_op jit(solution)/shard_map/all_to_all | solution.py:308
  78.3 0.7 shard_map.79
  (2 shorter events, 0.0 us)
Async XLA Ops:
  0.0 9.1 %copy-start.1 = (bf16[4,1024]{1,0:T(4,128)(2,1)S(1)}, bf16[4,1024]{1,0:T(4,128)(2,1)}, u32[]{:S(2)}) copy-start(bf16[4,1024]{1,0:T(4,128)(2,1)} %param.13) | copy-start | bytes 24580
  2.4 13.5 %all-to-all-start = ((bf16[8,32,768]{2,1,0:T(8,128)(2,1)}), bf16[8,32,768]{2,1,0:T(8,128)(2,1)S(1)}, u32[]{:S(2)}, u32[]{:S(2)}) async-start(bf16[8,32,768]{2,1,0:T(8,128)(2,1)} %shard_map.73), calls=%async_computation | async-start | bytes 786432 | tf_op jit(solution)/shard_map/all_to_all | solution.py:278
  16.5 11.1 %copy-start = (s32[32]{0:T(128)S(1)}, s32[32]{0:T(128)}, u32[]{:S(2)}) copy-start(s32[32]{0:T(128)} %seq_ref.1) | copy-start | bytes 388
  16.5 15.2 %all-to-all-start.2 = ((bf16[8,4,1024]{2,1,0:T(4,128)(2,1)}), bf16[8,4,1024]{2,1,0:T(4,128)(2,1)S(1)}, u32[]{:S(2)}, u32[]{:S(2)}) async-start(bf16[8,4,1024]{2,1,0:T(4,128)(2,1)} %broadcast_in_dim.12), calls=%async_computation.2 | async-start | bytes 131072 | tf_op jit(solution)/shard_map/all_to_all | solution.py:241
  31.7 33.0 %all-to-all-start.1 = ((bf16[8,256,128]{2,1,0:T(8,128)(2,1)}), bf16[8,256,128]{2,1,0:T(8,128)(2,1)S(1)}, u32[]{:S(2)}, u32[]{:S(2)}) async-start(bf16[8,256,128]{2,1,0:T(8,128)(2,1)} %shard_map.75), calls=%async_computation.1 | async-start | bytes 1048576 | tf_op jit(solution)/shard_map/all_to_all | solution.py:299
  35.2 15.7 %collective-permute-start = (bf16[32,1024]{1,0:T(8,128)(2,1)S(1)}, bf16[32,1024]{1,0:T(8,128)(2,1)S(1)}, u32[]{:S(2)}, u32[]{:S(2)}) collective-permute-start(bf16[32,1024]{1,0:T(8,128)(2,1)S(1)} %reshape.17.refs_0_), channel_id=1, source_target_pairs={{0,16},{8,24},{16,0},{24,8},{32,48},{40,56},{48,32},{56,40},{64,80... | collective-permute-start | bytes 196616 | tf_op jit(solution)/shard_map/ppermute | solution.py:245
  41.0 10.3 %collective-permute-start.1 = (bf16[32,1024]{1,0:T(8,128)(2,1)S(1)}, bf16[32,1024]{1,0:T(8,128)(2,1)S(1)}, u32[]{:S(2)}, u32[]{:S(2)}) collective-permute-start(bf16[32,1024]{1,0:T(8,128)(2,1)S(1)} %reshape.17.refs_0_), channel_id=1, source_target_pairs={{0,32},{8,40},{16,48},{24,56},{32,0},{40,8},{48,16},{56,24},{64,96... | collective-permute-start | bytes 196616 | tf_op jit(solution)/shard_map/ppermute | solution.py:245
  49.0 7.2 %collective-permute-start.2 = (bf16[32,1024]{1,0:T(8,128)(2,1)S(1)}, bf16[32,1024]{1,0:T(8,128)(2,1)S(1)}, u32[]{:S(2)}, u32[]{:S(2)}) collective-permute-start(bf16[32,1024]{1,0:T(8,128)(2,1)S(1)} %reshape.17.refs_0_), channel_id=1, source_target_pairs={{0,48},{8,56},{16,32},{24,40},{32,16},{40,24},{48,0},{56,8},{64,11... | collective-permute-start | bytes 196616 | tf_op jit(solution)/shard_map/ppermute | solution.py:245
  56.2 8.0 %collective-permute-start.3 = (bf16[128,1024]{1,0:T(8,128)(2,1)S(1)}, bf16[128,1024]{1,0:T(8,128)(2,1)S(1)}, u32[]{:S(2)}, u32[]{:S(2)}) collective-permute-start(bf16[128,1024]{1,0:T(8,128)(2,1)S(1)} %shard_map.76), channel_id=1, source_target_pairs={{0,8},{8,0},{16,24},{24,16},{32,40},{40,32},{48,56},{56,48},{64,72... | collective-permute-start | bytes 786440 | tf_op jit(solution)/shard_map/ppermute | solution.py:254

commit v5 on v4

--- a/solution.py
+++ b/solution.py
@@ -154,28 +154,22 @@
             out_ref[p, r:r + GROUP * half, :] = both_k.astype(BF16)
 
 
-def join_kernel(*refs):
-    rows = refs[0].shape[0]
-    for n, ref in enumerate(refs[:-1]):
-        refs[-1][n * rows:(n + 1) * rows, :] = ref[...]
-
-
-def valid_kernel(own_ref, *refs):
-    pieces, other_ref, out_ref, squares_ref = refs[:-3], refs[-3], refs[-2], refs[-1]
-    half = other_ref.shape[0]
-    count = 2 * half
-    lane = lax.broadcasted_iota(jnp.int32, (8, count), 1)
-    group = (((lane >> 7) & 1) | (((lane >> 5) & 3) << 1)) ^ own_ref[0]
-    index = (((lane >> 2) & 7) << 5) | ((group & 7) << 2) | (lane & 3)
-    row = lax.broadcasted_iota(jnp.int32, (count, count), 0)
-    order = (row == jnp.broadcast_to(index[:1], (count, count))).astype(F32).astype(BF16)
+def valid_kernel(own_ref, half_ref, other_ref, out_ref, squares_ref):
+    count = half_ref.shape[0]
+    place = lax.broadcasted_iota(jnp.int32, (8, 2 * count), 1)
+    core = ((place >> 8) ^ own_ref[0]) & 1
+    index = (((place >> 3) & 31) << 3) | (core << 2) | ((place >> 1) & 3)
+    row = lax.broadcasted_iota(jnp.int32, (count, 2 * count), 0)
     squares = jnp.zeros((count, 128), F32)
-    for b in range(8):
-        lanes = slice(b * 128, (b + 1) * 128)
-        held = jnp.concatenate([ref[:, lanes] for ref in (*pieces, other_ref)], axis=0)
-        rows = dot(order, held, NN)
-        squares = squares + rows * rows
-        out_ref[:, lanes] = rows.astype(BF16)
+    for h in range(2):
+        source = jnp.where((place & 1) == h, index, -1)
+        order = (row == jnp.broadcast_to(source[:1], row.shape)).astype(F32).astype(BF16)
+        for q in range(4):
+            lanes = slice(q * 128, (q + 1) * 128)
+            rows = dot(order[:, :count], half_ref[:, lanes], NN) + dot(order[:, count:], other_ref[:, lanes], NN)
+            squares = squares + rows * rows
+            b = h * 4 + q
+            out_ref[:, b * 128:(b + 1) * 128] = rows.astype(BF16)
     squares_ref[...] = jnp.sum(squares.T, axis=0, keepdims=True)
 
 
@@ -232,25 +226,12 @@
     owned = kl // peers
     valid_count = valid_grads.shape[0] * groups
     scaling = math.sqrt(kl * proj)
-    mesh_y = 8
-    inner = groups // mesh_y
-
-    own_valid = valid_grads.reshape(-1, owned, 2, 8).transpose(0, 3, 2, 1).reshape(1, -1, owned * proj)
-    far = [[y * inner + j for y in range(mesh_y)] for j in range(inner)]
-    own_valid = jnp.broadcast_to(own_valid, (mesh_y,) + own_valid.shape[1:])
-    held = lax.all_to_all(own_valid, "ex", 0, 0, tiled=True, axis_index_groups=far)
-    held = held.reshape(-1, owned * proj)
-    pieces = [held]
-    for bit in (2, 4, 6):
-        pieces.append(lax.ppermute(held, "ex", [(i, i ^ bit) for i in range(groups)]))
-    pieces = [on_chip(piece) for piece in pieces]
-    half = call(
-        join_kernel,
-        jax.ShapeDtypeStruct((valid_count // 2, owned * proj), BF16),
-        0,
-        2 * valid_count * owned * proj,
-        args=pieces,
-    )
+
+    own_valid = valid_grads.reshape(-1, owned, 2, 8).transpose(0, 3, 2, 1).reshape(1, -1, owned * proj // 2)
+    own_valid = jnp.broadcast_to(own_valid, (groups // 2,) + own_valid.shape[1:])
+    same_core = [[i * 2 + c for i in range(groups // 2)] for c in range(2)]
+    half = lax.all_to_all(own_valid, "ex", 0, 0, tiled=True, axis_index_groups=same_core)
+    half = half.reshape(valid_count, owned * proj // 2)
     other = lax.ppermute(half, "ex", [(i, i ^ 1) for i in range(groups)])
     own_group = jnp.full((1,), lax.axis_index("ex"), jnp.int32)
     valid, valid_squares = call(
@@ -262,7 +243,7 @@
         2 * valid_count * valid_count * owned * proj,
         2 * valid_count * owned * proj * 2,
         smem=1,
-        args=(own_group, *pieces, on_chip(other)),
+        args=(own_group, on_chip(half), on_chip(other)),
     )
 
     right_in = (proj_inputs.reshape(layers, tokens, inputs), frozen_adapter, right_factor.swapaxes(1, 2))

time: 79.5 us -> 70.5 us (0.89)
  the two profiles are of different devices: /device:TPU:1 before, /device:TPU:8 now
where the time goes in v5:
time: 70.5 us; the launch traced here: 70.1 us
  starting transfers between devices  26.8 us (38%)
  waiting for transfers between devices  22.1 us (31%)
  blocking collectives  10.3 us (15%)
  Pallas kernels  9.69 us (14%)
  local copies, waits for them, and re-layouts  1.1 us (2%)
    all_to_all x1, starting transfers between devices, scores_of(): lax.all_to_all(own_valid, 'ex', 0, 0, tiled=True, axis_index_groups=same_...  15.3 us
    all_to_all x1, blocking collectives, scores_of(): products = lax.all_to_all(products, 'feat', 0, 0, tiled=True)  10.3 us
    pallas_call x6, Pallas kernels, call(): pl.pallas_call(kernel, out_shape=out_shape, in_specs=specs, out_specs=jax...  9.69 us
    all_to_all x1, waiting for transfers between devices, scores_of(): right_parts = lax.all_to_all(right_parts, 'feat', 0, 0, tiled=True)  8.28 us
    all_to_all x1, waiting for transfers between devices, scores_of(): lax.all_to_all(own_valid, 'ex', 0, 0, tiled=True, axis_index_groups=same_...  7.95 us
    all_to_all x1, starting transfers between devices, scores_of(): right_parts = lax.all_to_all(right_parts, 'feat', 0, 0, tiled=True)  6.12 us
    all_to_all x1, waiting for transfers between devices, scores_of(): parts = lax.all_to_all(parts, 'feat', 0, 0, tiled=True)  4.41 us
    all_to_all x1, starting transfers between devices, scores_of(): parts = lax.all_to_all(parts, 'feat', 0, 0, tiled=True)  3.49 us
  transfers between devices with their start and end apart: 4, of which 4 were waited for; matrix products, arithmetic and copies ran while one was open for 1% of the time, Pallas kernels for 9%

profile of v5, /device:TPU:8, one launch (start us, length us, event | category | flops | bytes accessed | tf_op | source)
XLA Modules:
  0.0 70.1 jit_solution(3577828410329060068)
XLA Ops:
  0.0 0.0 copy-start.1
  0.0 2.4 %shard_map.73 = bf16[8,32,768]{2,1,0:T(8,128)(2,1)} custom-call(bf16[2,768,256]{2,1,0:T(8,128)(2,1)} %bitcast.8, bf16[2,128,256]{2,1,0:T(8,128)(2,1)} %a_hbm.1, bf16[2,16,128]{2,1,0:T(8,128)(2,1)} %bitcast.10), custom_call_target="tpu_custom_call" | custom-call | flops 201326592 | bytes 786432 | tf_op jit(solution)/shard_map/pallas_call | solution.py:44
  2.4 6.1 %all-to-all-start = ((bf16[8,32,768]{2,1,0:T(8,128)(2,1)}), bf16[8,32,768]{2,1,0:T(8,128)(2,1)S(1)}, u32[]{:S(2)}, u32[]{:S(2)}) async-start(bf16[8,32,768]{2,1,0:T(8,128)(2,1)} %shard_map.73), calls=%async_computation | async-start | bytes 786432 | tf_op jit(solution)/shard_map/all_to_all | solution.py:259
  8.5 0.0 copy-done.1
  8.5 0.2 reshape.16
  8.7 0.1 copy.8
  8.8 0.1 broadcast_in_dim.11
  8.9 8.3 %all-to-all-done.rr_ref = bf16[8,32,768]{2,1,0:T(8,128)(2,1)S(1)} async-done(((bf16[8,32,768]{2,1,0:T(8,128)(2,1)}), bf16[8,32,768]{2,1,0:T(8,128)(2,1)S(1)}, u32[]{:S(2)}, u32[]{:S(2)}) %all-to-all-start) | async-done | bytes 393248 | tf_op jit(solution)/shard_map/all_to_all | solution.py:259
  17.2 0.7 %broadcast_in_dim.12 = bf16[32,8,512]{2,1,0:T(8,128)(2,1)} broadcast(bf16[8,512]{1,0:T(8,128)(2,1)S(1)} %broadcast_in_dim.11), dimensions={1,2} | broadcast | bytes 270336 | tf_op jit(solution)/shard_map/broadcast_in_dim | solution.py:231
  17.9 15.3 %all-to-all-start.2 = ((bf16[32,8,512]{2,1,0:T(8,128)(2,1)}), bf16[32,8,512]{2,1,0:T(8,128)(2,1)S(1)}, u32[]{:S(2)}, u32[]{:S(2)}) async-start(bf16[32,8,512]{2,1,0:T(8,128)(2,1)} %broadcast_in_dim.12), calls=%async_computation.2 | async-start | bytes 524288 | tf_op jit(solution)/shard_map/all_to_all | solution.py:233
  33.2 0.0 copy-start
  33.2 3.2 %shard_map.74 = (bf16[2,768,512]{2,1,0:T(8,128)(2,1)S(1)}, bf16[2,768,512]{2,1,0:T(8,128)(2,1)S(1)}) custom-call(bf16[2,768,512]{2,1,0:T(8,128)(2,1)} %bitcast.11, bf16[2,512,512]{2,1,0:T(8,128)(2,1)} %l_hbm.1), custom_call_target="tpu_custom_call" | custom-call | flops 805306368 | bytes 5767168 | tf_op jit(solution)/shard_map/pallas_call | solution.py:44
  36.4 0.0 copy-done
  36.4 2.2 %shard_map.75 = bf16[8,256,128]{2,1,0:T(8,128)(2,1)} custom-call(s32[32]{0:T(128)S(1)} %copy-done, bf16[8,32,768]{2,1,0:T(8,128)(2,1)S(1)} %all-to-all-done.rr_ref, bf16[2,768,512]{2,1,0:T(8,128)(2,1)S(1)} %get-tuple-element.9.high_ref, bf16[2,768,512]{2,1,0:T(8,128)(2,1)S(1)} %get-tuple-element.10.low_ref), custom_call_target="tpu_custom_call" | custom-call | flops 402653184 | bytes 3145728 | tf_op jit(solution)/shard_map/pallas_call | solution.py:44
  38.6 8.0 %all-to-all-done.2 = bf16[32,8,512]{2,1,0:T(8,128)(2,1)S(1)} async-done(((bf16[32,8,512]{2,1,0:T(8,128)(2,1)}), bf16[32,8,512]{2,1,0:T(8,128)(2,1)S(1)}, u32[]{:S(2)}, u32[]{:S(2)}) %all-to-all-start.2) | async-done | bytes 262176 | tf_op jit(solution)/shard_map/all_to_all | solution.py:233
  46.6 3.5 %all-to-all-start.1 = ((bf16[8,256,128]{2,1,0:T(8,128)(2,1)}), bf16[8,256,128]{2,1,0:T(8,128)(2,1)S(1)}, u32[]{:S(2)}, u32[]{:S(2)}) async-start(bf16[8,256,128]{2,1,0:T(8,128)(2,1)} %shard_map.75), calls=%async_computation.1 | async-start | bytes 1048576 | tf_op jit(solution)/shard_map/all_to_all | solution.py:280
  50.1 1.9 %collective-permute-start = (bf16[256,512]{1,0:T(8,128)(2,1)S(1)}, bf16[256,512]{1,0:T(8,128)(2,1)S(1)}, u32[]{:S(2)}, u32[]{:S(2)}) collective-permute-start(bf16[256,512]{1,0:T(8,128)(2,1)S(1)} %bitcast.6), channel_id=1, source_target_pairs={{0,8},{8,0},{16,24},{24,16},{32,40},{40,32},{48,56},{56,48},{64,72... | collective-permute-start | bytes 786440 | tf_op jit(solution)/shard_map/ppermute | solution.py:235
  52.0 1.5 %collective-permute-done.other_ref = bf16[256,512]{1,0:T(8,128)(2,1)S(1)} collective-permute-done((bf16[256,512]{1,0:T(8,128)(2,1)S(1)}, bf16[256,512]{1,0:T(8,128)(2,1)S(1)}, u32[]{:S(2)}, u32[]{:S(2)}) %collective-permute-start) | collective-permute-done | bytes 262176 | tf_op jit(solution)/shard_map/ppermute | solution.py:235
  53.5 0.8 %shard_map.76 = (bf16[256,1024]{1,0:T(8,128)(2,1)S(1)}, f32[1,256]{1,0:T(1,128)S(1)}) custom-call(s32[1]{0:T(128)} %bitcast.3.own_ref, bf16[256,512]{1,0:T(8,128)(2,1)S(1)} %bitcast.7, bf16[256,512]{1,0:T(8,128)(2,1)S(1)} %collective-permute-done.other_ref), custom_call_target="tpu_custom_call" | custom-call | flops 134217728 | bytes 1048576 | tf_op jit(solution)/shard_map/pallas_call | solution.py:44
  54.3 4.4 %all-to-all-done.1.part_ref = bf16[8,256,128]{2,1,0:T(8,128)(2,1)S(1)} async-done(((bf16[8,256,128]{2,1,0:T(8,128)(2,1)}), bf16[8,256,128]{2,1,0:T(8,128)(2,1)S(1)}, u32[]{:S(2)}, u32[]{:S(2)}) %all-to-all-start.1) | async-done | bytes 524320 | tf_op jit(solution)/shard_map/all_to_all | solution.py:280
  58.7 0.4 shard_map.77
  59.1 10.3 %all_to_all.20.part_ref = f32[8,40,256]{2,1,0:T(8,128)S(1)} all-to-all(f32[8,40,256]{2,1,0:T(8,128)S(1)} %shard_map.77), channel_id=1, replica_groups=mesh['ex'=64,'feat'=8] {'feat'}, dimensions={0} | all-to-all | bytes 655360 | tf_op jit(solution)/shard_map/all_to_all | solution.py:289
  69.4 0.7 %shard_map.78 = f32[32,256]{1,0:T(8,128)} custom-call(f32[8,40,256]{2,1,0:T(8,128)S(1)} %all_to_all.20.part_ref), custom_call_target="tpu_custom_call" | custom-call | flops 131072 | bytes 327680 | tf_op jit(solution)/shard_map/pallas_call | solution.py:44
Async XLA Ops:
  0.0 8.5 %copy-start.1 = (bf16[4,1024]{1,0:T(4,128)(2,1)S(1)}, bf16[4,1024]{1,0:T(4,128)(2,1)}, u32[]{:S(2)}) copy-start(bf16[4,1024]{1,0:T(4,128)(2,1)} %param.13) | copy-start | bytes 24580
  2.4 14.8 %all-to-all-start = ((bf16[8,32,768]{2,1,0:T(8,128)(2,1)}), bf16[8,32,768]{2,1,0:T(8,128)(2,1)S(1)}, u32[]{:S(2)}, u32[]{:S(2)}) async-start(bf16[8,32,768]{2,1,0:T(8,128)(2,1)} %shard_map.73), calls=%async_computation | async-start | bytes 786432 | tf_op jit(solution)/shard_map/all_to_all | solution.py:259
  17.9 28.7 %all-to-all-start.2 = ((bf16[32,8,512]{2,1,0:T(8,128)(2,1)}), bf16[32,8,512]{2,1,0:T(8,128)(2,1)S(1)}, u32[]{:S(2)}, u32[]{:S(2)}) async-start(bf16[32,8,512]{2,1,0:T(8,128)(2,1)} %broadcast_in_dim.12), calls=%async_computation.2 | async-start | bytes 524288 | tf_op jit(solution)/shard_map/all_to_all | solution.py:233
  33.2 3.2 %copy-start = (s32[32]{0:T(128)S(1)}, s32[32]{0:T(128)}, u32[]{:S(2)}) copy-start(s32[32]{0:T(128)} %seq_ref.1) | copy-start | bytes 388
  46.6 12.1 %all-to-all-start.1 = ((bf16[8,256,128]{2,1,0:T(8,128)(2,1)}), bf16[8,256,128]{2,1,0:T(8,128)(2,1)S(1)}, u32[]{:S(2)}, u32[]{:S(2)}) async-start(bf16[8,256,128]{2,1,0:T(8,128)(2,1)} %shard_map.75), calls=%async_computation.1 | async-start | bytes 1048576 | tf_op jit(solution)/shard_map/all_to_all | solution.py:280
  50.1 3.4 %collective-permute-start = (bf16[256,512]{1,0:T(8,128)(2,1)S(1)}, bf16[256,512]{1,0:T(8,128)(2,1)S(1)}, u32[]{:S(2)}, u32[]{:S(2)}) collective-permute-start(bf16[256,512]{1,0:T(8,128)(2,1)S(1)} %bitcast.6), channel_id=1, source_target_pairs={{0,8},{8,0},{16,24},{24,16},{32,40},{40,32},{48,56},{56,48},{64,72... | collective-permute-start | bytes 786440 | tf_op jit(solution)/shard_map/ppermute | solution.py:235

commit v6 on v5

--- a/solution.py
+++ b/solution.py
@@ -154,11 +154,18 @@
             out_ref[p, r:r + GROUP * half, :] = both_k.astype(BF16)
 
 
+def spread_kernel(own_ref, far_ref, out_ref):
+    for n in range(out_ref.shape[0]):
+        out_ref[n, 0] = own_ref[...]
+        out_ref[n, 1] = far_ref[...]
+
+
 def valid_kernel(own_ref, half_ref, other_ref, out_ref, squares_ref):
     count = half_ref.shape[0]
     place = lax.broadcasted_iota(jnp.int32, (8, 2 * count), 1)
     core = ((place >> 8) ^ own_ref[0]) & 1
-    index = (((place >> 3) & 31) << 3) | (core << 2) | ((place >> 1) & 3)
+    far = ((place >> 3) ^ (own_ref[0] >> 2)) & 1
+    index = (((place >> 5) & 7) << 5) | (far << 4) | (((place >> 4) & 1) << 3) | (core << 2) | ((place >> 1) & 3)
     row = lax.broadcasted_iota(jnp.int32, (count, 2 * count), 0)
     squares = jnp.zeros((count, 128), F32)
     for h in range(2):
@@ -227,10 +234,18 @@
     valid_count = valid_grads.shape[0] * groups
     scaling = math.sqrt(kl * proj)
 
-    own_valid = valid_grads.reshape(-1, owned, 2, 8).transpose(0, 3, 2, 1).reshape(1, -1, owned * proj // 2)
-    own_valid = jnp.broadcast_to(own_valid, (groups // 2,) + own_valid.shape[1:])
-    same_core = [[i * 2 + c for i in range(groups // 2)] for c in range(2)]
-    half = lax.all_to_all(own_valid, "ex", 0, 0, tiled=True, axis_index_groups=same_core)
+    own_valid = valid_grads.reshape(-1, owned, 2, 8).transpose(0, 3, 2, 1).reshape(-1, owned * proj // 2)
+    far_valid = lax.ppermute(own_valid, "ex", [(i, i ^ 4) for i in range(groups)])
+    count = groups // 4
+    spread = call(
+        spread_kernel,
+        jax.ShapeDtypeStruct((count, 2) + own_valid.shape, BF16),
+        0,
+        valid_grads.size * 2 * count,
+        args=(on_chip(own_valid), on_chip(far_valid)),
+    )
+    members = [[y * 8 + z * 4 + i * 2 + c for y in range(groups // 8) for i in range(2)] for z in range(2) for c in range(2)]
+    half = lax.all_to_all(spread, "ex", 0, 0, tiled=True, axis_index_groups=members)
     half = half.reshape(valid_count, owned * proj // 2)
     other = lax.ppermute(half, "ex", [(i, i ^ 1) for i in range(groups)])
     own_group = jnp.full((1,), lax.axis_index("ex"), jnp.int32)

time: 70.5 us -> 68.4 us (0.970)
  the two profiles are of different devices: /device:TPU:8 before, /device:TPU:1 now
where the time goes in v6:
time: 68.4 us; the launch traced here: 67.1 us
  starting transfers between devices  36 us (53%)
  blocking collectives  11.8 us (17%)
  Pallas kernels  10.4 us (15%)
  waiting for transfers between devices  8.35 us (12%)
    all_to_all x1, blocking collectives, scores_of(): products = lax.all_to_all(products, 'feat', 0, 0, tiled=True)  11.8 us
    pallas_call x7, Pallas kernels, call(): pl.pallas_call(kernel, out_shape=out_shape, in_specs=specs, out_specs=jax...  10.4 us
    ppermute x1, starting transfers between devices, scores_of(): lax.ppermute(own_valid, 'ex', [(i, i ^ 4) for i in range(groups)])  9.73 us
    all_to_all x1, starting transfers between devices, scores_of(): lax.all_to_all(spread, 'ex', 0, 0, tiled=True, axis_index_groups=members)  8.83 us
    all_to_all x1, starting transfers between devices, scores_of(): right_parts = lax.all_to_all(right_parts, 'feat', 0, 0, tiled=True)  6.66 us
    ppermute x1, starting transfers between devices, scores_of(): other = lax.ppermute(half, 'ex', [(i, i ^ 1) for i in range(groups)])  5.97 us
    all_to_all x1, waiting for transfers between devices, scores_of(): lax.all_to_all(spread, 'ex', 0, 0, tiled=True, axis_index_groups=members)  5.1 us
    all_to_all x1, starting transfers between devices, scores_of(): parts = lax.all_to_all(parts, 'feat', 0, 0, tiled=True)  4.81 us
  transfers between devices with their start and end apart: 5, of which 3 were waited for; matrix products, arithmetic and copies ran while one was open for 1% of the time, Pallas kernels for 10%

profile of v6, /device:TPU:1, one launch (start us, length us, event | category | flops | bytes accessed | tf_op | source)
XLA Modules:
  0.0 67.1 jit_solution(17505278242669013798)
XLA Ops:
  0.0 0.0 copy-start.1
  0.0 2.4 %shard_map.73 = bf16[8,32,768]{2,1,0:T(8,128)(2,1)} custom-call(bf16[2,768,256]{2,1,0:T(8,128)(2,1)} %bitcast.8, bf16[2,128,256]{2,1,0:T(8,128)(2,1)} %a_hbm.1, bf16[2,16,128]{2,1,0:T(8,128)(2,1)} %bitcast.10), custom_call_target="tpu_custom_call" | custom-call | flops 201326592 | bytes 786432 | tf_op jit(solution)/shard_map/pallas_call | solution.py:44
  2.4 6.7 %all-to-all-start = ((bf16[8,32,768]{2,1,0:T(8,128)(2,1)}), bf16[8,32,768]{2,1,0:T(8,128)(2,1)S(1)}, u32[]{:S(2)}, u32[]{:S(2)}) async-start(bf16[8,32,768]{2,1,0:T(8,128)(2,1)} %shard_map.73), calls=%async_computation | async-start | bytes 786432 | tf_op jit(solution)/shard_map/all_to_all | solution.py:274
  9.1 0.0 copy-done.1
  9.1 0.2 reshape.17
  9.3 0.1 copy.9
  9.4 0.1 reshape.18.own_ref
  9.5 9.7 %collective-permute-start = (bf16[8,512]{1,0:T(8,128)(2,1)S(1)}, bf16[8,512]{1,0:T(8,128)(2,1)S(1)}, u32[]{:S(2)}, u32[]{:S(2)}) collective-permute-start(bf16[8,512]{1,0:T(8,128)(2,1)S(1)} %reshape.18.own_ref), channel_id=1, source_target_pairs={{0,32},{8,40},{16,48},{24,56},{32,0},{40,8},{48,16},{56,24},{64,96... | collective-permute-start | bytes 24584 | tf_op jit(solution)/shard_map/ppermute | solution.py:238
  19.2 2.1 %collective-permute-done.far_ref = bf16[8,512]{1,0:T(8,128)(2,1)S(1)} collective-permute-done((bf16[8,512]{1,0:T(8,128)(2,1)S(1)}, bf16[8,512]{1,0:T(8,128)(2,1)S(1)}, u32[]{:S(2)}, u32[]{:S(2)}) %collective-permute-start) | collective-permute-done | bytes 8224 | tf_op jit(solution)/shard_map/ppermute | solution.py:238
  21.3 0.7 %shard_map.76 = bf16[16,2,8,512]{3,2,1,0:T(8,128)(2,1)} custom-call(bf16[8,512]{1,0:T(8,128)(2,1)S(1)} %reshape.18.own_ref, bf16[8,512]{1,0:T(8,128)(2,1)S(1)} %collective-permute-done.far_ref), custom_call_target="tpu_custom_call" | custom-call | bytes 131072 | tf_op jit(solution)/shard_map/pallas_call | solution.py:44
  22.0 0.0 all-to-all-done.rr_ref
  22.0 8.8 %all-to-all-start.2 = ((bf16[16,2,8,512]{3,2,1,0:T(8,128)(2,1)}), bf16[16,2,8,512]{3,2,1,0:T(8,128)(2,1)S(1)}, u32[]{:S(2)}, u32[]{:S(2)}) async-start(bf16[16,2,8,512]{3,2,1,0:T(8,128)(2,1)} %shard_map.76), calls=%async_computation.2 | async-start | bytes 524288 | tf_op jit(solution)/shard_map/all_to_all | solution.py:248
  30.9 0.0 copy-start
  30.9 3.2 %shard_map.74 = (bf16[2,768,512]{2,1,0:T(8,128)(2,1)S(1)}, bf16[2,768,512]{2,1,0:T(8,128)(2,1)S(1)}) custom-call(bf16[2,768,512]{2,1,0:T(8,128)(2,1)} %bitcast.11, bf16[2,512,512]{2,1,0:T(8,128)(2,1)} %l_hbm.1), custom_call_target="tpu_custom_call" | custom-call | flops 805306368 | bytes 5767168 | tf_op jit(solution)/shard_map/pallas_call | solution.py:44
  34.1 0.0 copy-done
  34.1 2.2 %shard_map.75 = bf16[8,256,128]{2,1,0:T(8,128)(2,1)} custom-call(s32[32]{0:T(128)S(1)} %copy-done, bf16[8,32,768]{2,1,0:T(8,128)(2,1)S(1)} %all-to-all-done.rr_ref, bf16[2,768,512]{2,1,0:T(8,128)(2,1)S(1)} %get-tuple-element.9.high_ref, bf16[2,768,512]{2,1,0:T(8,128)(2,1)S(1)} %get-tuple-element.10.low_ref), custom_call_target="tpu_custom_call" | custom-call | flops 402653184 | bytes 3145728 | tf_op jit(solution)/shard_map/pallas_call | solution.py:44
  36.3 5.1 %all-to-all-done.2 = bf16[16,2,8,512]{3,2,1,0:T(8,128)(2,1)S(1)} async-done(((bf16[16,2,8,512]{3,2,1,0:T(8,128)(2,1)}), bf16[16,2,8,512]{3,2,1,0:T(8,128)(2,1)S(1)}, u32[]{:S(2)}, u32[]{:S(2)}) %all-to-all-start.2) | async-done | bytes 262176 | tf_op jit(solution)/shard_map/all_to_all | solution.py:248
  41.4 4.8 %all-to-all-start.1 = ((bf16[8,256,128]{2,1,0:T(8,128)(2,1)}), bf16[8,256,128]{2,1,0:T(8,128)(2,1)S(1)}, u32[]{:S(2)}, u32[]{:S(2)}) async-start(bf16[8,256,128]{2,1,0:T(8,128)(2,1)} %shard_map.75), calls=%async_computation.1 | async-start | bytes 1048576 | tf_op jit(solution)/shard_map/all_to_all | solution.py:295
  46.2 6.0 %collective-permute-start.1 = (bf16[256,512]{1,0:T(8,128)(2,1)S(1)}, bf16[256,512]{1,0:T(8,128)(2,1)S(1)}, u32[]{:S(2)}, u32[]{:S(2)}) collective-permute-start(bf16[256,512]{1,0:T(8,128)(2,1)S(1)} %bitcast.6), channel_id=1, source_target_pairs={{0,8},{8,0},{16,24},{24,16},{32,40},{40,32},{48,56},{56,48},{64,72... | collective-permute-start | bytes 786440 | tf_op jit(solution)/shard_map/ppermute | solution.py:250
  52.2 1.1 %collective-permute-done.1.other_ref = bf16[256,512]{1,0:T(8,128)(2,1)S(1)} collective-permute-done((bf16[256,512]{1,0:T(8,128)(2,1)S(1)}, bf16[256,512]{1,0:T(8,128)(2,1)S(1)}, u32[]{:S(2)}, u32[]{:S(2)}) %collective-permute-start.1) | collective-permute-done | bytes 262176 | tf_op jit(solution)/shard_map/ppermute | solution.py:250
  53.3 0.8 %shard_map.77 = (bf16[256,1024]{1,0:T(8,128)(2,1)S(1)}, f32[1,256]{1,0:T(1,128)S(1)}) custom-call(s32[1]{0:T(128)} %bitcast.3.own_ref, bf16[256,512]{1,0:T(8,128)(2,1)S(1)} %bitcast.7, bf16[256,512]{1,0:T(8,128)(2,1)S(1)} %collective-permute-done.1.other_ref), custom_call_target="tpu_custom_call" | custom-call | flops 134217728 | bytes 1048576 | tf_op jit(solution)/shard_map/pallas_call | solution.py:44
  54.1 0.0 all-to-all-done.1.part_ref
  54.1 0.4 shard_map.78
  54.5 11.8 %all_to_all.20.part_ref = f32[8,40,256]{2,1,0:T(8,128)S(1)} all-to-all(f32[8,40,256]{2,1,0:T(8,128)S(1)} %shard_map.78), channel_id=1, replica_groups=mesh['ex'=64,'feat'=8] {'feat'}, dimensions={0} | all-to-all | bytes 655360 | tf_op jit(solution)/shard_map/all_to_all | solution.py:304
  66.3 0.7 %shard_map.79 = f32[32,256]{1,0:T(8,128)} custom-call(f32[8,40,256]{2,1,0:T(8,128)S(1)} %all_to_all.20.part_ref), custom_call_target="tpu_custom_call" | custom-call | flops 131072 | bytes 327680 | tf_op jit(solution)/shard_map/pallas_call | solution.py:44
Async XLA Ops:
  0.0 9.1 %copy-start.1 = (bf16[4,1024]{1,0:T(4,128)(2,1)S(1)}, bf16[4,1024]{1,0:T(4,128)(2,1)}, u32[]{:S(2)}) copy-start(bf16[4,1024]{1,0:T(4,128)(2,1)} %param.13) | copy-start | bytes 24580
  2.4 19.6 %all-to-all-start = ((bf16[8,32,768]{2,1,0:T(8,128)(2,1)}), bf16[8,32,768]{2,1,0:T(8,128)(2,1)S(1)}, u32[]{:S(2)}, u32[]{:S(2)}) async-start(bf16[8,32,768]{2,1,0:T(8,128)(2,1)} %shard_map.73), calls=%async_computation | async-start | bytes 786432 | tf_op jit(solution)/shard_map/all_to_all | solution.py:274
  9.5 11.8 %collective-permute-start = (bf16[8,512]{1,0:T(8,128)(2,1)S(1)}, bf16[8,512]{1,0:T(8,128)(2,1)S(1)}, u32[]{:S(2)}, u32[]{:S(2)}) collective-permute-start(bf16[8,512]{1,0:T(8,128)(2,1)S(1)} %reshape.18.own_ref), channel_id=1, source_target_pairs={{0,32},{8,40},{16,48},{24,56},{32,0},{40,8},{48,16},{56,24},{64,96... | collective-permute-start | bytes 24584 | tf_op jit(solution)/shard_map/ppermute | solution.py:238
  22.0 19.4 %all-to-all-start.2 = ((bf16[16,2,8,512]{3,2,1,0:T(8,128)(2,1)}), bf16[16,2,8,512]{3,2,1,0:T(8,128)(2,1)S(1)}, u32[]{:S(2)}, u32[]{:S(2)}) async-start(bf16[16,2,8,512]{3,2,1,0:T(8,128)(2,1)} %shard_map.76), calls=%async_computation.2 | async-start | bytes 524288 | tf_op jit(solution)/shard_map/all_to_all | solution.py:248
  30.9 3.2 %copy-start = (s32[32]{0:T(128)S(1)}, s32[32]{0:T(128)}, u32[]{:S(2)}) copy-start(s32[32]{0:T(128)} %seq_ref.1) | copy-start | bytes 388
  41.4 12.7 %all-to-all-start.1 = ((bf16[8,256,128]{2,1,0:T(8,128)(2,1)}), bf16[8,256,128]{2,1,0:T(8,128)(2,1)S(1)}, u32[]{:S(2)}, u32[]{:S(2)}) async-start(bf16[8,256,128]{2,1,0:T(8,128)(2,1)} %shard_map.75), calls=%async_computation.1 | async-start | bytes 1048576 | tf_op jit(solution)/shard_map/all_to_all | solution.py:295
  46.2 7.1 %collective-permute-start.1 = (bf16[256,512]{1,0:T(8,128)(2,1)S(1)}, bf16[256,512]{1,0:T(8,128)(2,1)S(1)}, u32[]{:S(2)}, u32[]{:S(2)}) collective-permute-start(bf16[256,512]{1,0:T(8,128)(2,1)S(1)} %bitcast.6), channel_id=1, source_target_pairs={{0,8},{8,0},{16,24},{24,16},{32,40},{40,32},{48,56},{56,48},{64,72... | collective-permute-start | bytes 786440 | tf_op jit(solution)/shard_map/ppermute | solution.py:250

commit v7 on v5

--- a/solution.py
+++ b/solution.py
@@ -154,11 +154,18 @@
             out_ref[p, r:r + GROUP * half, :] = both_k.astype(BF16)
 
 
+def join_kernel(near_ref, far_ref, out_ref):
+    rows = near_ref.shape[0]
+    out_ref[:rows] = near_ref[...]
+    out_ref[rows:] = far_ref[...]
+
+
 def valid_kernel(own_ref, half_ref, other_ref, out_ref, squares_ref):
     count = half_ref.shape[0]
     place = lax.broadcasted_iota(jnp.int32, (8, 2 * count), 1)
     core = ((place >> 8) ^ own_ref[0]) & 1
-    index = (((place >> 3) & 31) << 3) | (core << 2) | ((place >> 1) & 3)
+    far = ((place >> 7) ^ (own_ref[0] >> 2)) & 1
+    index = (((place >> 4) & 7) << 5) | (far << 4) | (((place >> 3) & 1) << 3) | (core << 2) | ((place >> 1) & 3)
     row = lax.broadcasted_iota(jnp.int32, (count, 2 * count), 0)
     squares = jnp.zeros((count, 128), F32)
     for h in range(2):
@@ -228,10 +235,18 @@
     scaling = math.sqrt(kl * proj)
 
     own_valid = valid_grads.reshape(-1, owned, 2, 8).transpose(0, 3, 2, 1).reshape(1, -1, owned * proj // 2)
-    own_valid = jnp.broadcast_to(own_valid, (groups // 2,) + own_valid.shape[1:])
-    same_core = [[i * 2 + c for i in range(groups // 2)] for c in range(2)]
-    half = lax.all_to_all(own_valid, "ex", 0, 0, tiled=True, axis_index_groups=same_core)
-    half = half.reshape(valid_count, owned * proj // 2)
+    own_valid = jnp.broadcast_to(own_valid, (groups // 4,) + own_valid.shape[1:])
+    members = [[y * 8 + z * 4 + i * 2 + c for y in range(groups // 8) for i in range(2)] for z in range(2) for c in range(2)]
+    near = lax.all_to_all(own_valid, "ex", 0, 0, tiled=True, axis_index_groups=members)
+    near = near.reshape(valid_count // 2, owned * proj // 2)
+    far = lax.ppermute(near, "ex", [(i, i ^ 4) for i in range(groups)])
+    half = call(
+        join_kernel,
+        jax.ShapeDtypeStruct((valid_count, owned * proj // 2), BF16),
+        0,
+        2 * valid_count * owned * proj,
+        args=(on_chip(near), on_chip(far)),
+    )
     other = lax.ppermute(half, "ex", [(i, i ^ 1) for i in range(groups)])
     own_group = jnp.full((1,), lax.axis_index("ex"), jnp.int32)
     valid, valid_squares = call(

time: 70.5 us -> 77.9 us (1.10)
  the two profiles are of different devices: /device:TPU:8 before, /device:TPU:1 now
where the time goes in v7:
time: 77.9 us; the launch traced here: 77.5 us
  starting transfers between devices  38.5 us (49%)
  waiting for transfers between devices  15.8 us (20%)
  blocking collectives  12.3 us (16%)
  Pallas kernels  9.7 us (12%)
  local copies, waits for them, and re-layouts  1.04 us (1%)
    all_to_all x1, blocking collectives, scores_of(): products = lax.all_to_all(products, 'feat', 0, 0, tiled=True)  12.3 us
    all_to_all x1, starting transfers between devices, scores_of(): lax.all_to_all(own_valid, 'ex', 0, 0, tiled=True, axis_index_groups=members)  11.7 us
    pallas_call x7, Pallas kernels, call(): pl.pallas_call(kernel, out_shape=out_shape, in_specs=specs, out_specs=jax...  9.7 us
    ppermute x1, starting transfers between devices, scores_of(): other = lax.ppermute(half, 'ex', [(i, i ^ 1) for i in range(groups)])  8.77 us
    ppermute x1, starting transfers between devices, scores_of(): far = lax.ppermute(near, 'ex', [(i, i ^ 4) for i in range(groups)])  7.94 us
    all_to_all x1, starting transfers between devices, scores_of(): right_parts = lax.all_to_all(right_parts, 'feat', 0, 0, tiled=True)  6.66 us
    all_to_all x1, waiting for transfers between devices, scores_of(): right_parts = lax.all_to_all(right_parts, 'feat', 0, 0, tiled=True)  6.44 us
    ppermute x1, waiting for transfers between devices, scores_of(): far = lax.ppermute(near, 'ex', [(i, i ^ 4) for i in range(groups)])  4.29 us
  transfers between devices with their start and end apart: 5, of which 4 were waited for; matrix products, arithmetic and copies ran while one was open for 0% of the time, Pallas kernels for 8%

profile of v7, /device:TPU:1, one launch (start us, length us, event | category | flops | bytes accessed | tf_op | source)
XLA Modules:
  0.0 77.5 jit_solution(10210361992281084356)
XLA Ops:
  0.0 0.0 copy-start.1
  0.0 2.4 %shard_map.73 = bf16[8,32,768]{2,1,0:T(8,128)(2,1)} custom-call(bf16[2,768,256]{2,1,0:T(8,128)(2,1)} %bitcast.8, bf16[2,128,256]{2,1,0:T(8,128)(2,1)} %a_hbm.1, bf16[2,16,128]{2,1,0:T(8,128)(2,1)} %bitcast.10), custom_call_target="tpu_custom_call" | custom-call | flops 201326592 | bytes 786432 | tf_op jit(solution)/shard_map/pallas_call | solution.py:44
  2.4 6.7 %all-to-all-start = ((bf16[8,32,768]{2,1,0:T(8,128)(2,1)}), bf16[8,32,768]{2,1,0:T(8,128)(2,1)S(1)}, u32[]{:S(2)}, u32[]{:S(2)}) async-start(bf16[8,32,768]{2,1,0:T(8,128)(2,1)} %shard_map.73), calls=%async_computation | async-start | bytes 786432 | tf_op jit(solution)/shard_map/all_to_all | solution.py:274
  9.1 0.0 copy-done.1
  9.1 0.2 reshape.16
  9.3 0.1 copy.8
  9.4 0.1 broadcast_in_dim.11
  9.5 6.4 %all-to-all-done.rr_ref = bf16[8,32,768]{2,1,0:T(8,128)(2,1)S(1)} async-done(((bf16[8,32,768]{2,1,0:T(8,128)(2,1)}), bf16[8,32,768]{2,1,0:T(8,128)(2,1)S(1)}, u32[]{:S(2)}, u32[]{:S(2)}) %all-to-all-start) | async-done | bytes 393248 | tf_op jit(solution)/shard_map/all_to_all | solution.py:274
  15.9 0.7 broadcast_in_dim.12
  16.6 0.0 copy-start
  16.6 11.7 %all-to-all-start.2 = ((bf16[16,8,512]{2,1,0:T(8,128)(2,1)}), bf16[16,8,512]{2,1,0:T(8,128)(2,1)S(1)}, u32[]{:S(2)}, u32[]{:S(2)}) async-start(bf16[16,8,512]{2,1,0:T(8,128)(2,1)} %broadcast_in_dim.12), calls=%async_computation.2 | async-start | bytes 262144 | tf_op jit(solution)/shard_map/all_to_all | solution.py:240
  28.2 3.2 %shard_map.74 = (bf16[2,768,512]{2,1,0:T(8,128)(2,1)S(1)}, bf16[2,768,512]{2,1,0:T(8,128)(2,1)S(1)}) custom-call(bf16[2,768,512]{2,1,0:T(8,128)(2,1)} %bitcast.11, bf16[2,512,512]{2,1,0:T(8,128)(2,1)} %l_hbm.1), custom_call_target="tpu_custom_call" | custom-call | flops 805306368 | bytes 5767168 | tf_op jit(solution)/shard_map/pallas_call | solution.py:44
  31.4 0.0 copy-done
  31.5 2.2 %shard_map.75 = bf16[8,256,128]{2,1,0:T(8,128)(2,1)} custom-call(s32[32]{0:T(128)S(1)} %copy-done, bf16[8,32,768]{2,1,0:T(8,128)(2,1)S(1)} %all-to-all-done.rr_ref, bf16[2,768,512]{2,1,0:T(8,128)(2,1)S(1)} %get-tuple-element.9.high_ref, bf16[2,768,512]{2,1,0:T(8,128)(2,1)S(1)} %get-tuple-element.10.low_ref), custom_call_target="tpu_custom_call" | custom-call | flops 402653184 | bytes 3145728 | tf_op jit(solution)/shard_map/pallas_call | solution.py:44
  33.7 4.0 %all-to-all-done.2 = bf16[16,8,512]{2,1,0:T(8,128)(2,1)S(1)} async-done(((bf16[16,8,512]{2,1,0:T(8,128)(2,1)}), bf16[16,8,512]{2,1,0:T(8,128)(2,1)S(1)}, u32[]{:S(2)}, u32[]{:S(2)}) %all-to-all-start.2) | async-done | bytes 131104 | tf_op jit(solution)/shard_map/all_to_all | solution.py:240
  37.6 3.5 %all-to-all-start.1 = ((bf16[8,256,128]{2,1,0:T(8,128)(2,1)}), bf16[8,256,128]{2,1,0:T(8,128)(2,1)S(1)}, u32[]{:S(2)}, u32[]{:S(2)}) async-start(bf16[8,256,128]{2,1,0:T(8,128)(2,1)} %shard_map.75), calls=%async_computation.1 | async-start | bytes 1048576 | tf_op jit(solution)/shard_map/all_to_all | solution.py:295
  41.1 7.9 %collective-permute-start = (bf16[128,512]{1,0:T(8,128)(2,1)S(1)}, bf16[128,512]{1,0:T(8,128)(2,1)S(1)}, u32[]{:S(2)}, u32[]{:S(2)}) collective-permute-start(bf16[128,512]{1,0:T(8,128)(2,1)S(1)} %bitcast.6), channel_id=1, source_target_pairs={{0,32},{8,40},{16,48},{24,56},{32,0},{40,8},{48,16},{56,24},{64,96... | collective-permute-start | bytes 393224 | tf_op jit(solution)/shard_map/ppermute | solution.py:242
  49.1 4.3 %collective-permute-done.far_ref = bf16[128,512]{1,0:T(8,128)(2,1)S(1)} collective-permute-done((bf16[128,512]{1,0:T(8,128)(2,1)S(1)}, bf16[128,512]{1,0:T(8,128)(2,1)S(1)}, u32[]{:S(2)}, u32[]{:S(2)}) %collective-permute-start) | collective-permute-done | bytes 131104 | tf_op jit(solution)/shard_map/ppermute | solution.py:242
  53.4 8.8 %collective-permute-start.1 = (bf16[256,512]{1,0:T(8,128)(2,1)S(1)}, bf16[256,512]{1,0:T(8,128)(2,1)S(1)}, u32[]{:S(2)}, u32[]{:S(2)}) collective-permute-start(bf16[256,512]{1,0:T(8,128)(2,1)S(1)} %shard_map.76.half_ref), channel_id=1, source_target_pairs={{0,8},{8,0},{16,24},{24,16},{32,40},{40,32},{48,56},{56,48},{64,72... | collective-permute-start | bytes 786440 | tf_op jit(solution)/shard_map/ppermute | solution.py:250
  62.2 1.1 %collective-permute-done.1.other_ref = bf16[256,512]{1,0:T(8,128)(2,1)S(1)} collective-permute-done((bf16[256,512]{1,0:T(8,128)(2,1)S(1)}, bf16[256,512]{1,0:T(8,128)(2,1)S(1)}, u32[]{:S(2)}, u32[]{:S(2)}) %collective-permute-start.1) | collective-permute-done | bytes 262176 | tf_op jit(solution)/shard_map/ppermute | solution.py:250
  63.3 0.8 %shard_map.77 = (bf16[256,1024]{1,0:T(8,128)(2,1)S(1)}, f32[1,256]{1,0:T(1,128)S(1)}) custom-call(s32[1]{0:T(128)} %bitcast.3.own_ref, bf16[256,512]{1,0:T(8,128)(2,1)S(1)} %shard_map.76.half_ref, bf16[256,512]{1,0:T(8,128)(2,1)S(1)} %collective-permute-done.1.other_ref), custom_call_target="tpu_custom_call" | custom-call | flops 134217728 | bytes 1048576 | tf_op jit(solution)/shard_map/pallas_call | solution.py:44
  64.1 0.0 all-to-all-done.1.part_ref
  64.1 0.4 shard_map.78
  64.5 12.3 %all_to_all.20.part_ref = f32[8,40,256]{2,1,0:T(8,128)S(1)} all-to-all(f32[8,40,256]{2,1,0:T(8,128)S(1)} %shard_map.78), channel_id=1, replica_groups=mesh['ex'=64,'feat'=8] {'feat'}, dimensions={0} | all-to-all | bytes 655360 | tf_op jit(solution)/shard_map/all_to_all | solution.py:304
  76.8 0.7 shard_map.79
  (1 shorter events, 0.0 us)
Async XLA Ops:
  0.0 9.1 %copy-start.1 = (bf16[4,1024]{1,0:T(4,128)(2,1)S(1)}, bf16[4,1024]{1,0:T(4,128)(2,1)}, u32[]{:S(2)}) copy-start(bf16[4,1024]{1,0:T(4,128)(2,1)} %param.13) | copy-start | bytes 24580
  2.4 13.5 %all-to-all-start = ((bf16[8,32,768]{2,1,0:T(8,128)(2,1)}), bf16[8,32,768]{2,1,0:T(8,128)(2,1)S(1)}, u32[]{:S(2)}, u32[]{:S(2)}) async-start(bf16[8,32,768]{2,1,0:T(8,128)(2,1)} %shard_map.73), calls=%async_computation | async-start | bytes 786432 | tf_op jit(solution)/shard_map/all_to_all | solution.py:274
  16.6 14.9 %copy-start = (s32[32]{0:T(128)S(1)}, s32[32]{0:T(128)}, u32[]{:S(2)}) copy-start(s32[32]{0:T(128)} %seq_ref.1) | copy-start | bytes 388
  16.6 21.0 %all-to-all-start.2 = ((bf16[16,8,512]{2,1,0:T(8,128)(2,1)}), bf16[16,8,512]{2,1,0:T(8,128)(2,1)S(1)}, u32[]{:S(2)}, u32[]{:S(2)}) async-start(bf16[16,8,512]{2,1,0:T(8,128)(2,1)} %broadcast_in_dim.12), calls=%async_computation.2 | async-start | bytes 262144 | tf_op jit(solution)/shard_map/all_to_all | solution.py:240
  37.6 26.5 %all-to-all-start.1 = ((bf16[8,256,128]{2,1,0:T(8,128)(2,1)}), bf16[8,256,128]{2,1,0:T(8,128)(2,1)S(1)}, u32[]{:S(2)}, u32[]{:S(2)}) async-start(bf16[8,256,128]{2,1,0:T(8,128)(2,1)} %shard_map.75), calls=%async_computation.1 | async-start | bytes 1048576 | tf_op jit(solution)/shard_map/all_to_all | solution.py:295
  41.1 12.2 %collective-permute-start = (bf16[128,512]{1,0:T(8,128)(2,1)S(1)}, bf16[128,512]{1,0:T(8,128)(2,1)S(1)}, u32[]{:S(2)}, u32[]{:S(2)}) collective-permute-start(bf16[128,512]{1,0:T(8,128)(2,1)S(1)} %bitcast.6), channel_id=1, source_target_pairs={{0,32},{8,40},{16,48},{24,56},{32,0},{40,8},{48,16},{56,24},{64,96... | collective-permute-start | bytes 393224 | tf_op jit(solution)/shard_map/ppermute | solution.py:242
  53.4 9.9 %collective-permute-start.1 = (bf16[256,512]{1,0:T(8,128)(2,1)S(1)}, bf16[256,512]{1,0:T(8,128)(2,1)S(1)}, u32[]{:S(2)}, u32[]{:S(2)}) collective-permute-start(bf16[256,512]{1,0:T(8,128)(2,1)S(1)} %shard_map.76.half_ref), channel_id=1, source_target_pairs={{0,8},{8,0},{16,24},{24,16},{32,40},{40,32},{48,56},{56,48},{64,72... | collective-permute-start | bytes 786440 | tf_op jit(solution)/shard_map/ppermute | solution.py:250

commit v8 on v7

--- a/solution.py
+++ b/solution.py
@@ -38,16 +38,20 @@
     return tuple(pltpu.VMEM(x.shape, x.dtype) for x in arrays)
 
 
-def call(kernel, out_shape, flops, bytes_accessed, scratch=(), smem=0, args=(), hbm=False):
+def call(kernel, out_shape, flops, bytes_accessed, scratch=(), smem=0, args=(), hbm=(), hbm_out=()):
     specs = [pl.BlockSpec(memory_space=pltpu.SMEM)] * smem
-    specs += [pl.BlockSpec(memory_space=pltpu.HBM if hbm else pltpu.VMEM)] * (len(args) - smem)
+    specs += [pl.BlockSpec(memory_space=pltpu.HBM if n in hbm else pltpu.VMEM) for n in range(smem, len(args))]
+    if isinstance(out_shape, tuple):
+        out_specs = tuple(
+            pl.BlockSpec(memory_space=pltpu.HBM if n in hbm_out else pltpu.VMEM) for n in range(len(out_shape))
+        )
+    else:
+        out_specs = pl.BlockSpec(memory_space=pltpu.VMEM)
     return pl.pallas_call(
         kernel,
         out_shape=out_shape,
         in_specs=specs,
-        out_specs=jax.tree.map(
-            lambda _: pl.BlockSpec(memory_space=pltpu.VMEM), out_shape, is_leaf=lambda x: hasattr(x, "shape")
-        ),
+        out_specs=out_specs,
         scratch_shapes=list(scratch),
         cost_estimate=pl.CostEstimate(flops=flops, bytes_accessed=bytes_accessed, transcendentals=0),
         compiler_params=pltpu.CompilerParams(vmem_limit_bytes=VMEM_LIMIT),
@@ -79,7 +83,7 @@
             out_ref[p, l * proj:(l + 1) * proj, :] = rows
 
 
-def left_kernel(c_hbm, l_hbm, high_ref, low_ref, c_ref, l_ref, sems):
+def left_kernel(c_hbm, l_hbm, high_ref, low_hbm, c_ref, l_ref, low_ref, sems):
     layers, tokens, _ = c_ref.shape
     step = LEFT_STEP
     factors, pieces = [], []
@@ -91,16 +95,23 @@
             copy = pltpu.make_async_copy(c_hbm.at[l, rows], c_ref.at[l, rows], sems.at[layers + len(pieces)])
             copy.start()
             pieces.append((l, t, copy))
+    stores = []
     for l, t, copy in pieces:
         if t == 0:
             factors[l].wait()
         copy.wait()
+        rows = pl.ds(t, step)
         high, low = split(dot(c_ref[l, t:t + step, :], l_ref[l], NT))
         high_ref[l, t:t + step, :] = high
         low_ref[l, t:t + step, :] = low
-
-
-def project_kernel(seq_ref, rr_ref, high_ref, low_ref, out_ref):
+        sem = sems.at[layers + len(pieces) + len(stores)]
+        stores.append(pltpu.make_async_copy(low_ref.at[l, rows], low_hbm.at[l, rows], sem))
+        stores[-1].start()
+    for store in stores:
+        store.wait()
+
+
+def project_kernel(seq_ref, rr_ref, high_ref, low_hbm, out_ref, low_ref, sems):
     peers, two_proj, tokens = rr_ref.shape
     layers, _, kl = high_ref.shape
     proj = two_proj // layers
@@ -110,6 +121,14 @@
     seq = tokens // examples
     span = GROUP * seq
     width = 2 * 128
+    chunk = 2 * span
+    loads = []
+    for t in range(0, tokens, chunk):
+        rows = pl.ds(t, chunk)
+        for l in range(layers):
+            load = pltpu.make_async_copy(low_hbm.at[l, rows], low_ref.at[l, rows], sems.at[len(loads)])
+            load.start()
+            loads.append(load)
     total = rr_ref[0].astype(F32)
     for p in range(1, peers):
         total = total + rr_ref[p].astype(F32)
@@ -133,6 +152,9 @@
         both = jnp.concatenate([high, low], axis=0)[:, :layers * span]
         high = high[:, :layers * span]
         t = g * span
+        if t % chunk == 0:
+            for l in range(layers):
+                loads[t // chunk * layers + l].wait()
         left_high = jnp.concatenate([high_ref[l, t:t + span, :] for l in range(layers)], axis=0)
         left_low = jnp.concatenate([low_ref[l, t:t + span, :] for l in range(layers)], axis=0)
         rows = GROUP * proj
@@ -269,28 +291,35 @@
         proj_inputs.size * 2,
         scratch=(*staged(right_in), pltpu.SemaphoreType.DMA((2 + layers,))),
         args=tuple(off_chip(x) for x in right_in),
-        hbm=True,
+        hbm=(0, 1, 2),
     )
     right_parts = lax.all_to_all(right_parts, "feat", 0, 0, tiled=True)
 
-    left_shape = pltpu.VMEM((layers, tokens, kl), BF16)
+    left_shape = (layers, tokens, kl)
+    left_copies = layers * tokens // LEFT_STEP
     left_in = (out_cotangent.reshape(layers, tokens, width), left_factor)
     left_high, left_low = call(
         left_kernel,
-        (left_shape, left_shape),
+        (pltpu.VMEM(left_shape, BF16), pltpu.HBM(left_shape, BF16)),
         2 * layers * tokens * width * kl,
         (out_cotangent.size + left_factor.size) * 2 + layers * tokens * kl * 4,
-        scratch=(*staged(left_in), pltpu.SemaphoreType.DMA((layers + layers * tokens // LEFT_STEP,))),
+        scratch=(*staged(left_in), pltpu.VMEM(left_shape, BF16), pltpu.SemaphoreType.DMA((layers + 2 * left_copies,))),
         args=tuple(off_chip(x) for x in left_in),
-        hbm=True,
+        hbm=(0, 1),
+        hbm_out=(1,),
     )
     parts = call(
         project_kernel,
         pltpu.VMEM((peers, examples * 8, 128), BF16),
         2 * layers * tokens * kl * 256,
         layers * tokens * kl * 4,
+        scratch=(
+            pltpu.VMEM(left_shape, BF16),
+            pltpu.SemaphoreType.DMA((layers * examples // (2 * GROUP),)),
+        ),
         smem=1,
-        args=(seq_lengths, on_chip(right_parts), on_chip(left_high), on_chip(left_low)),
+        args=(seq_lengths, on_chip(right_parts), on_chip(left_high), off_chip(left_low)),
+        hbm=(3,),
     )
     parts = lax.all_to_all(parts, "feat", 0, 0, tiled=True)
     products = call(

time: 77.9 us -> 78 us (level)
  Pallas kernels: 9.7 us -> 12.1 us
  waiting for transfers between devices: 15.8 us -> 13.4 us
    all_to_all x1, waiting for transfers between devices: 3.96 us -> 1.51 us  [scores_of(): lax.all_to_all(own_valid, 'ex', 0, 0, tiled=True, axis_index_groups=members)]
    pallas_call x7, Pallas kernels: 9.7 us -> 12.1 us  [call(): pl.pallas_call(kernel, out_shape=out_shape, in_specs=specs, out_specs=out...]
  transfers between devices with their start and end apart: 5 -> 5, of which waited for: 4 -> 4; matrix products, arithmetic and copies ran while one was open for 0% -> 0% of each run, Pallas kernels for 8% -> 11%
where the time goes in v8:
time: 78 us; the launch traced here: 77.5 us
  starting transfers between devices  38.5 us (49%)
  waiting for transfers between devices  13.4 us (17%)
  blocking collectives  12.3 us (16%)
  Pallas kernels  12.1 us (16%)
  local copies, waits for them, and re-layouts  1.05 us (1%)
    all_to_all x1, blocking collectives, scores_of(): products = lax.all_to_all(products, 'feat', 0, 0, tiled=True)  12.3 us
    pallas_call x7, Pallas kernels, call(): pl.pallas_call(kernel, out_shape=out_shape, in_specs=specs, out_specs=out...  12.1 us
    all_to_all x1, starting transfers between devices, scores_of(): lax.all_to_all(own_valid, 'ex', 0, 0, tiled=True, axis_index_groups=members)  11.7 us
    ppermute x1, starting transfers between devices, scores_of(): other = lax.ppermute(half, 'ex', [(i, i ^ 1) for i in range(groups)])  8.77 us
    ppermute x1, starting transfers between devices, scores_of(): far = lax.ppermute(near, 'ex', [(i, i ^ 4) for i in range(groups)])  7.94 us
    all_to_all x1, starting transfers between devices, scores_of(): right_parts = lax.all_to_all(right_parts, 'feat', 0, 0, tiled=True)  6.66 us
    all_to_all x1, waiting for transfers between devices, scores_of(): right_parts = lax.all_to_all(right_parts, 'feat', 0, 0, tiled=True)  6.44 us
    ppermute x1, waiting for transfers between devices, scores_of(): far = lax.ppermute(near, 'ex', [(i, i ^ 4) for i in range(groups)])  4.29 us
  transfers between devices with their start and end apart: 5, of which 4 were waited for; matrix products, arithmetic and copies ran while one was open for 0% of the time, Pallas kernels for 11%

profile of v8, /device:TPU:1, one launch (start us, length us, event | category | flops | bytes accessed | tf_op | source)
XLA Modules:
  0.0 77.5 jit_solution(3951347302508085169)
XLA Ops:
  0.0 0.0 copy-start.1
  0.0 2.4 %shard_map.73 = bf16[8,32,768]{2,1,0:T(8,128)(2,1)} custom-call(bf16[2,768,256]{2,1,0:T(8,128)(2,1)} %bitcast.8, bf16[2,128,256]{2,1,0:T(8,128)(2,1)} %a_hbm.1, bf16[2,16,128]{2,1,0:T(8,128)(2,1)} %bitcast.10), custom_call_target="tpu_custom_call" | custom-call | flops 201326592 | bytes 786432 | tf_op jit(solution)/shard_map/pallas_call | solution.py:50
  2.4 6.7 %all-to-all-start = ((bf16[8,32,768]{2,1,0:T(8,128)(2,1)}), bf16[8,32,768]{2,1,0:T(8,128)(2,1)S(1)}, u32[]{:S(2)}, u32[]{:S(2)}) async-start(bf16[8,32,768]{2,1,0:T(8,128)(2,1)} %shard_map.73), calls=%async_computation | async-start | bytes 786432 | tf_op jit(solution)/shard_map/all_to_all | solution.py:296
  9.1 0.0 copy-done.1
  9.1 0.2 reshape.16
  9.3 0.1 copy.8
  9.4 0.1 broadcast_in_dim.11
  9.5 6.4 %all-to-all-done.rr_ref = bf16[8,32,768]{2,1,0:T(8,128)(2,1)S(1)} async-done(((bf16[8,32,768]{2,1,0:T(8,128)(2,1)}), bf16[8,32,768]{2,1,0:T(8,128)(2,1)S(1)}, u32[]{:S(2)}, u32[]{:S(2)}) %all-to-all-start) | async-done | bytes 393248 | tf_op jit(solution)/shard_map/all_to_all | solution.py:296
  15.9 0.7 broadcast_in_dim.12
  16.6 0.0 copy-start
  16.6 11.7 %all-to-all-start.2 = ((bf16[16,8,512]{2,1,0:T(8,128)(2,1)}), bf16[16,8,512]{2,1,0:T(8,128)(2,1)S(1)}, u32[]{:S(2)}, u32[]{:S(2)}) async-start(bf16[16,8,512]{2,1,0:T(8,128)(2,1)} %broadcast_in_dim.12), calls=%async_computation.2 | async-start | bytes 262144 | tf_op jit(solution)/shard_map/all_to_all | solution.py:262
  28.2 4.0 %shard_map.74 = (bf16[2,768,512]{2,1,0:T(8,128)(2,1)S(1)}, bf16[2,768,512]{2,1,0:T(8,128)(2,1)}) custom-call(bf16[2,768,512]{2,1,0:T(8,128)(2,1)} %bitcast.11, bf16[2,512,512]{2,1,0:T(8,128)(2,1)} %l_hbm.1), custom_call_target="tpu_custom_call" | custom-call | flops 805306368 | bytes 5767168 | tf_op jit(solution)/shard_map/pallas_call | solution.py:50
  32.2 0.0 copy-done
  32.2 3.9 %shard_map.75 = bf16[8,256,128]{2,1,0:T(8,128)(2,1)} custom-call(s32[32]{0:T(128)S(1)} %copy-done, bf16[8,32,768]{2,1,0:T(8,128)(2,1)S(1)} %all-to-all-done.rr_ref, bf16[2,768,512]{2,1,0:T(8,128)(2,1)S(1)} %get-tuple-element.9.high_ref, bf16[2,768,512]{2,1,0:T(8,128)(2,1)} %get-tuple-element.10.low_hbm), custom_call_target="tpu_custom_call" | custom-call | flops 402653184 | bytes 3145728 | tf_op jit(solution)/shard_map/pallas_call | solution.py:50
  36.1 1.5 %all-to-all-done.2 = bf16[16,8,512]{2,1,0:T(8,128)(2,1)S(1)} async-done(((bf16[16,8,512]{2,1,0:T(8,128)(2,1)}), bf16[16,8,512]{2,1,0:T(8,128)(2,1)S(1)}, u32[]{:S(2)}, u32[]{:S(2)}) %all-to-all-start.2) | async-done | bytes 131104 | tf_op jit(solution)/shard_map/all_to_all | solution.py:262
  37.6 3.5 %all-to-all-start.1 = ((bf16[8,256,128]{2,1,0:T(8,128)(2,1)}), bf16[8,256,128]{2,1,0:T(8,128)(2,1)S(1)}, u32[]{:S(2)}, u32[]{:S(2)}) async-start(bf16[8,256,128]{2,1,0:T(8,128)(2,1)} %shard_map.75), calls=%async_computation.1 | async-start | bytes 1048576 | tf_op jit(solution)/shard_map/all_to_all | solution.py:324
  41.1 7.9 %collective-permute-start = (bf16[128,512]{1,0:T(8,128)(2,1)S(1)}, bf16[128,512]{1,0:T(8,128)(2,1)S(1)}, u32[]{:S(2)}, u32[]{:S(2)}) collective-permute-start(bf16[128,512]{1,0:T(8,128)(2,1)S(1)} %bitcast.6), channel_id=1, source_target_pairs={{0,32},{8,40},{16,48},{24,56},{32,0},{40,8},{48,16},{56,24},{64,96... | collective-permute-start | bytes 393224 | tf_op jit(solution)/shard_map/ppermute | solution.py:264
  49.1 4.3 %collective-permute-done.far_ref = bf16[128,512]{1,0:T(8,128)(2,1)S(1)} collective-permute-done((bf16[128,512]{1,0:T(8,128)(2,1)S(1)}, bf16[128,512]{1,0:T(8,128)(2,1)S(1)}, u32[]{:S(2)}, u32[]{:S(2)}) %collective-permute-start) | collective-permute-done | bytes 131104 | tf_op jit(solution)/shard_map/ppermute | solution.py:264
  53.4 8.8 %collective-permute-start.1 = (bf16[256,512]{1,0:T(8,128)(2,1)S(1)}, bf16[256,512]{1,0:T(8,128)(2,1)S(1)}, u32[]{:S(2)}, u32[]{:S(2)}) collective-permute-start(bf16[256,512]{1,0:T(8,128)(2,1)S(1)} %shard_map.76.half_ref), channel_id=1, source_target_pairs={{0,8},{8,0},{16,24},{24,16},{32,40},{40,32},{48,56},{56,48},{64,72... | collective-permute-start | bytes 786440 | tf_op jit(solution)/shard_map/ppermute | solution.py:272
  62.2 1.1 %collective-permute-done.1.other_ref = bf16[256,512]{1,0:T(8,128)(2,1)S(1)} collective-permute-done((bf16[256,512]{1,0:T(8,128)(2,1)S(1)}, bf16[256,512]{1,0:T(8,128)(2,1)S(1)}, u32[]{:S(2)}, u32[]{:S(2)}) %collective-permute-start.1) | collective-permute-done | bytes 262176 | tf_op jit(solution)/shard_map/ppermute | solution.py:272
  63.3 0.8 %shard_map.77 = (bf16[256,1024]{1,0:T(8,128)(2,1)S(1)}, f32[1,256]{1,0:T(1,128)S(1)}) custom-call(s32[1]{0:T(128)} %bitcast.3.own_ref, bf16[256,512]{1,0:T(8,128)(2,1)S(1)} %shard_map.76.half_ref, bf16[256,512]{1,0:T(8,128)(2,1)S(1)} %collective-permute-done.1.other_ref), custom_call_target="tpu_custom_call" | custom-call | flops 134217728 | bytes 1048576 | tf_op jit(solution)/shard_map/pallas_call | solution.py:50
  64.1 0.0 all-to-all-done.1.part_ref
  64.1 0.4 shard_map.78
  64.5 12.3 %all_to_all.20.part_ref = f32[8,40,256]{2,1,0:T(8,128)S(1)} all-to-all(f32[8,40,256]{2,1,0:T(8,128)S(1)} %shard_map.78), channel_id=1, replica_groups=mesh['ex'=64,'feat'=8] {'feat'}, dimensions={0} | all-to-all | bytes 655360 | tf_op jit(solution)/shard_map/all_to_all | solution.py:333
  76.8 0.7 shard_map.79
  (1 shorter events, 0.0 us)
Async XLA Ops:
  0.0 9.1 %copy-start.1 = (bf16[4,1024]{1,0:T(4,128)(2,1)S(1)}, bf16[4,1024]{1,0:T(4,128)(2,1)}, u32[]{:S(2)}) copy-start(bf16[4,1024]{1,0:T(4,128)(2,1)} %param.13) | copy-start | bytes 24580
  2.4 13.5 %all-to-all-start = ((bf16[8,32,768]{2,1,0:T(8,128)(2,1)}), bf16[8,32,768]{2,1,0:T(8,128)(2,1)S(1)}, u32[]{:S(2)}, u32[]{:S(2)}) async-start(bf16[8,32,768]{2,1,0:T(8,128)(2,1)} %shard_map.73), calls=%async_computation | async-start | bytes 786432 | tf_op jit(solution)/shard_map/all_to_all | solution.py:296
  16.6 15.6 %copy-start = (s32[32]{0:T(128)S(1)}, s32[32]{0:T(128)}, u32[]{:S(2)}) copy-start(s32[32]{0:T(128)} %seq_ref.1) | copy-start | bytes 388
  16.6 21.0 %all-to-all-start.2 = ((bf16[16,8,512]{2,1,0:T(8,128)(2,1)}), bf16[16,8,512]{2,1,0:T(8,128)(2,1)S(1)}, u32[]{:S(2)}, u32[]{:S(2)}) async-start(bf16[16,8,512]{2,1,0:T(8,128)(2,1)} %broadcast_in_dim.12), calls=%async_computation.2 | async-start | bytes 262144 | tf_op jit(solution)/shard_map/all_to_all | solution.py:262
  37.6 26.5 %all-to-all-start.1 = ((bf16[8,256,128]{2,1,0:T(8,128)(2,1)}), bf16[8,256,128]{2,1,0:T(8,128)(2,1)S(1)}, u32[]{:S(2)}, u32[]{:S(2)}) async-start(bf16[8,256,128]{2,1,0:T(8,128)(2,1)} %shard_map.75), calls=%async_computation.1 | async-start | bytes 1048576 | tf_op jit(solution)/shard_map/all_to_all | solution.py:324
  41.1 12.2 %collective-permute-start = (bf16[128,512]{1,0:T(8,128)(2,1)S(1)}, bf16[128,512]{1,0:T(8,128)(2,1)S(1)}, u32[]{:S(2)}, u32[]{:S(2)}) collective-permute-start(bf16[128,512]{1,0:T(8,128)(2,1)S(1)} %bitcast.6), channel_id=1, source_target_pairs={{0,32},{8,40},{16,48},{24,56},{32,0},{40,8},{48,16},{56,24},{64,96... | collective-permute-start | bytes 393224 | tf_op jit(solution)/shard_map/ppermute | solution.py:264
  53.4 9.9 %collective-permute-start.1 = (bf16[256,512]{1,0:T(8,128)(2,1)S(1)}, bf16[256,512]{1,0:T(8,128)(2,1)S(1)}, u32[]{:S(2)}, u32[]{:S(2)}) collective-permute-start(bf16[256,512]{1,0:T(8,128)(2,1)S(1)} %shard_map.76.half_ref), channel_id=1, source_target_pairs={{0,8},{8,0},{16,24},{24,16},{32,40},{40,32},{48,56},{56,48},{64,72... | collective-permute-start | bytes 786440 | tf_op jit(solution)/shard_map/ppermute | solution.py:272

commit v9 on v8

--- a/solution.py
+++ b/solution.py
@@ -11,7 +11,8 @@
 F32 = jnp.float32
 BF16 = jnp.bfloat16
 VMEM_LIMIT = 24 << 20
-LEFT_STEP = 256
+LEFT_STEP = 192
+LOW_KEPT = 576
 GROUP = 4
 NT = (((1,), (1,)), ((), ()))
 NN = (((1,), (0,)), ((), ()))
@@ -83,8 +84,9 @@
             out_ref[p, l * proj:(l + 1) * proj, :] = rows
 
 
-def left_kernel(c_hbm, l_hbm, high_ref, low_hbm, c_ref, l_ref, low_ref, sems):
+def left_kernel(c_hbm, l_hbm, high_ref, kept_ref, low_hbm, c_ref, l_ref, low_ref, sems):
     layers, tokens, _ = c_ref.shape
+    kept = kept_ref.shape[1]
     step = LEFT_STEP
     factors, pieces = [], []
     for l in range(layers):
@@ -100,10 +102,13 @@
         if t == 0:
             factors[l].wait()
         copy.wait()
-        rows = pl.ds(t, step)
         high, low = split(dot(c_ref[l, t:t + step, :], l_ref[l], NT))
         high_ref[l, t:t + step, :] = high
-        low_ref[l, t:t + step, :] = low
+        if t < kept:
+            kept_ref[l, t:t + step, :] = low
+            continue
+        low_ref[l, t - kept:t - kept + step, :] = low
+        rows = pl.ds(t - kept, step)
         sem = sems.at[layers + len(pieces) + len(stores)]
         stores.append(pltpu.make_async_copy(low_ref.at[l, rows], low_hbm.at[l, rows], sem))
         stores[-1].start()
@@ -111,7 +116,7 @@
         store.wait()
 
 
-def project_kernel(seq_ref, rr_ref, high_ref, low_hbm, out_ref, low_ref, sems):
+def project_kernel(seq_ref, rr_ref, high_ref, kept_ref, low_hbm, out_ref, low_ref, sems):
     peers, two_proj, tokens = rr_ref.shape
     layers, _, kl = high_ref.shape
     proj = two_proj // layers
@@ -121,9 +126,10 @@
     seq = tokens // examples
     span = GROUP * seq
     width = 2 * 128
+    kept = kept_ref.shape[1]
     chunk = 2 * span
     loads = []
-    for t in range(0, tokens, chunk):
+    for t in range(0, tokens - kept, chunk):
         rows = pl.ds(t, chunk)
         for l in range(layers):
             load = pltpu.make_async_copy(low_hbm.at[l, rows], low_ref.at[l, rows], sems.at[len(loads)])
@@ -152,11 +158,12 @@
         both = jnp.concatenate([high, low], axis=0)[:, :layers * span]
         high = high[:, :layers * span]
         t = g * span
-        if t % chunk == 0:
+        if t >= kept and (t - kept) % chunk == 0:
             for l in range(layers):
-                loads[t // chunk * layers + l].wait()
+                loads[(t - kept) // chunk * layers + l].wait()
+        source, first_row = (kept_ref, t) if t < kept else (low_ref, t - kept)
         left_high = jnp.concatenate([high_ref[l, t:t + span, :] for l in range(layers)], axis=0)
-        left_low = jnp.concatenate([low_ref[l, t:t + span, :] for l in range(layers)], axis=0)
+        left_low = jnp.concatenate([source[l, first_row:first_row + span, :] for l in range(layers)], axis=0)
         rows = GROUP * proj
         part = dot(both, left_high, NN)
         part = part[:rows] + part[rows:] + dot(high, left_low, NN)
@@ -296,17 +303,22 @@
     right_parts = lax.all_to_all(right_parts, "feat", 0, 0, tiled=True)
 
     left_shape = (layers, tokens, kl)
+    low_shape = (layers, tokens - LOW_KEPT, kl)
     left_copies = layers * tokens // LEFT_STEP
     left_in = (out_cotangent.reshape(layers, tokens, width), left_factor)
-    left_high, left_low = call(
+    left_high, left_kept, left_low = call(
         left_kernel,
-        (pltpu.VMEM(left_shape, BF16), pltpu.HBM(left_shape, BF16)),
+        (
+            pltpu.VMEM(left_shape, BF16),
+            pltpu.VMEM((layers, LOW_KEPT, kl), BF16),
+            pltpu.HBM(low_shape, BF16),
+        ),
         2 * layers * tokens * width * kl,
         (out_cotangent.size + left_factor.size) * 2 + layers * tokens * kl * 4,
-        scratch=(*staged(left_in), pltpu.VMEM(left_shape, BF16), pltpu.SemaphoreType.DMA((layers + 2 * left_copies,))),
+        scratch=(*staged(left_in), pltpu.VMEM(low_shape, BF16), pltpu.SemaphoreType.DMA((layers + 2 * left_copies,))),
         args=tuple(off_chip(x) for x in left_in),
         hbm=(0, 1),
-        hbm_out=(1,),
+        hbm_out=(2,),
     )
     parts = call(
         project_kernel,
@@ -314,12 +326,12 @@
         2 * layers * tokens * kl * 256,
         layers * tokens * kl * 4,
         scratch=(
-            pltpu.VMEM(left_shape, BF16),
+            pltpu.VMEM(low_shape, BF16),
             pltpu.SemaphoreType.DMA((layers * examples // (2 * GROUP),)),
         ),
         smem=1,
-        args=(seq_lengths, on_chip(right_parts), on_chip(left_high), off_chip(left_low)),
-        hbm=(3,),
+        args=(seq_lengths, on_chip(right_parts), on_chip(left_high), on_chip(left_kept), off_chip(left_low)),
+        hbm=(4,),
     )
     parts = lax.all_to_all(parts, "feat", 0, 0, tiled=True)
     products = call(

time: 78 us -> 78 us (level)
  no operation moved by 1% of the time
where the time goes in v9:
time: 78 us; the launch traced here: 77.5 us
  starting transfers between devices  38.5 us (49%)
  waiting for transfers between devices  13.4 us (17%)
  blocking collectives  12.3 us (16%)
  Pallas kernels  12.1 us (16%)
  local copies, waits for them, and re-layouts  1.04 us (1%)
    all_to_all x1, blocking collectives, scores_of(): products = lax.all_to_all(products, 'feat', 0, 0, tiled=True)  12.3 us
    pallas_call x7, Pallas kernels, call(): pl.pallas_call(kernel, out_shape=out_shape, in_specs=specs, out_specs=out...  12.1 us
    all_to_all x1, starting transfers between devices, scores_of(): lax.all_to_all(own_valid, 'ex', 0, 0, tiled=True, axis_index_groups=members)  11.7 us
    ppermute x1, starting transfers between devices, scores_of(): other = lax.ppermute(half, 'ex', [(i, i ^ 1) for i in range(groups)])  8.77 us
    ppermute x1, starting transfers between devices, scores_of(): far = lax.ppermute(near, 'ex', [(i, i ^ 4) for i in range(groups)])  7.94 us
    all_to_all x1, starting transfers between devices, scores_of(): right_parts = lax.all_to_all(right_parts, 'feat', 0, 0, tiled=True)  6.66 us
    all_to_all x1, waiting for transfers between devices, scores_of(): right_parts = lax.all_to_all(right_parts, 'feat', 0, 0, tiled=True)  6.44 us
    ppermute x1, waiting for transfers between devices, scores_of(): far = lax.ppermute(near, 'ex', [(i, i ^ 4) for i in range(groups)])  4.29 us
  transfers between devices with their start and end apart: 5, of which 4 were waited for; matrix products, arithmetic and copies ran while one was open for 0% of the time, Pallas kernels for 11%

profile of v9, /device:TPU:1, one launch (start us, length us, event | category | flops | bytes accessed | tf_op | source)
XLA Modules:
  0.0 77.5 jit_solution(14342660459624787757)
XLA Ops:
  0.0 0.0 copy-start.1
  0.0 2.4 %shard_map.73 = bf16[8,32,768]{2,1,0:T(8,128)(2,1)} custom-call(bf16[2,768,256]{2,1,0:T(8,128)(2,1)} %bitcast.8, bf16[2,128,256]{2,1,0:T(8,128)(2,1)} %a_hbm.1, bf16[2,16,128]{2,1,0:T(8,128)(2,1)} %bitcast.10), custom_call_target="tpu_custom_call" | custom-call | flops 201326592 | bytes 786432 | tf_op jit(solution)/shard_map/pallas_call | solution.py:51
  2.4 6.7 %all-to-all-start = ((bf16[8,32,768]{2,1,0:T(8,128)(2,1)}), bf16[8,32,768]{2,1,0:T(8,128)(2,1)S(1)}, u32[]{:S(2)}, u32[]{:S(2)}) async-start(bf16[8,32,768]{2,1,0:T(8,128)(2,1)} %shard_map.73), calls=%async_computation | async-start | bytes 786432 | tf_op jit(solution)/shard_map/all_to_all | solution.py:303
  9.1 0.0 copy-done.1
  9.1 0.2 reshape.16
  9.3 0.1 copy.8
  9.4 0.1 broadcast_in_dim.11
  9.5 6.4 %all-to-all-done.rr_ref = bf16[8,32,768]{2,1,0:T(8,128)(2,1)S(1)} async-done(((bf16[8,32,768]{2,1,0:T(8,128)(2,1)}), bf16[8,32,768]{2,1,0:T(8,128)(2,1)S(1)}, u32[]{:S(2)}, u32[]{:S(2)}) %all-to-all-start) | async-done | bytes 393248 | tf_op jit(solution)/shard_map/all_to_all | solution.py:303
  15.9 0.7 broadcast_in_dim.12
  16.6 0.0 copy-start
  16.6 11.7 %all-to-all-start.2 = ((bf16[16,8,512]{2,1,0:T(8,128)(2,1)}), bf16[16,8,512]{2,1,0:T(8,128)(2,1)S(1)}, u32[]{:S(2)}, u32[]{:S(2)}) async-start(bf16[16,8,512]{2,1,0:T(8,128)(2,1)} %broadcast_in_dim.12), calls=%async_computation.2 | async-start | bytes 262144 | tf_op jit(solution)/shard_map/all_to_all | solution.py:269
  28.2 4.6 %shard_map.74 = (bf16[2,768,512]{2,1,0:T(8,128)(2,1)S(1)}, bf16[2,576,512]{2,1,0:T(8,128)(2,1)S(1)}, bf16[2,192,512]{2,1,0:T(8,128)(2,1)}) custom-call(bf16[2,768,512]{2,1,0:T(8,128)(2,1)} %bitcast.11, bf16[2,512,512]{2,1,0:T(8,128)(2,1)} %l_hbm.1), custom_call_target="tpu_custom_call" | custom-call | flops 805306368 | bytes 5767168 | tf_op jit(solution)/shard_map/pallas_call | solution.py:51
  32.8 0.0 copy-done
  32.8 3.3 %shard_map.75 = bf16[8,256,128]{2,1,0:T(8,128)(2,1)} custom-call(s32[32]{0:T(128)S(1)} %copy-done, bf16[8,32,768]{2,1,0:T(8,128)(2,1)S(1)} %all-to-all-done.rr_ref, bf16[2,768,512]{2,1,0:T(8,128)(2,1)S(1)} %get-tuple-element.10.high_ref, bf16[2,576,512]{2,1,0:T(8,128)(2,1)S(1)} %get-tuple-element.11.kept_ref, bf16[2,192,512]{2,1,0:T(8,128)(2,1)} %get-tuple-element.12.low_hbm), custom_call_target="tpu_custom_call" | custom-call | flops 402653184 | bytes 3145728 | tf_op jit(solution)/shard_map/pallas_call | solution.py:51
  36.1 1.5 %all-to-all-done.2 = bf16[16,8,512]{2,1,0:T(8,128)(2,1)S(1)} async-done(((bf16[16,8,512]{2,1,0:T(8,128)(2,1)}), bf16[16,8,512]{2,1,0:T(8,128)(2,1)S(1)}, u32[]{:S(2)}, u32[]{:S(2)}) %all-to-all-start.2) | async-done | bytes 131104 | tf_op jit(solution)/shard_map/all_to_all | solution.py:269
  37.6 3.5 %all-to-all-start.1 = ((bf16[8,256,128]{2,1,0:T(8,128)(2,1)}), bf16[8,256,128]{2,1,0:T(8,128)(2,1)S(1)}, u32[]{:S(2)}, u32[]{:S(2)}) async-start(bf16[8,256,128]{2,1,0:T(8,128)(2,1)} %shard_map.75), calls=%async_computation.1 | async-start | bytes 1048576 | tf_op jit(solution)/shard_map/all_to_all | solution.py:336
  41.1 7.9 %collective-permute-start = (bf16[128,512]{1,0:T(8,128)(2,1)S(1)}, bf16[128,512]{1,0:T(8,128)(2,1)S(1)}, u32[]{:S(2)}, u32[]{:S(2)}) collective-permute-start(bf16[128,512]{1,0:T(8,128)(2,1)S(1)} %bitcast.6), channel_id=1, source_target_pairs={{0,32},{8,40},{16,48},{24,56},{32,0},{40,8},{48,16},{56,24},{64,96... | collective-permute-start | bytes 393224 | tf_op jit(solution)/shard_map/ppermute | solution.py:271
  49.1 4.3 %collective-permute-done.far_ref = bf16[128,512]{1,0:T(8,128)(2,1)S(1)} collective-permute-done((bf16[128,512]{1,0:T(8,128)(2,1)S(1)}, bf16[128,512]{1,0:T(8,128)(2,1)S(1)}, u32[]{:S(2)}, u32[]{:S(2)}) %collective-permute-start) | collective-permute-done | bytes 131104 | tf_op jit(solution)/shard_map/ppermute | solution.py:271
  53.4 8.8 %collective-permute-start.1 = (bf16[256,512]{1,0:T(8,128)(2,1)S(1)}, bf16[256,512]{1,0:T(8,128)(2,1)S(1)}, u32[]{:S(2)}, u32[]{:S(2)}) collective-permute-start(bf16[256,512]{1,0:T(8,128)(2,1)S(1)} %shard_map.76.half_ref), channel_id=1, source_target_pairs={{0,8},{8,0},{16,24},{24,16},{32,40},{40,32},{48,56},{56,48},{64,72... | collective-permute-start | bytes 786440 | tf_op jit(solution)/shard_map/ppermute | solution.py:279
  62.2 1.1 %collective-permute-done.1.other_ref = bf16[256,512]{1,0:T(8,128)(2,1)S(1)} collective-permute-done((bf16[256,512]{1,0:T(8,128)(2,1)S(1)}, bf16[256,512]{1,0:T(8,128)(2,1)S(1)}, u32[]{:S(2)}, u32[]{:S(2)}) %collective-permute-start.1) | collective-permute-done | bytes 262176 | tf_op jit(solution)/shard_map/ppermute | solution.py:279
  63.3 0.8 %shard_map.77 = (bf16[256,1024]{1,0:T(8,128)(2,1)S(1)}, f32[1,256]{1,0:T(1,128)S(1)}) custom-call(s32[1]{0:T(128)} %bitcast.3.own_ref, bf16[256,512]{1,0:T(8,128)(2,1)S(1)} %shard_map.76.half_ref, bf16[256,512]{1,0:T(8,128)(2,1)S(1)} %collective-permute-done.1.other_ref), custom_call_target="tpu_custom_call" | custom-call | flops 134217728 | bytes 1048576 | tf_op jit(solution)/shard_map/pallas_call | solution.py:51
  64.1 0.0 all-to-all-done.1.part_ref
  64.1 0.4 shard_map.78
  64.5 12.3 %all_to_all.20.part_ref = f32[8,40,256]{2,1,0:T(8,128)S(1)} all-to-all(f32[8,40,256]{2,1,0:T(8,128)S(1)} %shard_map.78), channel_id=1, replica_groups=mesh['ex'=64,'feat'=8] {'feat'}, dimensions={0} | all-to-all | bytes 655360 | tf_op jit(solution)/shard_map/all_to_all | solution.py:345
  76.8 0.7 shard_map.79
  (1 shorter events, 0.0 us)
Async XLA Ops:
  0.0 9.1 %copy-start.1 = (bf16[4,1024]{1,0:T(4,128)(2,1)S(1)}, bf16[4,1024]{1,0:T(4,128)(2,1)}, u32[]{:S(2)}) copy-start(bf16[4,1024]{1,0:T(4,128)(2,1)} %param.13) | copy-start | bytes 24580
  2.4 13.5 %all-to-all-start = ((bf16[8,32,768]{2,1,0:T(8,128)(2,1)}), bf16[8,32,768]{2,1,0:T(8,128)(2,1)S(1)}, u32[]{:S(2)}, u32[]{:S(2)}) async-start(bf16[8,32,768]{2,1,0:T(8,128)(2,1)} %shard_map.73), calls=%async_computation | async-start | bytes 786432 | tf_op jit(solution)/shard_map/all_to_all | solution.py:303
  16.6 16.2 %copy-start = (s32[32]{0:T(128)S(1)}, s32[32]{0:T(128)}, u32[]{:S(2)}) copy-start(s32[32]{0:T(128)} %seq_ref.1) | copy-start | bytes 388
  16.6 21.0 %all-to-all-start.2 = ((bf16[16,8,512]{2,1,0:T(8,128)(2,1)}), bf16[16,8,512]{2,1,0:T(8,128)(2,1)S(1)}, u32[]{:S(2)}, u32[]{:S(2)}) async-start(bf16[16,8,512]{2,1,0:T(8,128)(2,1)} %broadcast_in_dim.12), calls=%async_computation.2 | async-start | bytes 262144 | tf_op jit(solution)/shard_map/all_to_all | solution.py:269
  37.6 26.5 %all-to-all-start.1 = ((bf16[8,256,128]{2,1,0:T(8,128)(2,1)}), bf16[8,256,128]{2,1,0:T(8,128)(2,1)S(1)}, u32[]{:S(2)}, u32[]{:S(2)}) async-start(bf16[8,256,128]{2,1,0:T(8,128)(2,1)} %shard_map.75), calls=%async_computation.1 | async-start | bytes 1048576 | tf_op jit(solution)/shard_map/all_to_all | solution.py:336
  41.1 12.2 %collective-permute-start = (bf16[128,512]{1,0:T(8,128)(2,1)S(1)}, bf16[128,512]{1,0:T(8,128)(2,1)S(1)}, u32[]{:S(2)}, u32[]{:S(2)}) collective-permute-start(bf16[128,512]{1,0:T(8,128)(2,1)S(1)} %bitcast.6), channel_id=1, source_target_pairs={{0,32},{8,40},{16,48},{24,56},{32,0},{40,8},{48,16},{56,24},{64,96... | collective-permute-start | bytes 393224 | tf_op jit(solution)/shard_map/ppermute | solution.py:271
  53.4 9.9 %collective-permute-start.1 = (bf16[256,512]{1,0:T(8,128)(2,1)S(1)}, bf16[256,512]{1,0:T(8,128)(2,1)S(1)}, u32[]{:S(2)}, u32[]{:S(2)}) collective-permute-start(bf16[256,512]{1,0:T(8,128)(2,1)S(1)} %shard_map.76.half_ref), channel_id=1, source_target_pairs={{0,8},{8,0},{16,24},{24,16},{32,40},{40,32},{48,56},{56,48},{64,72... | collective-permute-start | bytes 786440 | tf_op jit(solution)/shard_map/ppermute | solution.py:279

commit v10 on v9

--- a/solution.py
+++ b/solution.py
@@ -11,8 +11,8 @@
 F32 = jnp.float32
 BF16 = jnp.bfloat16
 VMEM_LIMIT = 24 << 20
-LEFT_STEP = 192
-LOW_KEPT = 576
+LEFT_STEP = 96
+LOW_KEPT = 672
 GROUP = 4
 NT = (((1,), (1,)), ((), ()))
 NN = (((1,), (0,)), ((), ()))
@@ -116,7 +116,7 @@
         store.wait()
 
 
-def project_kernel(seq_ref, rr_ref, high_ref, kept_ref, low_hbm, out_ref, low_ref, sems):
+def project_kernel(seq_ref, rr_ref, high_ref, kept_ref, low_hbm, out_hbm, out_ref, low_ref, sems, out_sems):
     peers, two_proj, tokens = rr_ref.shape
     layers, _, kl = high_ref.shape
     proj = two_proj // layers
@@ -127,7 +127,7 @@
     span = GROUP * seq
     width = 2 * 128
     kept = kept_ref.shape[1]
-    chunk = 2 * span
+    chunk = span
     loads = []
     for t in range(0, tokens - kept, chunk):
         rows = pl.ds(t, chunk)
@@ -142,6 +142,7 @@
     second = total[proj:]
     lane = lax.broadcasted_iota(jnp.int32, (proj, width), 1)
     out_lane = lax.broadcasted_iota(jnp.int32, (GROUP * half, 128), 1)
+    stores = []
     for g in range(examples // GROUP):
         x0 = first if g == 0 else pltpu.roll(first, (tokens - g * span) % tokens, 1)
         x1 = pltpu.roll(second, (tokens + span - g * span) % tokens, 1)
@@ -181,6 +182,11 @@
             both_k = jnp.where(out_lane < 64, e, o)
             r = g * GROUP * half
             out_ref[p, r:r + GROUP * half, :] = both_k.astype(BF16)
+        rows = pl.ds(g * GROUP * half, GROUP * half)
+        stores.append(pltpu.make_async_copy(out_ref.at[:, rows], out_hbm.at[:, rows], out_sems.at[g]))
+        stores[-1].start()
+    for store in stores:
+        store.wait()
 
 
 def join_kernel(near_ref, far_ref, out_ref):
@@ -320,18 +326,22 @@
         hbm=(0, 1),
         hbm_out=(2,),
     )
-    parts = call(
+    parts_shape = (peers, examples * 8, 128)
+    (parts,) = call(
         project_kernel,
-        pltpu.VMEM((peers, examples * 8, 128), BF16),
+        (pltpu.HBM(parts_shape, BF16),),
         2 * layers * tokens * kl * 256,
         layers * tokens * kl * 4,
         scratch=(
+            pltpu.VMEM(parts_shape, BF16),
             pltpu.VMEM(low_shape, BF16),
-            pltpu.SemaphoreType.DMA((layers * examples // (2 * GROUP),)),
+            pltpu.SemaphoreType.DMA((layers * examples // GROUP,)),
+            pltpu.SemaphoreType.DMA((examples // GROUP,)),
         ),
         smem=1,
         args=(seq_lengths, on_chip(right_parts), on_chip(left_high), on_chip(left_kept), off_chip(left_low)),
         hbm=(4,),
+        hbm_out=(0,),
     )
     parts = lax.all_to_all(parts, "feat", 0, 0, tiled=True)
     products = call(

time: 78 us -> 77.4 us (level)
  Pallas kernels: 12.1 us -> 14.3 us
  starting transfers between devices: 38.5 us -> 36.7 us
  waiting for transfers between devices: 13.4 us -> 12.5 us
    pallas_call x7, Pallas kernels: 12.1 us -> 14.3 us  [call(): pl.pallas_call(kernel, out_shape=out_shape, in_specs=specs, out_specs=out...]
    ppermute x1, starting transfers between devices: 8.77 us -> 6.92 us  [scores_of(): other = lax.ppermute(half, 'ex', [(i, i ^ 1) for i in range(groups)])]
    all_to_all x1, waiting for transfers between devices: 1.53 us -> 0.01 us  [scores_of(): lax.all_to_all(own_valid, 'ex', 0, 0, tiled=True, axis_index_groups=members)]
  transfers between devices with their start and end apart: 5 -> 5, of which waited for: 4 -> 3; matrix products, arithmetic and copies ran while one was open for 0% -> 0% of each run, Pallas kernels for 11% -> 14%
where the time goes in v10:
time: 77.4 us; the launch traced here: 76.8 us
  starting transfers between devices  36.7 us (47%)
  Pallas kernels  14.3 us (18%)
  waiting for transfers between devices  12.5 us (16%)
  blocking collectives  12.2 us (16%)
  local copies, waits for them, and re-layouts  1.06 us (1%)
    pallas_call x7, Pallas kernels, call(): pl.pallas_call(kernel, out_shape=out_shape, in_specs=specs, out_specs=out...  14.3 us
    all_to_all x1, blocking collectives, scores_of(): products = lax.all_to_all(products, 'feat', 0, 0, tiled=True)  12.2 us
    all_to_all x1, starting transfers between devices, scores_of(): lax.all_to_all(own_valid, 'ex', 0, 0, tiled=True, axis_index_groups=members)  11.7 us
    ppermute x1, starting transfers between devices, scores_of(): far = lax.ppermute(near, 'ex', [(i, i ^ 4) for i in range(groups)])  7.94 us
    ppermute x1, starting transfers between devices, scores_of(): other = lax.ppermute(half, 'ex', [(i, i ^ 1) for i in range(groups)])  6.92 us
    all_to_all x1, starting transfers between devices, scores_of(): right_parts = lax.all_to_all(right_parts, 'feat', 0, 0, tiled=True)  6.66 us
    all_to_all x1, waiting for transfers between devices, scores_of(): right_parts = lax.all_to_all(right_parts, 'feat', 0, 0, tiled=True)  6.44 us
    ppermute x1, waiting for transfers between devices, scores_of(): far = lax.ppermute(near, 'ex', [(i, i ^ 4) for i in range(groups)])  4.91 us
  transfers between devices with their start and end apart: 5, of which 3 were waited for; matrix products, arithmetic and copies ran while one was open for 0% of the time, Pallas kernels for 14%

profile of v10, /device:TPU:1, one launch (start us, length us, event | category | flops | bytes accessed | tf_op | source)
XLA Modules:
  0.0 76.8 jit_solution(11230332798584235505)
XLA Ops:
  0.0 0.0 copy-start.1
  0.0 2.4 %shard_map.73 = bf16[8,32,768]{2,1,0:T(8,128)(2,1)} custom-call(bf16[2,768,256]{2,1,0:T(8,128)(2,1)} %bitcast.8, bf16[2,128,256]{2,1,0:T(8,128)(2,1)} %a_hbm.1, bf16[2,16,128]{2,1,0:T(8,128)(2,1)} %bitcast.10), custom_call_target="tpu_custom_call" | custom-call | flops 201326592 | bytes 786432 | tf_op jit(solution)/shard_map/pallas_call | solution.py:51
  2.4 6.7 %all-to-all-start = ((bf16[8,32,768]{2,1,0:T(8,128)(2,1)}), bf16[8,32,768]{2,1,0:T(8,128)(2,1)S(1)}, u32[]{:S(2)}, u32[]{:S(2)}) async-start(bf16[8,32,768]{2,1,0:T(8,128)(2,1)} %shard_map.73), calls=%async_computation | async-start | bytes 786432 | tf_op jit(solution)/shard_map/all_to_all | solution.py:309
  9.1 0.0 copy-done.1
  9.1 0.2 reshape.16
  9.3 0.1 copy.8
  9.4 0.1 broadcast_in_dim.11
  9.5 6.4 %all-to-all-done.rr_ref = bf16[8,32,768]{2,1,0:T(8,128)(2,1)S(1)} async-done(((bf16[8,32,768]{2,1,0:T(8,128)(2,1)}), bf16[8,32,768]{2,1,0:T(8,128)(2,1)S(1)}, u32[]{:S(2)}, u32[]{:S(2)}) %all-to-all-start) | async-done | bytes 393248 | tf_op jit(solution)/shard_map/all_to_all | solution.py:309
  15.9 0.7 broadcast_in_dim.12
  16.6 0.0 copy-start
  16.6 11.7 %all-to-all-start.2 = ((bf16[16,8,512]{2,1,0:T(8,128)(2,1)}), bf16[16,8,512]{2,1,0:T(8,128)(2,1)S(1)}, u32[]{:S(2)}, u32[]{:S(2)}) async-start(bf16[16,8,512]{2,1,0:T(8,128)(2,1)} %broadcast_in_dim.12), calls=%async_computation.2 | async-start | bytes 262144 | tf_op jit(solution)/shard_map/all_to_all | solution.py:275
  28.2 6.7 %shard_map.74 = (bf16[2,768,512]{2,1,0:T(8,128)(2,1)S(1)}, bf16[2,672,512]{2,1,0:T(8,128)(2,1)S(1)}, bf16[2,96,512]{2,1,0:T(8,128)(2,1)}) custom-call(bf16[2,768,512]{2,1,0:T(8,128)(2,1)} %bitcast.11, bf16[2,512,512]{2,1,0:T(8,128)(2,1)} %l_hbm.1), custom_call_target="tpu_custom_call" | custom-call | flops 805306368 | bytes 5767168 | tf_op jit(solution)/shard_map/pallas_call | solution.py:51
  35.0 0.0 copy-done
  35.0 3.2 %shard_map.75 = bf16[8,256,128]{2,1,0:T(8,128)(2,1)} custom-call(s32[32]{0:T(128)S(1)} %copy-done, bf16[8,32,768]{2,1,0:T(8,128)(2,1)S(1)} %all-to-all-done.rr_ref, bf16[2,768,512]{2,1,0:T(8,128)(2,1)S(1)} %get-tuple-element.10.high_ref, bf16[2,672,512]{2,1,0:T(8,128)(2,1)S(1)} %get-tuple-element.11.kept_ref, bf16[2,96,512]{2,1,0:T(8,128)(2,1)} %get-tuple-element.12.low_hbm), custom_call_target="tpu_custom_call" | custom-call | flops 402653184 | bytes 3145728 | tf_op jit(solution)/shard_map/pallas_call | solution.py:51
  38.2 0.0 all-to-all-done.2
  38.2 3.5 %all-to-all-start.1 = ((bf16[8,256,128]{2,1,0:T(8,128)(2,1)}), bf16[8,256,128]{2,1,0:T(8,128)(2,1)S(1)}, u32[]{:S(2)}, u32[]{:S(2)}) async-start(bf16[8,256,128]{2,1,0:T(8,128)(2,1)} %shard_map.75), calls=%async_computation.1 | async-start | bytes 1048576 | tf_op jit(solution)/shard_map/all_to_all | solution.py:346
  41.7 7.9 %collective-permute-start = (bf16[128,512]{1,0:T(8,128)(2,1)S(1)}, bf16[128,512]{1,0:T(8,128)(2,1)S(1)}, u32[]{:S(2)}, u32[]{:S(2)}) collective-permute-start(bf16[128,512]{1,0:T(8,128)(2,1)S(1)} %bitcast.6), channel_id=1, source_target_pairs={{0,32},{8,40},{16,48},{24,56},{32,0},{40,8},{48,16},{56,24},{64,96... | collective-permute-start | bytes 393224 | tf_op jit(solution)/shard_map/ppermute | solution.py:277
  49.7 4.9 %collective-permute-done.far_ref = bf16[128,512]{1,0:T(8,128)(2,1)S(1)} collective-permute-done((bf16[128,512]{1,0:T(8,128)(2,1)S(1)}, bf16[128,512]{1,0:T(8,128)(2,1)S(1)}, u32[]{:S(2)}, u32[]{:S(2)}) %collective-permute-start) | collective-permute-done | bytes 131104 | tf_op jit(solution)/shard_map/ppermute | solution.py:277
  54.6 6.9 %collective-permute-start.1 = (bf16[256,512]{1,0:T(8,128)(2,1)S(1)}, bf16[256,512]{1,0:T(8,128)(2,1)S(1)}, u32[]{:S(2)}, u32[]{:S(2)}) collective-permute-start(bf16[256,512]{1,0:T(8,128)(2,1)S(1)} %shard_map.76.half_ref), channel_id=1, source_target_pairs={{0,8},{8,0},{16,24},{24,16},{32,40},{40,32},{48,56},{56,48},{64,72... | collective-permute-start | bytes 786440 | tf_op jit(solution)/shard_map/ppermute | solution.py:285
  61.6 1.1 %collective-permute-done.1.other_ref = bf16[256,512]{1,0:T(8,128)(2,1)S(1)} collective-permute-done((bf16[256,512]{1,0:T(8,128)(2,1)S(1)}, bf16[256,512]{1,0:T(8,128)(2,1)S(1)}, u32[]{:S(2)}, u32[]{:S(2)}) %collective-permute-start.1) | collective-permute-done | bytes 262176 | tf_op jit(solution)/shard_map/ppermute | solution.py:285
  62.7 0.8 %shard_map.77 = (bf16[256,1024]{1,0:T(8,128)(2,1)S(1)}, f32[1,256]{1,0:T(1,128)S(1)}) custom-call(s32[1]{0:T(128)} %bitcast.3.own_ref, bf16[256,512]{1,0:T(8,128)(2,1)S(1)} %shard_map.76.half_ref, bf16[256,512]{1,0:T(8,128)(2,1)S(1)} %collective-permute-done.1.other_ref), custom_call_target="tpu_custom_call" | custom-call | flops 134217728 | bytes 1048576 | tf_op jit(solution)/shard_map/pallas_call | solution.py:51
  63.5 0.0 all-to-all-done.1.part_ref
  63.5 0.4 shard_map.78
  63.9 12.2 %all_to_all.20.part_ref = f32[8,40,256]{2,1,0:T(8,128)S(1)} all-to-all(f32[8,40,256]{2,1,0:T(8,128)S(1)} %shard_map.78), channel_id=1, replica_groups=mesh['ex'=64,'feat'=8] {'feat'}, dimensions={0} | all-to-all | bytes 655360 | tf_op jit(solution)/shard_map/all_to_all | solution.py:355
  76.0 0.7 shard_map.79
  (1 shorter events, 0.0 us)
Async XLA Ops:
  0.0 9.1 %copy-start.1 = (bf16[4,1024]{1,0:T(4,128)(2,1)S(1)}, bf16[4,1024]{1,0:T(4,128)(2,1)}, u32[]{:S(2)}) copy-start(bf16[4,1024]{1,0:T(4,128)(2,1)} %param.13) | copy-start | bytes 24580
  2.4 13.5 %all-to-all-start = ((bf16[8,32,768]{2,1,0:T(8,128)(2,1)}), bf16[8,32,768]{2,1,0:T(8,128)(2,1)S(1)}, u32[]{:S(2)}, u32[]{:S(2)}) async-start(bf16[8,32,768]{2,1,0:T(8,128)(2,1)} %shard_map.73), calls=%async_computation | async-start | bytes 786432 | tf_op jit(solution)/shard_map/all_to_all | solution.py:309
  16.6 18.4 %copy-start = (s32[32]{0:T(128)S(1)}, s32[32]{0:T(128)}, u32[]{:S(2)}) copy-start(s32[32]{0:T(128)} %seq_ref.1) | copy-start | bytes 388
  16.6 21.6 %all-to-all-start.2 = ((bf16[16,8,512]{2,1,0:T(8,128)(2,1)}), bf16[16,8,512]{2,1,0:T(8,128)(2,1)S(1)}, u32[]{:S(2)}, u32[]{:S(2)}) async-start(bf16[16,8,512]{2,1,0:T(8,128)(2,1)} %broadcast_in_dim.12), calls=%async_computation.2 | async-start | bytes 262144 | tf_op jit(solution)/shard_map/all_to_all | solution.py:275
  38.2 25.3 %all-to-all-start.1 = ((bf16[8,256,128]{2,1,0:T(8,128)(2,1)}), bf16[8,256,128]{2,1,0:T(8,128)(2,1)S(1)}, u32[]{:S(2)}, u32[]{:S(2)}) async-start(bf16[8,256,128]{2,1,0:T(8,128)(2,1)} %shard_map.75), calls=%async_computation.1 | async-start | bytes 1048576 | tf_op jit(solution)/shard_map/all_to_all | solution.py:346
  41.7 12.9 %collective-permute-start = (bf16[128,512]{1,0:T(8,128)(2,1)S(1)}, bf16[128,512]{1,0:T(8,128)(2,1)S(1)}, u32[]{:S(2)}, u32[]{:S(2)}) collective-permute-start(bf16[128,512]{1,0:T(8,128)(2,1)S(1)} %bitcast.6), channel_id=1, source_target_pairs={{0,32},{8,40},{16,48},{24,56},{32,0},{40,8},{48,16},{56,24},{64,96... | collective-permute-start | bytes 393224 | tf_op jit(solution)/shard_map/ppermute | solution.py:277
  54.6 8.1 %collective-permute-start.1 = (bf16[256,512]{1,0:T(8,128)(2,1)S(1)}, bf16[256,512]{1,0:T(8,128)(2,1)S(1)}, u32[]{:S(2)}, u32[]{:S(2)}) collective-permute-start(bf16[256,512]{1,0:T(8,128)(2,1)S(1)} %shard_map.76.half_ref), channel_id=1, source_target_pairs={{0,8},{8,0},{16,24},{24,16},{32,40},{40,32},{48,56},{56,48},{64,72... | collective-permute-start | bytes 786440 | tf_op jit(solution)/shard_map/ppermute | solution.py:285

commit v11 on v7

--- a/solution.py
+++ b/solution.py
@@ -12,6 +12,7 @@
 BF16 = jnp.bfloat16
 VMEM_LIMIT = 24 << 20
 LEFT_STEP = 256
+LOW_ROWS = 672
 GROUP = 4
 NT = (((1,), (1,)), ((), ()))
 NN = (((1,), (0,)), ((), ()))
@@ -38,16 +39,20 @@
     return tuple(pltpu.VMEM(x.shape, x.dtype) for x in arrays)
 
 
-def call(kernel, out_shape, flops, bytes_accessed, scratch=(), smem=0, args=(), hbm=False):
+def call(kernel, out_shape, flops, bytes_accessed, scratch=(), smem=0, args=(), hbm=(), hbm_out=()):
     specs = [pl.BlockSpec(memory_space=pltpu.SMEM)] * smem
-    specs += [pl.BlockSpec(memory_space=pltpu.HBM if hbm else pltpu.VMEM)] * (len(args) - smem)
+    specs += [pl.BlockSpec(memory_space=pltpu.HBM if n in hbm else pltpu.VMEM) for n in range(smem, len(args))]
+    if isinstance(out_shape, tuple):
+        out_specs = tuple(
+            pl.BlockSpec(memory_space=pltpu.HBM if n in hbm_out else pltpu.VMEM) for n in range(len(out_shape))
+        )
+    else:
+        out_specs = pl.BlockSpec(memory_space=pltpu.VMEM)
     return pl.pallas_call(
         kernel,
         out_shape=out_shape,
         in_specs=specs,
-        out_specs=jax.tree.map(
-            lambda _: pl.BlockSpec(memory_space=pltpu.VMEM), out_shape, is_leaf=lambda x: hasattr(x, "shape")
-        ),
+        out_specs=out_specs,
         scratch_shapes=list(scratch),
         cost_estimate=pl.CostEstimate(flops=flops, bytes_accessed=bytes_accessed, transcendentals=0),
         compiler_params=pltpu.CompilerParams(vmem_limit_bytes=VMEM_LIMIT),
@@ -97,10 +102,12 @@
         copy.wait()
         high, low = split(dot(c_ref[l, t:t + step, :], l_ref[l], NT))
         high_ref[l, t:t + step, :] = high
-        low_ref[l, t:t + step, :] = low
-
-
-def project_kernel(seq_ref, rr_ref, high_ref, low_ref, out_ref):
+        stop = min(t + step, low_ref.shape[1])
+        if t < stop:
+            low_ref[l, t:stop, :] = low[:stop - t]
+
+
+def project_kernel(seq_ref, rr_ref, high_ref, low_ref, out_hbm, out_ref, out_sems):
     peers, two_proj, tokens = rr_ref.shape
     layers, _, kl = high_ref.shape
     proj = two_proj // layers
@@ -117,6 +124,7 @@
     second = total[proj:]
     lane = lax.broadcasted_iota(jnp.int32, (proj, width), 1)
     out_lane = lax.broadcasted_iota(jnp.int32, (GROUP * half, 128), 1)
+    stores = []
     for g in range(examples // GROUP):
         x0 = first if g == 0 else pltpu.roll(first, (tokens - g * span) % tokens, 1)
         x1 = pltpu.roll(second, (tokens + span - g * span) % tokens, 1)
@@ -134,10 +142,12 @@
         high = high[:, :layers * span]
         t = g * span
         left_high = jnp.concatenate([high_ref[l, t:t + span, :] for l in range(layers)], axis=0)
-        left_low = jnp.concatenate([low_ref[l, t:t + span, :] for l in range(layers)], axis=0)
         rows = GROUP * proj
         part = dot(both, left_high, NN)
-        part = part[:rows] + part[rows:] + dot(high, left_low, NN)
+        part = part[:rows] + part[rows:]
+        if t < low_ref.shape[1]:
+            left_low = jnp.concatenate([low_ref[l, t:t + span, :] for l in range(layers)], axis=0)
+            part = part + dot(high, left_low, NN)
         part = part.reshape(GROUP, 2, half, kl)
         even = part[:, 0].reshape(GROUP * half, kl)
         odd = part[:, 1].reshape(GROUP * half, kl)
@@ -152,6 +162,11 @@
             both_k = jnp.where(out_lane < 64, e, o)
             r = g * GROUP * half
             out_ref[p, r:r + GROUP * half, :] = both_k.astype(BF16)
+        rows = pl.ds(g * GROUP * half, GROUP * half)
+        stores.append(pltpu.make_async_copy(out_ref.at[:, rows], out_hbm.at[:, rows], out_sems.at[g]))
+        stores[-1].start()
+    for store in stores:
+        store.wait()
 
 
 def join_kernel(near_ref, far_ref, out_ref):
@@ -269,26 +284,33 @@
         proj_inputs.size * 2,
         scratch=(*staged(right_in), pltpu.SemaphoreType.DMA((2 + layers,))),
         args=tuple(off_chip(x) for x in right_in),
-        hbm=True,
+        hbm=(0, 1, 2),
     )
     right_parts = lax.all_to_all(right_parts, "feat", 0, 0, tiled=True)
 
-    left_shape = pltpu.VMEM((layers, tokens, kl), BF16)
+    left_shape = (layers, tokens, kl)
+    left_copies = layers * tokens // LEFT_STEP
     left_in = (out_cotangent.reshape(layers, tokens, width), left_factor)
     left_high, left_low = call(
         left_kernel,
-        (left_shape, left_shape),
+        (
+            pltpu.VMEM(left_shape, BF16),
+            pltpu.VMEM((layers, LOW_ROWS, kl), BF16),
+        ),
         2 * layers * tokens * width * kl,
         (out_cotangent.size + left_factor.size) * 2 + layers * tokens * kl * 4,
-        scratch=(*staged(left_in), pltpu.SemaphoreType.DMA((layers + layers * tokens // LEFT_STEP,))),
+        scratch=(*staged(left_in), pltpu.SemaphoreType.DMA((layers + left_copies,))),
         args=tuple(off_chip(x) for x in left_in),
-        hbm=True,
-    )
-    parts = call(
+        hbm=(0, 1),
+    )
+    parts_shape = (peers, examples * 8, 128)
+    (parts,) = call(
         project_kernel,
-        pltpu.VMEM((peers, examples * 8, 128), BF16),
+        (pltpu.HBM(parts_shape, BF16),),
         2 * layers * tokens * kl * 256,
         layers * tokens * kl * 4,
+        scratch=(pltpu.VMEM(parts_shape, BF16), pltpu.SemaphoreType.DMA((examples // GROUP,))),
+        hbm_out=(0,),
         smem=1,
         args=(seq_lengths, on_chip(right_parts), on_chip(left_high), on_chip(left_low)),
     )

time: 77.9 us -> 77.9 us (level)
  no operation moved by 1% of the time
where the time goes in v11:
time: 77.9 us; the launch traced here: 77.5 us
  starting transfers between devices  38.5 us (49%)
  waiting for transfers between devices  15.9 us (20%)
  blocking collectives  12.3 us (16%)
  Pallas kernels  9.61 us (12%)
  local copies, waits for them, and re-layouts  1.04 us (1%)
    all_to_all x1, blocking collectives, scores_of(): products = lax.all_to_all(products, 'feat', 0, 0, tiled=True)  12.3 us
    all_to_all x1, starting transfers between devices, scores_of(): lax.all_to_all(own_valid, 'ex', 0, 0, tiled=True, axis_index_groups=members)  11.7 us
    pallas_call x7, Pallas kernels, call(): pl.pallas_call(kernel, out_shape=out_shape, in_specs=specs, out_specs=out...  9.61 us
    ppermute x1, starting transfers between devices, scores_of(): other = lax.ppermute(half, 'ex', [(i, i ^ 1) for i in range(groups)])  8.77 us
    ppermute x1, starting transfers between devices, scores_of(): far = lax.ppermute(near, 'ex', [(i, i ^ 4) for i in range(groups)])  7.94 us
    all_to_all x1, starting transfers between devices, scores_of(): right_parts = lax.all_to_all(right_parts, 'feat', 0, 0, tiled=True)  6.66 us
    all_to_all x1, waiting for transfers between devices, scores_of(): right_parts = lax.all_to_all(right_parts, 'feat', 0, 0, tiled=True)  6.44 us
    ppermute x1, waiting for transfers between devices, scores_of(): far = lax.ppermute(near, 'ex', [(i, i ^ 4) for i in range(groups)])  4.29 us
  transfers between devices with their start and end apart: 5, of which 4 were waited for; matrix products, arithmetic and copies ran while one was open for 0% of the time, Pallas kernels for 8%

profile of v11, /device:TPU:1, one launch (start us, length us, event | category | flops | bytes accessed | tf_op | source)
XLA Modules:
  0.0 77.5 jit_solution(1119877600338088773)
XLA Ops:
  0.0 0.0 copy-start.1
  0.0 2.4 %shard_map.73 = bf16[8,32,768]{2,1,0:T(8,128)(2,1)} custom-call(bf16[2,768,256]{2,1,0:T(8,128)(2,1)} %bitcast.8, bf16[2,128,256]{2,1,0:T(8,128)(2,1)} %a_hbm.1, bf16[2,16,128]{2,1,0:T(8,128)(2,1)} %bitcast.10), custom_call_target="tpu_custom_call" | custom-call | flops 201326592 | bytes 786432 | tf_op jit(solution)/shard_map/pallas_call | solution.py:51
  2.4 6.7 %all-to-all-start = ((bf16[8,32,768]{2,1,0:T(8,128)(2,1)}), bf16[8,32,768]{2,1,0:T(8,128)(2,1)S(1)}, u32[]{:S(2)}, u32[]{:S(2)}) async-start(bf16[8,32,768]{2,1,0:T(8,128)(2,1)} %shard_map.73), calls=%async_computation | async-start | bytes 786432 | tf_op jit(solution)/shard_map/all_to_all | solution.py:289
  9.1 0.0 copy-done.1
  9.1 0.2 reshape.16
  9.3 0.1 copy.8
  9.4 0.1 broadcast_in_dim.11
  9.5 6.4 %all-to-all-done.rr_ref = bf16[8,32,768]{2,1,0:T(8,128)(2,1)S(1)} async-done(((bf16[8,32,768]{2,1,0:T(8,128)(2,1)}), bf16[8,32,768]{2,1,0:T(8,128)(2,1)S(1)}, u32[]{:S(2)}, u32[]{:S(2)}) %all-to-all-start) | async-done | bytes 393248 | tf_op jit(solution)/shard_map/all_to_all | solution.py:289
  15.9 0.7 broadcast_in_dim.12
  16.6 0.0 copy-start
  16.6 11.7 %all-to-all-start.2 = ((bf16[16,8,512]{2,1,0:T(8,128)(2,1)}), bf16[16,8,512]{2,1,0:T(8,128)(2,1)S(1)}, u32[]{:S(2)}, u32[]{:S(2)}) async-start(bf16[16,8,512]{2,1,0:T(8,128)(2,1)} %broadcast_in_dim.12), calls=%async_computation.2 | async-start | bytes 262144 | tf_op jit(solution)/shard_map/all_to_all | solution.py:255
  28.2 3.2 %shard_map.74 = (bf16[2,768,512]{2,1,0:T(8,128)(2,1)S(1)}, bf16[2,672,512]{2,1,0:T(8,128)(2,1)S(1)}) custom-call(bf16[2,768,512]{2,1,0:T(8,128)(2,1)} %bitcast.11, bf16[2,512,512]{2,1,0:T(8,128)(2,1)} %l_hbm.1), custom_call_target="tpu_custom_call" | custom-call | flops 805306368 | bytes 5767168 | tf_op jit(solution)/shard_map/pallas_call | solution.py:51
  31.4 0.0 copy-done
  31.4 2.1 %shard_map.75 = bf16[8,256,128]{2,1,0:T(8,128)(2,1)} custom-call(s32[32]{0:T(128)S(1)} %copy-done, bf16[8,32,768]{2,1,0:T(8,128)(2,1)S(1)} %all-to-all-done.rr_ref, bf16[2,768,512]{2,1,0:T(8,128)(2,1)S(1)} %get-tuple-element.9.high_ref, bf16[2,672,512]{2,1,0:T(8,128)(2,1)S(1)} %get-tuple-element.10.low_ref), custom_call_target="tpu_custom_call" | custom-call | flops 402653184 | bytes 3145728 | tf_op jit(solution)/shard_map/pallas_call | solution.py:51
  33.6 4.0 %all-to-all-done.2 = bf16[16,8,512]{2,1,0:T(8,128)(2,1)S(1)} async-done(((bf16[16,8,512]{2,1,0:T(8,128)(2,1)}), bf16[16,8,512]{2,1,0:T(8,128)(2,1)S(1)}, u32[]{:S(2)}, u32[]{:S(2)}) %all-to-all-start.2) | async-done | bytes 131104 | tf_op jit(solution)/shard_map/all_to_all | solution.py:255
  37.6 3.5 %all-to-all-start.1 = ((bf16[8,256,128]{2,1,0:T(8,128)(2,1)}), bf16[8,256,128]{2,1,0:T(8,128)(2,1)S(1)}, u32[]{:S(2)}, u32[]{:S(2)}) async-start(bf16[8,256,128]{2,1,0:T(8,128)(2,1)} %shard_map.75), calls=%async_computation.1 | async-start | bytes 1048576 | tf_op jit(solution)/shard_map/all_to_all | solution.py:317
  41.1 7.9 %collective-permute-start = (bf16[128,512]{1,0:T(8,128)(2,1)S(1)}, bf16[128,512]{1,0:T(8,128)(2,1)S(1)}, u32[]{:S(2)}, u32[]{:S(2)}) collective-permute-start(bf16[128,512]{1,0:T(8,128)(2,1)S(1)} %bitcast.6), channel_id=1, source_target_pairs={{0,32},{8,40},{16,48},{24,56},{32,0},{40,8},{48,16},{56,24},{64,96... | collective-permute-start | bytes 393224 | tf_op jit(solution)/shard_map/ppermute | solution.py:257
  49.1 4.3 %collective-permute-done.far_ref = bf16[128,512]{1,0:T(8,128)(2,1)S(1)} collective-permute-done((bf16[128,512]{1,0:T(8,128)(2,1)S(1)}, bf16[128,512]{1,0:T(8,128)(2,1)S(1)}, u32[]{:S(2)}, u32[]{:S(2)}) %collective-permute-start) | collective-permute-done | bytes 131104 | tf_op jit(solution)/shard_map/ppermute | solution.py:257
  53.4 8.8 %collective-permute-start.1 = (bf16[256,512]{1,0:T(8,128)(2,1)S(1)}, bf16[256,512]{1,0:T(8,128)(2,1)S(1)}, u32[]{:S(2)}, u32[]{:S(2)}) collective-permute-start(bf16[256,512]{1,0:T(8,128)(2,1)S(1)} %shard_map.76.half_ref), channel_id=1, source_target_pairs={{0,8},{8,0},{16,24},{24,16},{32,40},{40,32},{48,56},{56,48},{64,72... | collective-permute-start | bytes 786440 | tf_op jit(solution)/shard_map/ppermute | solution.py:265
  62.2 1.1 %collective-permute-done.1.other_ref = bf16[256,512]{1,0:T(8,128)(2,1)S(1)} collective-permute-done((bf16[256,512]{1,0:T(8,128)(2,1)S(1)}, bf16[256,512]{1,0:T(8,128)(2,1)S(1)}, u32[]{:S(2)}, u32[]{:S(2)}) %collective-permute-start.1) | collective-permute-done | bytes 262176 | tf_op jit(solution)/shard_map/ppermute | solution.py:265
  63.3 0.8 %shard_map.77 = (bf16[256,1024]{1,0:T(8,128)(2,1)S(1)}, f32[1,256]{1,0:T(1,128)S(1)}) custom-call(s32[1]{0:T(128)} %bitcast.3.own_ref, bf16[256,512]{1,0:T(8,128)(2,1)S(1)} %shard_map.76.half_ref, bf16[256,512]{1,0:T(8,128)(2,1)S(1)} %collective-permute-done.1.other_ref), custom_call_target="tpu_custom_call" | custom-call | flops 134217728 | bytes 1048576 | tf_op jit(solution)/shard_map/pallas_call | solution.py:51
  64.1 0.0 all-to-all-done.1.part_ref
  64.1 0.4 shard_map.78
  64.5 12.3 %all_to_all.20.part_ref = f32[8,40,256]{2,1,0:T(8,128)S(1)} all-to-all(f32[8,40,256]{2,1,0:T(8,128)S(1)} %shard_map.78), channel_id=1, replica_groups=mesh['ex'=64,'feat'=8] {'feat'}, dimensions={0} | all-to-all | bytes 655360 | tf_op jit(solution)/shard_map/all_to_all | solution.py:326
  76.8 0.7 shard_map.79
  (1 shorter events, 0.0 us)
Async XLA Ops:
  0.0 9.1 %copy-start.1 = (bf16[4,1024]{1,0:T(4,128)(2,1)S(1)}, bf16[4,1024]{1,0:T(4,128)(2,1)}, u32[]{:S(2)}) copy-start(bf16[4,1024]{1,0:T(4,128)(2,1)} %param.13) | copy-start | bytes 24580
  2.4 13.5 %all-to-all-start = ((bf16[8,32,768]{2,1,0:T(8,128)(2,1)}), bf16[8,32,768]{2,1,0:T(8,128)(2,1)S(1)}, u32[]{:S(2)}, u32[]{:S(2)}) async-start(bf16[8,32,768]{2,1,0:T(8,128)(2,1)} %shard_map.73), calls=%async_computation | async-start | bytes 786432 | tf_op jit(solution)/shard_map/all_to_all | solution.py:289
  16.6 14.9 %copy-start = (s32[32]{0:T(128)S(1)}, s32[32]{0:T(128)}, u32[]{:S(2)}) copy-start(s32[32]{0:T(128)} %seq_ref.1) | copy-start | bytes 388
  16.6 21.0 %all-to-all-start.2 = ((bf16[16,8,512]{2,1,0:T(8,128)(2,1)}), bf16[16,8,512]{2,1,0:T(8,128)(2,1)S(1)}, u32[]{:S(2)}, u32[]{:S(2)}) async-start(bf16[16,8,512]{2,1,0:T(8,128)(2,1)} %broadcast_in_dim.12), calls=%async_computation.2 | async-start | bytes 262144 | tf_op jit(solution)/shard_map/all_to_all | solution.py:255
  37.6 26.5 %all-to-all-start.1 = ((bf16[8,256,128]{2,1,0:T(8,128)(2,1)}), bf16[8,256,128]{2,1,0:T(8,128)(2,1)S(1)}, u32[]{:S(2)}, u32[]{:S(2)}) async-start(bf16[8,256,128]{2,1,0:T(8,128)(2,1)} %shard_map.75), calls=%async_computation.1 | async-start | bytes 1048576 | tf_op jit(solution)/shard_map/all_to_all | solution.py:317
  41.1 12.2 %collective-permute-start = (bf16[128,512]{1,0:T(8,128)(2,1)S(1)}, bf16[128,512]{1,0:T(8,128)(2,1)S(1)}, u32[]{:S(2)}, u32[]{:S(2)}) collective-permute-start(bf16[128,512]{1,0:T(8,128)(2,1)S(1)} %bitcast.6), channel_id=1, source_target_pairs={{0,32},{8,40},{16,48},{24,56},{32,0},{40,8},{48,16},{56,24},{64,96... | collective-permute-start | bytes 393224 | tf_op jit(solution)/shard_map/ppermute | solution.py:257
  53.4 9.9 %collective-permute-start.1 = (bf16[256,512]{1,0:T(8,128)(2,1)S(1)}, bf16[256,512]{1,0:T(8,128)(2,1)S(1)}, u32[]{:S(2)}, u32[]{:S(2)}) collective-permute-start(bf16[256,512]{1,0:T(8,128)(2,1)S(1)} %shard_map.76.half_ref), channel_id=1, source_target_pairs={{0,8},{8,0},{16,24},{24,16},{32,40},{40,32},{48,56},{56,48},{64,72... | collective-permute-start | bytes 786440 | tf_op jit(solution)/shard_map/ppermute | solution.py:265

commit v12 on v11

--- a/solution.py
+++ b/solution.py
@@ -12,7 +12,6 @@
 BF16 = jnp.bfloat16
 VMEM_LIMIT = 24 << 20
 LEFT_STEP = 256
-LOW_ROWS = 672
 GROUP = 4
 NT = (((1,), (1,)), ((), ()))
 NN = (((1,), (0,)), ((), ()))
@@ -60,7 +59,6 @@
 
 
 def right_kernel(x_hbm, a_hbm, r_hbm, out_ref, x_ref, a_ref, r_ref, sems):
-    peers = out_ref.shape[0]
     layers = x_ref.shape[0]
     proj = r_ref.shape[1]
     small = [
@@ -79,12 +77,16 @@
     for l in range(layers):
         inputs[l].wait()
         rows = dot(mixes[l], x_ref[l], NT)
-        rows = (rows[:proj] + rows[proj:]).astype(BF16)
-        for p in range(peers):
-            out_ref[p, l * proj:(l + 1) * proj, :] = rows
-
-
-def left_kernel(c_hbm, l_hbm, high_ref, low_ref, c_ref, l_ref, sems):
+        out_ref[l * proj:(l + 1) * proj, :] = rows[:proj] + rows[proj:]
+
+
+def pair_kernel(own_ref, other_ref, out_ref):
+    total = own_ref[...] + other_ref[...]
+    for p in range(out_ref.shape[0]):
+        out_ref[p] = total
+
+
+def left_kernel(c_hbm, l_hbm, out_ref, c_ref, l_ref, sems):
     layers, tokens, _ = c_ref.shape
     step = LEFT_STEP
     factors, pieces = [], []
@@ -100,16 +102,13 @@
         if t == 0:
             factors[l].wait()
         copy.wait()
-        high, low = split(dot(c_ref[l, t:t + step, :], l_ref[l], NT))
-        high_ref[l, t:t + step, :] = high
-        stop = min(t + step, low_ref.shape[1])
-        if t < stop:
-            low_ref[l, t:stop, :] = low[:stop - t]
-
-
-def project_kernel(seq_ref, rr_ref, high_ref, low_ref, out_hbm, out_ref, out_sems):
-    peers, two_proj, tokens = rr_ref.shape
-    layers, _, kl = high_ref.shape
+        out_ref[l, t:t + step, :] = dot(c_ref[l, t:t + step, :], l_ref[l], NT).astype(BF16)
+
+
+def project_kernel(seq_ref, rr_ref, left_ref, out_hbm, out_ref, out_sems):
+    parts, two_proj, tokens = rr_ref.shape
+    layers, _, kl = left_ref.shape
+    peers = out_ref.shape[0]
     proj = two_proj // layers
     half = proj // 2
     owned = kl // peers
@@ -117,9 +116,9 @@
     seq = tokens // examples
     span = GROUP * seq
     width = 2 * 128
-    total = rr_ref[0].astype(F32)
-    for p in range(1, peers):
-        total = total + rr_ref[p].astype(F32)
+    total = rr_ref[0]
+    for p in range(1, parts):
+        total = total + rr_ref[p]
     first = total[:proj]
     second = total[proj:]
     lane = lax.broadcasted_iota(jnp.int32, (proj, width), 1)
@@ -136,18 +135,10 @@
             mask0 = (lane >= start) & (lane < stop)
             mask1 = (lane >= start + span) & (lane < stop + span)
             blocks.append(jnp.where(mask0, x0, jnp.where(mask1, x1, 0.0)))
-        spread = jnp.concatenate(blocks, axis=0)
-        high, low = split(spread)
-        both = jnp.concatenate([high, low], axis=0)[:, :layers * span]
-        high = high[:, :layers * span]
+        spread = jnp.concatenate(blocks, axis=0).astype(BF16)[:, :layers * span]
         t = g * span
-        left_high = jnp.concatenate([high_ref[l, t:t + span, :] for l in range(layers)], axis=0)
-        rows = GROUP * proj
-        part = dot(both, left_high, NN)
-        part = part[:rows] + part[rows:]
-        if t < low_ref.shape[1]:
-            left_low = jnp.concatenate([low_ref[l, t:t + span, :] for l in range(layers)], axis=0)
-            part = part + dot(high, left_low, NN)
+        left = jnp.concatenate([left_ref[l, t:t + span, :] for l in range(layers)], axis=0)
+        part = dot(spread, left, NN)
         part = part.reshape(GROUP, 2, half, kl)
         even = part[:, 0].reshape(GROUP * half, kl)
         odd = part[:, 1].reshape(GROUP * half, kl)
@@ -279,26 +270,31 @@
     right_in = (proj_inputs.reshape(layers, tokens, inputs), frozen_adapter, right_factor.swapaxes(1, 2))
     right_parts = call(
         right_kernel,
-        pltpu.VMEM((peers, layers * proj, tokens), BF16),
+        jax.ShapeDtypeStruct((layers * proj, tokens), F32),
         2 * layers * tokens * inputs * 256,
         proj_inputs.size * 2,
         scratch=(*staged(right_in), pltpu.SemaphoreType.DMA((2 + layers,))),
         args=tuple(off_chip(x) for x in right_in),
         hbm=(0, 1, 2),
     )
-    right_parts = lax.all_to_all(right_parts, "feat", 0, 0, tiled=True)
-
+    right_other = lax.ppermute(right_parts, "feat", [(i, i ^ 1) for i in range(peers)])
+    right_parts = call(
+        pair_kernel,
+        jax.ShapeDtypeStruct((peers // 2, layers * proj, tokens), F32),
+        layers * proj * tokens,
+        4 * peers * layers * proj * tokens,
+        args=(right_parts, right_other),
+    )
+    along_x = [[i * 2 + z for i in range(peers // 2)] for z in range(2)]
+    right_parts = lax.all_to_all(right_parts, "feat", 0, 0, tiled=True, axis_index_groups=along_x)
     left_shape = (layers, tokens, kl)
     left_copies = layers * tokens // LEFT_STEP
     left_in = (out_cotangent.reshape(layers, tokens, width), left_factor)
-    left_high, left_low = call(
+    left_rows = call(
         left_kernel,
-        (
-            pltpu.VMEM(left_shape, BF16),
-            pltpu.VMEM((layers, LOW_ROWS, kl), BF16),
-        ),
+        pltpu.VMEM(left_shape, BF16),
         2 * layers * tokens * width * kl,
-        (out_cotangent.size + left_factor.size) * 2 + layers * tokens * kl * 4,
+        (out_cotangent.size + left_factor.size) * 2 + layers * tokens * kl * 2,
         scratch=(*staged(left_in), pltpu.SemaphoreType.DMA((layers + left_copies,))),
         args=tuple(off_chip(x) for x in left_in),
         hbm=(0, 1),
@@ -312,7 +308,7 @@
         scratch=(pltpu.VMEM(parts_shape, BF16), pltpu.SemaphoreType.DMA((examples // GROUP,))),
         hbm_out=(0,),
         smem=1,
-        args=(seq_lengths, on_chip(right_parts), on_chip(left_high), on_chip(left_low)),
+        args=(seq_lengths, on_chip(right_parts), on_chip(left_rows)),
     )
     parts = lax.all_to_all(parts, "feat", 0, 0, tiled=True)
     products = call(

time: 77.9 us -> 80.7 us (1.036)
  starting transfers between devices: 38.5 us -> 39.7 us
    ppermute x0 -> x1, starting transfers between devices: none -> 4.82 us  [scores_of(): lax.ppermute(right_parts, 'feat', [(i, i ^ 1) for i in range(peers)])]
    all_to_all x1, starting transfers between devices: 6.66 us -> 4.5 us  [scores_of(): lax.all_to_all(right_parts, 'feat', 0, 0, tiled=True, axis_index_groups=a...]
    ppermute x0 -> x1, waiting for transfers between devices: none -> 1.99 us  [scores_of(): lax.ppermute(right_parts, 'feat', [(i, i ^ 1) for i in range(peers)])]
    all_to_all x1, starting transfers between devices: 11.7 us -> 10.7 us  [scores_of(): lax.all_to_all(own_valid, 'ex', 0, 0, tiled=True, axis_index_groups=members)]
    all_to_all x1, blocking collectives: 12.3 us -> 13.1 us  [scores_of(): products = lax.all_to_all(products, 'feat', 0, 0, tiled=True)]
    pallas_call x7 -> x8, Pallas kernels: 9.61 us -> 9.55 us  [call(): pl.pallas_call(kernel, out_shape=out_shape, in_specs=specs, out_specs=out...]
  transfers between devices with their start and end apart: 5 -> 6, of which waited for: 4 -> 5; matrix products, arithmetic and copies ran while one was open for 0% -> 0% of each run, Pallas kernels for 8% -> 8%
where the time goes in v12:
time: 80.7 us; the launch traced here: 80.2 us
  starting transfers between devices  39.7 us (49%)
  waiting for transfers between devices  16.7 us (21%)
  blocking collectives  13.1 us (16%)
  Pallas kernels  9.55 us (12%)
  local copies, waits for them, and re-layouts  1.04 us (1%)
    all_to_all x1, blocking collectives, scores_of(): products = lax.all_to_all(products, 'feat', 0, 0, tiled=True)  13.1 us
    all_to_all x1, starting transfers between devices, scores_of(): lax.all_to_all(own_valid, 'ex', 0, 0, tiled=True, axis_index_groups=members)  10.7 us
    pallas_call x8, Pallas kernels, call(): pl.pallas_call(kernel, out_shape=out_shape, in_specs=specs, out_specs=out...  9.55 us
    ppermute x1, starting transfers between devices, scores_of(): other = lax.ppermute(half, 'ex', [(i, i ^ 1) for i in range(groups)])  8.73 us
    ppermute x1, starting transfers between devices, scores_of(): far = lax.ppermute(near, 'ex', [(i, i ^ 4) for i in range(groups)])  7.49 us
    all_to_all x1, waiting for transfers between devices, scores_of(): lax.all_to_all(right_parts, 'feat', 0, 0, tiled=True, axis_index_groups=a...  5.84 us
    ppermute x1, starting transfers between devices, scores_of(): lax.ppermute(right_parts, 'feat', [(i, i ^ 1) for i in range(peers)])  4.82 us
    all_to_all x1, starting transfers between devices, scores_of(): lax.all_to_all(right_parts, 'feat', 0, 0, tiled=True, axis_index_groups=a...  4.5 us
  transfers between devices with their start and end apart: 6, of which 5 were waited for; matrix products, arithmetic and copies ran while one was open for 0% of the time, Pallas kernels for 8%

profile of v12, /device:TPU:1, one launch (start us, length us, event | category | flops | bytes accessed | tf_op | source)
XLA Modules:
  0.0 80.2 jit_solution(7319056906143487824)
XLA Ops:
  0.0 0.0 copy-start.1
  0.0 1.7 %shard_map.73.own_ref = f32[32,768]{1,0:T(8,128)S(1)} custom-call(bf16[2,768,256]{2,1,0:T(8,128)(2,1)} %bitcast.9, bf16[2,128,256]{2,1,0:T(8,128)(2,1)} %a_hbm.1, bf16[2,16,128]{2,1,0:T(8,128)(2,1)} %bitcast.11), custom_call_target="tpu_custom_call" | custom-call | flops 201326592 | bytes 786432 | tf_op jit(solution)/shard_map/pallas_call | solution.py:50
  1.7 4.8 %collective-permute-start = (f32[32,768]{1,0:T(8,128)S(1)}, f32[32,768]{1,0:T(8,128)S(1)}, u32[]{:S(2)}, u32[]{:S(2)}) collective-permute-start(f32[32,768]{1,0:T(8,128)S(1)} %shard_map.73.own_ref), channel_id=1, source_target_pairs={{0,1},{1,0},{2,3},{3,2},{4,5},{5,4},{6,7},{7,6},{8,9},{9,8},{10,11... | collective-permute-start | bytes 294920 | tf_op jit(solution)/shard_map/ppermute | solution.py:280
  6.5 2.0 %collective-permute-done.other_ref = f32[32,768]{1,0:T(8,128)S(1)} collective-permute-done((f32[32,768]{1,0:T(8,128)S(1)}, f32[32,768]{1,0:T(8,128)S(1)}, u32[]{:S(2)}, u32[]{:S(2)}) %collective-permute-start) | collective-permute-done | bytes 98336 | tf_op jit(solution)/shard_map/ppermute | solution.py:280
  8.5 0.8 shard_map.74
  9.3 4.5 %all-to-all-start = ((f32[4,32,768]{2,1,0:T(8,128)}), f32[4,32,768]{2,1,0:T(8,128)S(1)}, u32[]{:S(2)}, u32[]{:S(2)}) async-start(f32[4,32,768]{2,1,0:T(8,128)} %shard_map.74), calls=%async_computation | async-start | bytes 786432 | tf_op jit(solution)/shard_map/all_to_all | solution.py:289
  13.8 0.0 copy-done.1
  13.8 0.2 reshape.16
  14.0 0.1 copy.8
  14.0 0.1 broadcast_in_dim.11
  14.1 5.8 %all-to-all-done.rr_ref = f32[4,32,768]{2,1,0:T(8,128)S(1)} async-done(((f32[4,32,768]{2,1,0:T(8,128)}), f32[4,32,768]{2,1,0:T(8,128)S(1)}, u32[]{:S(2)}, u32[]{:S(2)}) %all-to-all-start) | async-done | bytes 393248 | tf_op jit(solution)/shard_map/all_to_all | solution.py:289
  20.0 0.7 broadcast_in_dim.12
  20.6 10.7 %all-to-all-start.2 = ((bf16[16,8,512]{2,1,0:T(8,128)(2,1)}), bf16[16,8,512]{2,1,0:T(8,128)(2,1)S(1)}, u32[]{:S(2)}, u32[]{:S(2)}) async-start(bf16[16,8,512]{2,1,0:T(8,128)(2,1)} %broadcast_in_dim.12), calls=%async_computation.2 | async-start | bytes 262144 | tf_op jit(solution)/shard_map/all_to_all | solution.py:246
  31.3 0.0 copy-start
  31.3 3.2 %shard_map.75.left_ref = bf16[2,768,512]{2,1,0:T(8,128)(2,1)S(1)} custom-call(bf16[2,768,512]{2,1,0:T(8,128)(2,1)} %bitcast.8, bf16[2,512,512]{2,1,0:T(8,128)(2,1)} %l_hbm.1), custom_call_target="tpu_custom_call" | custom-call | flops 805306368 | bytes 4194304 | tf_op jit(solution)/shard_map/pallas_call | solution.py:50
  34.5 0.0 copy-done
  34.5 2.0 %shard_map.76 = bf16[8,256,128]{2,1,0:T(8,128)(2,1)} custom-call(s32[32]{0:T(128)S(1)} %copy-done, f32[4,32,768]{2,1,0:T(8,128)S(1)} %all-to-all-done.rr_ref, bf16[2,768,512]{2,1,0:T(8,128)(2,1)S(1)} %shard_map.75.left_ref), custom_call_target="tpu_custom_call" | custom-call | flops 402653184 | bytes 3145728 | tf_op jit(solution)/shard_map/pallas_call | solution.py:50
  36.6 4.2 %all-to-all-done.2 = bf16[16,8,512]{2,1,0:T(8,128)(2,1)S(1)} async-done(((bf16[16,8,512]{2,1,0:T(8,128)(2,1)}), bf16[16,8,512]{2,1,0:T(8,128)(2,1)S(1)}, u32[]{:S(2)}, u32[]{:S(2)}) %all-to-all-start.2) | async-done | bytes 131104 | tf_op jit(solution)/shard_map/all_to_all | solution.py:246
  40.8 3.5 %all-to-all-start.1 = ((bf16[8,256,128]{2,1,0:T(8,128)(2,1)}), bf16[8,256,128]{2,1,0:T(8,128)(2,1)S(1)}, u32[]{:S(2)}, u32[]{:S(2)}) async-start(bf16[8,256,128]{2,1,0:T(8,128)(2,1)} %shard_map.76), calls=%async_computation.1 | async-start | bytes 1048576 | tf_op jit(solution)/shard_map/all_to_all | solution.py:313
  44.3 7.5 %collective-permute-start.1 = (bf16[128,512]{1,0:T(8,128)(2,1)S(1)}, bf16[128,512]{1,0:T(8,128)(2,1)S(1)}, u32[]{:S(2)}, u32[]{:S(2)}) collective-permute-start(bf16[128,512]{1,0:T(8,128)(2,1)S(1)} %bitcast.6), channel_id=1, source_target_pairs={{0,32},{8,40},{16,48},{24,56},{32,0},{40,8},{48,16},{56,24},{64,96... | collective-permute-start | bytes 393224 | tf_op jit(solution)/shard_map/ppermute | solution.py:248
  51.8 3.5 %collective-permute-done.1.far_ref = bf16[128,512]{1,0:T(8,128)(2,1)S(1)} collective-permute-done((bf16[128,512]{1,0:T(8,128)(2,1)S(1)}, bf16[128,512]{1,0:T(8,128)(2,1)S(1)}, u32[]{:S(2)}, u32[]{:S(2)}) %collective-permute-start.1) | collective-permute-done | bytes 131104 | tf_op jit(solution)/shard_map/ppermute | solution.py:248
  55.3 8.7 %collective-permute-start.2 = (bf16[256,512]{1,0:T(8,128)(2,1)S(1)}, bf16[256,512]{1,0:T(8,128)(2,1)S(1)}, u32[]{:S(2)}, u32[]{:S(2)}) collective-permute-start(bf16[256,512]{1,0:T(8,128)(2,1)S(1)} %shard_map.77.half_ref), channel_id=1, source_target_pairs={{0,8},{8,0},{16,24},{24,16},{32,40},{40,32},{48,56},{56,48},{64,72... | collective-permute-start | bytes 786440 | tf_op jit(solution)/shard_map/ppermute | solution.py:256
  64.1 1.1 %collective-permute-done.2.other_ref = bf16[256,512]{1,0:T(8,128)(2,1)S(1)} collective-permute-done((bf16[256,512]{1,0:T(8,128)(2,1)S(1)}, bf16[256,512]{1,0:T(8,128)(2,1)S(1)}, u32[]{:S(2)}, u32[]{:S(2)}) %collective-permute-start.2) | collective-permute-done | bytes 262176 | tf_op jit(solution)/shard_map/ppermute | solution.py:256
  65.2 0.8 shard_map.78
  66.0 0.0 all-to-all-done.1.part_ref
  66.0 0.4 shard_map.79
  66.4 13.1 %all_to_all.20.part_ref = f32[8,40,256]{2,1,0:T(8,128)S(1)} all-to-all(f32[8,40,256]{2,1,0:T(8,128)S(1)} %shard_map.79), channel_id=1, replica_groups=mesh['ex'=64,'feat'=8] {'feat'}, dimensions={0} | all-to-all | bytes 655360 | tf_op jit(solution)/shard_map/all_to_all | solution.py:322
  79.5 0.7 shard_map.80
  (1 shorter events, 0.0 us)
Async XLA Ops:
  0.0 13.8 %copy-start.1 = (bf16[4,1024]{1,0:T(4,128)(2,1)S(1)}, bf16[4,1024]{1,0:T(4,128)(2,1)}, u32[]{:S(2)}) copy-start(bf16[4,1024]{1,0:T(4,128)(2,1)} %param.13) | copy-start | bytes 24580
  1.7 6.8 %collective-permute-start = (f32[32,768]{1,0:T(8,128)S(1)}, f32[32,768]{1,0:T(8,128)S(1)}, u32[]{:S(2)}, u32[]{:S(2)}) collective-permute-start(f32[32,768]{1,0:T(8,128)S(1)} %shard_map.73.own_ref), channel_id=1, source_target_pairs={{0,1},{1,0},{2,3},{3,2},{4,5},{5,4},{6,7},{7,6},{8,9},{9,8},{10,11... | collective-permute-start | bytes 294920 | tf_op jit(solution)/shard_map/ppermute | solution.py:280
  9.3 10.7 %all-to-all-start = ((f32[4,32,768]{2,1,0:T(8,128)}), f32[4,32,768]{2,1,0:T(8,128)S(1)}, u32[]{:S(2)}, u32[]{:S(2)}) async-start(f32[4,32,768]{2,1,0:T(8,128)} %shard_map.74), calls=%async_computation | async-start | bytes 786432 | tf_op jit(solution)/shard_map/all_to_all | solution.py:289
  20.6 20.1 %all-to-all-start.2 = ((bf16[16,8,512]{2,1,0:T(8,128)(2,1)}), bf16[16,8,512]{2,1,0:T(8,128)(2,1)S(1)}, u32[]{:S(2)}, u32[]{:S(2)}) async-start(bf16[16,8,512]{2,1,0:T(8,128)(2,1)} %broadcast_in_dim.12), calls=%async_computation.2 | async-start | bytes 262144 | tf_op jit(solution)/shard_map/all_to_all | solution.py:246
  31.3 3.2 %copy-start = (s32[32]{0:T(128)S(1)}, s32[32]{0:T(128)}, u32[]{:S(2)}) copy-start(s32[32]{0:T(128)} %seq_ref.1) | copy-start | bytes 388
  40.8 25.2 %all-to-all-start.1 = ((bf16[8,256,128]{2,1,0:T(8,128)(2,1)}), bf16[8,256,128]{2,1,0:T(8,128)(2,1)S(1)}, u32[]{:S(2)}, u32[]{:S(2)}) async-start(bf16[8,256,128]{2,1,0:T(8,128)(2,1)} %shard_map.76), calls=%async_computation.1 | async-start | bytes 1048576 | tf_op jit(solution)/shard_map/all_to_all | solution.py:313
  44.3 11.0 %collective-permute-start.1 = (bf16[128,512]{1,0:T(8,128)(2,1)S(1)}, bf16[128,512]{1,0:T(8,128)(2,1)S(1)}, u32[]{:S(2)}, u32[]{:S(2)}) collective-permute-start(bf16[128,512]{1,0:T(8,128)(2,1)S(1)} %bitcast.6), channel_id=1, source_target_pairs={{0,32},{8,40},{16,48},{24,56},{32,0},{40,8},{48,16},{56,24},{64,96... | collective-permute-start | bytes 393224 | tf_op jit(solution)/shard_map/ppermute | solution.py:248
  55.3 9.9 %collective-permute-start.2 = (bf16[256,512]{1,0:T(8,128)(2,1)S(1)}, bf16[256,512]{1,0:T(8,128)(2,1)S(1)}, u32[]{:S(2)}, u32[]{:S(2)}) collective-permute-start(bf16[256,512]{1,0:T(8,128)(2,1)S(1)} %shard_map.77.half_ref), channel_id=1, source_target_pairs={{0,8},{8,0},{16,24},{24,16},{32,40},{40,32},{48,56},{56,48},{64,72... | collective-permute-start | bytes 786440 | tf_op jit(solution)/shard_map/ppermute | solution.py:256

commit v13 on v12

--- a/solution.py
+++ b/solution.py
@@ -125,9 +125,14 @@
     out_lane = lax.broadcasted_iota(jnp.int32, (GROUP * half, 128), 1)
     stores = []
     for g in range(examples // GROUP):
-        x0 = first if g == 0 else pltpu.roll(first, (tokens - g * span) % tokens, 1)
-        x1 = pltpu.roll(second, (tokens + span - g * span) % tokens, 1)
-        x0, x1 = x0[:, :width], x1[:, :width]
+        base = min(g * span // 128 * 128, tokens - width)
+        offset = g * span - base
+        x0 = first[:, base:base + width]
+        x1 = second[:, base:base + width]
+        if offset:
+            x0 = pltpu.roll(x0, width - offset, 1)
+        if offset != span:
+            x1 = pltpu.roll(x1, (width + span - offset) % width, 1)
         blocks = []
         for i in range(GROUP):
             start = i * seq
@@ -142,17 +147,14 @@
         part = part.reshape(GROUP, 2, half, kl)
         even = part[:, 0].reshape(GROUP * half, kl)
         odd = part[:, 1].reshape(GROUP * half, kl)
-        for p in range(peers):
-            tile = (p * owned) // 128 * 128
-            e = even[:, tile:tile + 128]
-            o = odd[:, tile:tile + 128]
-            if (p * owned) % 128 == 0:
-                o = pltpu.roll(o, 64, 1)
-            else:
-                e = pltpu.roll(e, 64, 1)
-            both_k = jnp.where(out_lane < 64, e, o)
-            r = g * GROUP * half
-            out_ref[p, r:r + GROUP * half, :] = both_k.astype(BF16)
+        r = g * GROUP * half
+        for tile in range(kl // 128):
+            e = even[:, tile * 128:(tile + 1) * 128]
+            o = odd[:, tile * 128:(tile + 1) * 128]
+            kept = jnp.where(out_lane < owned, e, o)
+            moved = pltpu.roll(jnp.where(out_lane < owned, o, e), owned, 1)
+            out_ref[2 * tile, r:r + GROUP * half, :] = jnp.where(out_lane < owned, kept, moved).astype(BF16)
+            out_ref[2 * tile + 1, r:r + GROUP * half, :] = jnp.where(out_lane < owned, moved, kept).astype(BF16)
         rows = pl.ds(g * GROUP * half, GROUP * half)
         stores.append(pltpu.make_async_copy(out_ref.at[:, rows], out_hbm.at[:, rows], out_sems.at[g]))
         stores[-1].start()

time: 80.7 us -> 80.7 us (level)
  transfers between devices with their start and end apart: 6 -> 6, of which waited for: 5 -> 5; matrix products, arithmetic and copies ran while one was open for 0% -> 0% of each run, Pallas kernels for 8% -> 7%
where the time goes in v13:
time: 80.7 us; the launch traced here: 80.2 us
  starting transfers between devices  39.7 us (49%)
  waiting for transfers between devices  16.9 us (21%)
  blocking collectives  13.1 us (16%)
  Pallas kernels  9.34 us (12%)
  local copies, waits for them, and re-layouts  1.04 us (1%)
    all_to_all x1, blocking collectives, scores_of(): products = lax.all_to_all(products, 'feat', 0, 0, tiled=True)  13.1 us
    all_to_all x1, starting transfers between devices, scores_of(): lax.all_to_all(own_valid, 'ex', 0, 0, tiled=True, axis_index_groups=members)  10.7 us
    pallas_call x8, Pallas kernels, call(): pl.pallas_call(kernel, out_shape=out_shape, in_specs=specs, out_specs=out...  9.34 us
    ppermute x1, starting transfers between devices, scores_of(): other = lax.ppermute(half, 'ex', [(i, i ^ 1) for i in range(groups)])  8.73 us
    ppermute x1, starting transfers between devices, scores_of(): far = lax.ppermute(near, 'ex', [(i, i ^ 4) for i in range(groups)])  7.49 us
    all_to_all x1, waiting for transfers between devices, scores_of(): lax.all_to_all(right_parts, 'feat', 0, 0, tiled=True, axis_index_groups=a...  5.84 us
    ppermute x1, starting transfers between devices, scores_of(): lax.ppermute(right_parts, 'feat', [(i, i ^ 1) for i in range(peers)])  4.82 us
    all_to_all x1, starting transfers between devices, scores_of(): lax.all_to_all(right_parts, 'feat', 0, 0, tiled=True, axis_index_groups=a...  4.5 us
  transfers between devices with their start and end apart: 6, of which 5 were waited for; matrix products, arithmetic and copies ran while one was open for 0% of the time, Pallas kernels for 7%

profile of v13, /device:TPU:1, one launch (start us, length us, event | category | flops | bytes accessed | tf_op | source)
XLA Modules:
  0.0 80.2 jit_solution(330299493896478891)
XLA Ops:
  0.0 0.0 copy-start.1
  0.0 1.7 %shard_map.73.own_ref = f32[32,768]{1,0:T(8,128)S(1)} custom-call(bf16[2,768,256]{2,1,0:T(8,128)(2,1)} %bitcast.9, bf16[2,128,256]{2,1,0:T(8,128)(2,1)} %a_hbm.1, bf16[2,16,128]{2,1,0:T(8,128)(2,1)} %bitcast.11), custom_call_target="tpu_custom_call" | custom-call | flops 201326592 | bytes 786432 | tf_op jit(solution)/shard_map/pallas_call | solution.py:50
  1.7 4.8 %collective-permute-start = (f32[32,768]{1,0:T(8,128)S(1)}, f32[32,768]{1,0:T(8,128)S(1)}, u32[]{:S(2)}, u32[]{:S(2)}) collective-permute-start(f32[32,768]{1,0:T(8,128)S(1)} %shard_map.73.own_ref), channel_id=1, source_target_pairs={{0,1},{1,0},{2,3},{3,2},{4,5},{5,4},{6,7},{7,6},{8,9},{9,8},{10,11... | collective-permute-start | bytes 294920 | tf_op jit(solution)/shard_map/ppermute | solution.py:282
  6.5 2.0 %collective-permute-done.other_ref = f32[32,768]{1,0:T(8,128)S(1)} collective-permute-done((f32[32,768]{1,0:T(8,128)S(1)}, f32[32,768]{1,0:T(8,128)S(1)}, u32[]{:S(2)}, u32[]{:S(2)}) %collective-permute-start) | collective-permute-done | bytes 98336 | tf_op jit(solution)/shard_map/ppermute | solution.py:282
  8.5 0.8 shard_map.74
  9.3 4.5 %all-to-all-start = ((f32[4,32,768]{2,1,0:T(8,128)}), f32[4,32,768]{2,1,0:T(8,128)S(1)}, u32[]{:S(2)}, u32[]{:S(2)}) async-start(f32[4,32,768]{2,1,0:T(8,128)} %shard_map.74), calls=%async_computation | async-start | bytes 786432 | tf_op jit(solution)/shard_map/all_to_all | solution.py:291
  13.8 0.0 copy-done.1
  13.8 0.2 reshape.16
  14.0 0.1 copy.8
  14.0 0.1 broadcast_in_dim.11
  14.1 5.8 %all-to-all-done.rr_ref = f32[4,32,768]{2,1,0:T(8,128)S(1)} async-done(((f32[4,32,768]{2,1,0:T(8,128)}), f32[4,32,768]{2,1,0:T(8,128)S(1)}, u32[]{:S(2)}, u32[]{:S(2)}) %all-to-all-start) | async-done | bytes 393248 | tf_op jit(solution)/shard_map/all_to_all | solution.py:291
  20.0 0.7 broadcast_in_dim.12
  20.6 10.7 %all-to-all-start.2 = ((bf16[16,8,512]{2,1,0:T(8,128)(2,1)}), bf16[16,8,512]{2,1,0:T(8,128)(2,1)S(1)}, u32[]{:S(2)}, u32[]{:S(2)}) async-start(bf16[16,8,512]{2,1,0:T(8,128)(2,1)} %broadcast_in_dim.12), calls=%async_computation.2 | async-start | bytes 262144 | tf_op jit(solution)/shard_map/all_to_all | solution.py:248
  31.3 0.0 copy-start
  31.3 3.2 %shard_map.75.left_ref = bf16[2,768,512]{2,1,0:T(8,128)(2,1)S(1)} custom-call(bf16[2,768,512]{2,1,0:T(8,128)(2,1)} %bitcast.8, bf16[2,512,512]{2,1,0:T(8,128)(2,1)} %l_hbm.1), custom_call_target="tpu_custom_call" | custom-call | flops 805306368 | bytes 4194304 | tf_op jit(solution)/shard_map/pallas_call | solution.py:50
  34.5 0.0 copy-done
  34.5 1.8 %shard_map.76 = bf16[8,256,128]{2,1,0:T(8,128)(2,1)} custom-call(s32[32]{0:T(128)S(1)} %copy-done, f32[4,32,768]{2,1,0:T(8,128)S(1)} %all-to-all-done.rr_ref, bf16[2,768,512]{2,1,0:T(8,128)(2,1)S(1)} %shard_map.75.left_ref), custom_call_target="tpu_custom_call" | custom-call | flops 402653184 | bytes 3145728 | tf_op jit(solution)/shard_map/pallas_call | solution.py:50
  36.4 4.4 %all-to-all-done.2 = bf16[16,8,512]{2,1,0:T(8,128)(2,1)S(1)} async-done(((bf16[16,8,512]{2,1,0:T(8,128)(2,1)}), bf16[16,8,512]{2,1,0:T(8,128)(2,1)S(1)}, u32[]{:S(2)}, u32[]{:S(2)}) %all-to-all-start.2) | async-done | bytes 131104 | tf_op jit(solution)/shard_map/all_to_all | solution.py:248
  40.8 3.5 %all-to-all-start.1 = ((bf16[8,256,128]{2,1,0:T(8,128)(2,1)}), bf16[8,256,128]{2,1,0:T(8,128)(2,1)S(1)}, u32[]{:S(2)}, u32[]{:S(2)}) async-start(bf16[8,256,128]{2,1,0:T(8,128)(2,1)} %shard_map.76), calls=%async_computation.1 | async-start | bytes 1048576 | tf_op jit(solution)/shard_map/all_to_all | solution.py:315
  44.3 7.5 %collective-permute-start.1 = (bf16[128,512]{1,0:T(8,128)(2,1)S(1)}, bf16[128,512]{1,0:T(8,128)(2,1)S(1)}, u32[]{:S(2)}, u32[]{:S(2)}) collective-permute-start(bf16[128,512]{1,0:T(8,128)(2,1)S(1)} %bitcast.6), channel_id=1, source_target_pairs={{0,32},{8,40},{16,48},{24,56},{32,0},{40,8},{48,16},{56,24},{64,96... | collective-permute-start | bytes 393224 | tf_op jit(solution)/shard_map/ppermute | solution.py:250
  51.8 3.5 %collective-permute-done.1.far_ref = bf16[128,512]{1,0:T(8,128)(2,1)S(1)} collective-permute-done((bf16[128,512]{1,0:T(8,128)(2,1)S(1)}, bf16[128,512]{1,0:T(8,128)(2,1)S(1)}, u32[]{:S(2)}, u32[]{:S(2)}) %collective-permute-start.1) | collective-permute-done | bytes 131104 | tf_op jit(solution)/shard_map/ppermute | solution.py:250
  55.3 8.7 %collective-permute-start.2 = (bf16[256,512]{1,0:T(8,128)(2,1)S(1)}, bf16[256,512]{1,0:T(8,128)(2,1)S(1)}, u32[]{:S(2)}, u32[]{:S(2)}) collective-permute-start(bf16[256,512]{1,0:T(8,128)(2,1)S(1)} %shard_map.77.half_ref), channel_id=1, source_target_pairs={{0,8},{8,0},{16,24},{24,16},{32,40},{40,32},{48,56},{56,48},{64,72... | collective-permute-start | bytes 786440 | tf_op jit(solution)/shard_map/ppermute | solution.py:258
  64.1 1.1 %collective-permute-done.2.other_ref = bf16[256,512]{1,0:T(8,128)(2,1)S(1)} collective-permute-done((bf16[256,512]{1,0:T(8,128)(2,1)S(1)}, bf16[256,512]{1,0:T(8,128)(2,1)S(1)}, u32[]{:S(2)}, u32[]{:S(2)}) %collective-permute-start.2) | collective-permute-done | bytes 262176 | tf_op jit(solution)/shard_map/ppermute | solution.py:258
  65.2 0.8 shard_map.78
  66.0 0.0 all-to-all-done.1.part_ref
  66.0 0.4 shard_map.79
  66.4 13.1 %all_to_all.20.part_ref = f32[8,40,256]{2,1,0:T(8,128)S(1)} all-to-all(f32[8,40,256]{2,1,0:T(8,128)S(1)} %shard_map.79), channel_id=1, replica_groups=mesh['ex'=64,'feat'=8] {'feat'}, dimensions={0} | all-to-all | bytes 655360 | tf_op jit(solution)/shard_map/all_to_all | solution.py:324
  79.5 0.7 shard_map.80
  (1 shorter events, 0.0 us)
Async XLA Ops:
  0.0 13.8 %copy-start.1 = (bf16[4,1024]{1,0:T(4,128)(2,1)S(1)}, bf16[4,1024]{1,0:T(4,128)(2,1)}, u32[]{:S(2)}) copy-start(bf16[4,1024]{1,0:T(4,128)(2,1)} %param.13) | copy-start | bytes 24580
  1.7 6.8 %collective-permute-start = (f32[32,768]{1,0:T(8,128)S(1)}, f32[32,768]{1,0:T(8,128)S(1)}, u32[]{:S(2)}, u32[]{:S(2)}) collective-permute-start(f32[32,768]{1,0:T(8,128)S(1)} %shard_map.73.own_ref), channel_id=1, source_target_pairs={{0,1},{1,0},{2,3},{3,2},{4,5},{5,4},{6,7},{7,6},{8,9},{9,8},{10,11... | collective-permute-start | bytes 294920 | tf_op jit(solution)/shard_map/ppermute | solution.py:282
  9.3 10.7 %all-to-all-start = ((f32[4,32,768]{2,1,0:T(8,128)}), f32[4,32,768]{2,1,0:T(8,128)S(1)}, u32[]{:S(2)}, u32[]{:S(2)}) async-start(f32[4,32,768]{2,1,0:T(8,128)} %shard_map.74), calls=%async_computation | async-start | bytes 786432 | tf_op jit(solution)/shard_map/all_to_all | solution.py:291
  20.6 20.1 %all-to-all-start.2 = ((bf16[16,8,512]{2,1,0:T(8,128)(2,1)}), bf16[16,8,512]{2,1,0:T(8,128)(2,1)S(1)}, u32[]{:S(2)}, u32[]{:S(2)}) async-start(bf16[16,8,512]{2,1,0:T(8,128)(2,1)} %broadcast_in_dim.12), calls=%async_computation.2 | async-start | bytes 262144 | tf_op jit(solution)/shard_map/all_to_all | solution.py:248
  31.3 3.2 %copy-start = (s32[32]{0:T(128)S(1)}, s32[32]{0:T(128)}, u32[]{:S(2)}) copy-start(s32[32]{0:T(128)} %seq_ref.1) | copy-start | bytes 388
  40.8 25.2 %all-to-all-start.1 = ((bf16[8,256,128]{2,1,0:T(8,128)(2,1)}), bf16[8,256,128]{2,1,0:T(8,128)(2,1)S(1)}, u32[]{:S(2)}, u32[]{:S(2)}) async-start(bf16[8,256,128]{2,1,0:T(8,128)(2,1)} %shard_map.76), calls=%async_computation.1 | async-start | bytes 1048576 | tf_op jit(solution)/shard_map/all_to_all | solution.py:315
  44.3 11.0 %collective-permute-start.1 = (bf16[128,512]{1,0:T(8,128)(2,1)S(1)}, bf16[128,512]{1,0:T(8,128)(2,1)S(1)}, u32[]{:S(2)}, u32[]{:S(2)}) collective-permute-start(bf16[128,512]{1,0:T(8,128)(2,1)S(1)} %bitcast.6), channel_id=1, source_target_pairs={{0,32},{8,40},{16,48},{24,56},{32,0},{40,8},{48,16},{56,24},{64,96... | collective-permute-start | bytes 393224 | tf_op jit(solution)/shard_map/ppermute | solution.py:250
  55.3 9.9 %collective-permute-start.2 = (bf16[256,512]{1,0:T(8,128)(2,1)S(1)}, bf16[256,512]{1,0:T(8,128)(2,1)S(1)}, u32[]{:S(2)}, u32[]{:S(2)}) collective-permute-start(bf16[256,512]{1,0:T(8,128)(2,1)S(1)} %shard_map.77.half_ref), channel_id=1, source_target_pairs={{0,8},{8,0},{16,24},{24,16},{32,40},{40,32},{48,56},{56,48},{64,72... | collective-permute-start | bytes 786440 | tf_op jit(solution)/shard_map/ppermute | solution.py:258

commit v14 on v13

--- a/solution.py
+++ b/solution.py
@@ -172,8 +172,8 @@
     count = half_ref.shape[0]
     place = lax.broadcasted_iota(jnp.int32, (8, 2 * count), 1)
     core = ((place >> 8) ^ own_ref[0]) & 1
-    far = ((place >> 7) ^ (own_ref[0] >> 2)) & 1
-    index = (((place >> 4) & 7) << 5) | (far << 4) | (((place >> 3) & 1) << 3) | (core << 2) | ((place >> 1) & 3)
+    far = ((place >> 7) ^ (own_ref[0] >> 5)) & 1
+    index = (far << 7) | (((place >> 3) & 15) << 3) | (core << 2) | ((place >> 1) & 3)
     row = lax.broadcasted_iota(jnp.int32, (count, 2 * count), 0)
     squares = jnp.zeros((count, 128), F32)
     for h in range(2):
@@ -244,10 +244,11 @@
 
     own_valid = valid_grads.reshape(-1, owned, 2, 8).transpose(0, 3, 2, 1).reshape(1, -1, owned * proj // 2)
     own_valid = jnp.broadcast_to(own_valid, (groups // 4,) + own_valid.shape[1:])
-    members = [[y * 8 + z * 4 + i * 2 + c for y in range(groups // 8) for i in range(2)] for z in range(2) for c in range(2)]
+    far_bit = groups // 2
+    members = [[y * far_bit + i * 2 + c for i in range(far_bit // 2)] for y in range(2) for c in range(2)]
     near = lax.all_to_all(own_valid, "ex", 0, 0, tiled=True, axis_index_groups=members)
     near = near.reshape(valid_count // 2, owned * proj // 2)
-    far = lax.ppermute(near, "ex", [(i, i ^ 4) for i in range(groups)])
+    far = lax.ppermute(near, "ex", [(i, i ^ far_bit) for i in range(groups)])
     half = call(
         join_kernel,
         jax.ShapeDtypeStruct((valid_count, owned * proj // 2), BF16),

time: 80.7 us -> 81.2 us (level)
  waiting for transfers between devices: 16.9 us -> 20.4 us
  starting transfers between devices: 39.7 us -> 37.4 us
    ppermute x1, starting transfers between devices: 7.49 us -> 4.76 us  [scores_of(): far = lax.ppermute(near, 'ex', [(i, i ^ far_bit) for i in range(groups)])]
    ppermute x1, waiting for transfers between devices: 3.54 us -> 6.26 us  [scores_of(): far = lax.ppermute(near, 'ex', [(i, i ^ far_bit) for i in range(groups)])]
    all_to_all x1, starting transfers between devices: 10.7 us -> 12 us  [scores_of(): lax.all_to_all(own_valid, 'ex', 0, 0, tiled=True, axis_index_groups=members)]
    ppermute x1, starting transfers between devices: 8.73 us -> 7.74 us  [scores_of(): other = lax.ppermute(half, 'ex', [(i, i ^ 1) for i in range(groups)])]
where the time goes in v14:
time: 81.2 us; the launch traced here: 80.8 us
  starting transfers between devices  37.4 us (46%)
  waiting for transfers between devices  20.4 us (25%)
  blocking collectives  12.6 us (16%)
  Pallas kernels  9.34 us (12%)
  local copies, waits for them, and re-layouts  1.04 us (1%)
    all_to_all x1, blocking collectives, scores_of(): products = lax.all_to_all(products, 'feat', 0, 0, tiled=True)  12.6 us
    all_to_all x1, starting transfers between devices, scores_of(): lax.all_to_all(own_valid, 'ex', 0, 0, tiled=True, axis_index_groups=members)  12 us
    pallas_call x8, Pallas kernels, call(): pl.pallas_call(kernel, out_shape=out_shape, in_specs=specs, out_specs=out...  9.34 us
    ppermute x1, starting transfers between devices, scores_of(): other = lax.ppermute(half, 'ex', [(i, i ^ 1) for i in range(groups)])  7.74 us
    ppermute x1, waiting for transfers between devices, scores_of(): far = lax.ppermute(near, 'ex', [(i, i ^ far_bit) for i in range(groups)])  6.26 us
    all_to_all x1, waiting for transfers between devices, scores_of(): lax.all_to_all(right_parts, 'feat', 0, 0, tiled=True, axis_index_groups=a...  5.84 us
    all_to_all x1, waiting for transfers between devices, scores_of(): lax.all_to_all(own_valid, 'ex', 0, 0, tiled=True, axis_index_groups=members)  5.12 us
    ppermute x1, starting transfers between devices, scores_of(): lax.ppermute(right_parts, 'feat', [(i, i ^ 1) for i in range(peers)])  4.82 us
  transfers between devices with their start and end apart: 6, of which 5 were waited for; matrix products, arithmetic and copies ran while one was open for 0% of the time, Pallas kernels for 7%

profile of v14, /device:TPU:1, one launch (start us, length us, event | category | flops | bytes accessed | tf_op | source)
XLA Modules:
  0.0 80.8 jit_solution(4985200883473520470)
XLA Ops:
  0.0 0.0 copy-start.1
  0.0 1.7 %shard_map.73.own_ref = f32[32,768]{1,0:T(8,128)S(1)} custom-call(bf16[2,768,256]{2,1,0:T(8,128)(2,1)} %bitcast.9, bf16[2,128,256]{2,1,0:T(8,128)(2,1)} %a_hbm.1, bf16[2,16,128]{2,1,0:T(8,128)(2,1)} %bitcast.11), custom_call_target="tpu_custom_call" | custom-call | flops 201326592 | bytes 786432 | tf_op jit(solution)/shard_map/pallas_call | solution.py:50
  1.7 4.8 %collective-permute-start = (f32[32,768]{1,0:T(8,128)S(1)}, f32[32,768]{1,0:T(8,128)S(1)}, u32[]{:S(2)}, u32[]{:S(2)}) collective-permute-start(f32[32,768]{1,0:T(8,128)S(1)} %shard_map.73.own_ref), channel_id=1, source_target_pairs={{0,1},{1,0},{2,3},{3,2},{4,5},{5,4},{6,7},{7,6},{8,9},{9,8},{10,11... | collective-permute-start | bytes 294920 | tf_op jit(solution)/shard_map/ppermute | solution.py:283
  6.5 2.0 %collective-permute-done.other_ref = f32[32,768]{1,0:T(8,128)S(1)} collective-permute-done((f32[32,768]{1,0:T(8,128)S(1)}, f32[32,768]{1,0:T(8,128)S(1)}, u32[]{:S(2)}, u32[]{:S(2)}) %collective-permute-start) | collective-permute-done | bytes 98336 | tf_op jit(solution)/shard_map/ppermute | solution.py:283
  8.5 0.8 shard_map.74
  9.3 4.5 %all-to-all-start = ((f32[4,32,768]{2,1,0:T(8,128)}), f32[4,32,768]{2,1,0:T(8,128)S(1)}, u32[]{:S(2)}, u32[]{:S(2)}) async-start(f32[4,32,768]{2,1,0:T(8,128)} %shard_map.74), calls=%async_computation | async-start | bytes 786432 | tf_op jit(solution)/shard_map/all_to_all | solution.py:292
  13.8 0.0 copy-done.1
  13.8 0.2 reshape.16
  14.0 0.1 copy.8
  14.0 0.1 broadcast_in_dim.11
  14.1 5.8 %all-to-all-done.rr_ref = f32[4,32,768]{2,1,0:T(8,128)S(1)} async-done(((f32[4,32,768]{2,1,0:T(8,128)}), f32[4,32,768]{2,1,0:T(8,128)S(1)}, u32[]{:S(2)}, u32[]{:S(2)}) %all-to-all-start) | async-done | bytes 393248 | tf_op jit(solution)/shard_map/all_to_all | solution.py:292
  20.0 0.7 broadcast_in_dim.12
  20.6 12.0 %all-to-all-start.2 = ((bf16[16,8,512]{2,1,0:T(8,128)(2,1)}), bf16[16,8,512]{2,1,0:T(8,128)(2,1)S(1)}, u32[]{:S(2)}, u32[]{:S(2)}) async-start(bf16[16,8,512]{2,1,0:T(8,128)(2,1)} %broadcast_in_dim.12), calls=%async_computation.2 | async-start | bytes 262144 | tf_op jit(solution)/shard_map/all_to_all | solution.py:249
  32.7 0.0 copy-start
  32.7 3.2 %shard_map.75.left_ref = bf16[2,768,512]{2,1,0:T(8,128)(2,1)S(1)} custom-call(bf16[2,768,512]{2,1,0:T(8,128)(2,1)} %bitcast.8, bf16[2,512,512]{2,1,0:T(8,128)(2,1)} %l_hbm.1), custom_call_target="tpu_custom_call" | custom-call | flops 805306368 | bytes 4194304 | tf_op jit(solution)/shard_map/pallas_call | solution.py:50
  35.9 0.0 copy-done
  35.9 1.8 %shard_map.76 = bf16[8,256,128]{2,1,0:T(8,128)(2,1)} custom-call(s32[32]{0:T(128)S(1)} %copy-done, f32[4,32,768]{2,1,0:T(8,128)S(1)} %all-to-all-done.rr_ref, bf16[2,768,512]{2,1,0:T(8,128)(2,1)S(1)} %shard_map.75.left_ref), custom_call_target="tpu_custom_call" | custom-call | flops 402653184 | bytes 3145728 | tf_op jit(solution)/shard_map/pallas_call | solution.py:50
  37.7 5.1 %all-to-all-done.2 = bf16[16,8,512]{2,1,0:T(8,128)(2,1)S(1)} async-done(((bf16[16,8,512]{2,1,0:T(8,128)(2,1)}), bf16[16,8,512]{2,1,0:T(8,128)(2,1)S(1)}, u32[]{:S(2)}, u32[]{:S(2)}) %all-to-all-start.2) | async-done | bytes 131104 | tf_op jit(solution)/shard_map/all_to_all | solution.py:249
  42.9 3.5 %all-to-all-start.1 = ((bf16[8,256,128]{2,1,0:T(8,128)(2,1)}), bf16[8,256,128]{2,1,0:T(8,128)(2,1)S(1)}, u32[]{:S(2)}, u32[]{:S(2)}) async-start(bf16[8,256,128]{2,1,0:T(8,128)(2,1)} %shard_map.76), calls=%async_computation.1 | async-start | bytes 1048576 | tf_op jit(solution)/shard_map/all_to_all | solution.py:316
  46.4 4.8 %collective-permute-start.1 = (bf16[128,512]{1,0:T(8,128)(2,1)S(1)}, bf16[128,512]{1,0:T(8,128)(2,1)S(1)}, u32[]{:S(2)}, u32[]{:S(2)}) collective-permute-start(bf16[128,512]{1,0:T(8,128)(2,1)S(1)} %bitcast.6), channel_id=1, source_target_pairs={{0,256},{8,264},{16,272},{24,280},{32,288},{40,296},{48,304},{56,3... | collective-permute-start | bytes 393224 | tf_op jit(solution)/shard_map/ppermute | solution.py:251
  51.1 6.3 %collective-permute-done.1.far_ref = bf16[128,512]{1,0:T(8,128)(2,1)S(1)} collective-permute-done((bf16[128,512]{1,0:T(8,128)(2,1)S(1)}, bf16[128,512]{1,0:T(8,128)(2,1)S(1)}, u32[]{:S(2)}, u32[]{:S(2)}) %collective-permute-start.1) | collective-permute-done | bytes 131104 | tf_op jit(solution)/shard_map/ppermute | solution.py:251
  57.4 7.7 %collective-permute-start.2 = (bf16[256,512]{1,0:T(8,128)(2,1)S(1)}, bf16[256,512]{1,0:T(8,128)(2,1)S(1)}, u32[]{:S(2)}, u32[]{:S(2)}) collective-permute-start(bf16[256,512]{1,0:T(8,128)(2,1)S(1)} %shard_map.77.half_ref), channel_id=1, source_target_pairs={{0,8},{8,0},{16,24},{24,16},{32,40},{40,32},{48,56},{56,48},{64,72... | collective-permute-start | bytes 786440 | tf_op jit(solution)/shard_map/ppermute | solution.py:259
  65.2 1.1 %collective-permute-done.2.other_ref = bf16[256,512]{1,0:T(8,128)(2,1)S(1)} collective-permute-done((bf16[256,512]{1,0:T(8,128)(2,1)S(1)}, bf16[256,512]{1,0:T(8,128)(2,1)S(1)}, u32[]{:S(2)}, u32[]{:S(2)}) %collective-permute-start.2) | collective-permute-done | bytes 262176 | tf_op jit(solution)/shard_map/ppermute | solution.py:259
  66.3 0.8 shard_map.78
  67.1 0.0 all-to-all-done.1.part_ref
  67.1 0.4 shard_map.79
  67.5 12.6 %all_to_all.20.part_ref = f32[8,40,256]{2,1,0:T(8,128)S(1)} all-to-all(f32[8,40,256]{2,1,0:T(8,128)S(1)} %shard_map.79), channel_id=1, replica_groups=mesh['ex'=64,'feat'=8] {'feat'}, dimensions={0} | all-to-all | bytes 655360 | tf_op jit(solution)/shard_map/all_to_all | solution.py:325
  80.0 0.7 shard_map.80
  (1 shorter events, 0.0 us)
Async XLA Ops:
  0.0 13.8 %copy-start.1 = (bf16[4,1024]{1,0:T(4,128)(2,1)S(1)}, bf16[4,1024]{1,0:T(4,128)(2,1)}, u32[]{:S(2)}) copy-start(bf16[4,1024]{1,0:T(4,128)(2,1)} %param.13) | copy-start | bytes 24580
  1.7 6.8 %collective-permute-start = (f32[32,768]{1,0:T(8,128)S(1)}, f32[32,768]{1,0:T(8,128)S(1)}, u32[]{:S(2)}, u32[]{:S(2)}) collective-permute-start(f32[32,768]{1,0:T(8,128)S(1)} %shard_map.73.own_ref), channel_id=1, source_target_pairs={{0,1},{1,0},{2,3},{3,2},{4,5},{5,4},{6,7},{7,6},{8,9},{9,8},{10,11... | collective-permute-start | bytes 294920 | tf_op jit(solution)/shard_map/ppermute | solution.py:283
  9.3 10.7 %all-to-all-start = ((f32[4,32,768]{2,1,0:T(8,128)}), f32[4,32,768]{2,1,0:T(8,128)S(1)}, u32[]{:S(2)}, u32[]{:S(2)}) async-start(f32[4,32,768]{2,1,0:T(8,128)} %shard_map.74), calls=%async_computation | async-start | bytes 786432 | tf_op jit(solution)/shard_map/all_to_all | solution.py:292
  20.6 22.2 %all-to-all-start.2 = ((bf16[16,8,512]{2,1,0:T(8,128)(2,1)}), bf16[16,8,512]{2,1,0:T(8,128)(2,1)S(1)}, u32[]{:S(2)}, u32[]{:S(2)}) async-start(bf16[16,8,512]{2,1,0:T(8,128)(2,1)} %broadcast_in_dim.12), calls=%async_computation.2 | async-start | bytes 262144 | tf_op jit(solution)/shard_map/all_to_all | solution.py:249
  32.7 3.2 %copy-start = (s32[32]{0:T(128)S(1)}, s32[32]{0:T(128)}, u32[]{:S(2)}) copy-start(s32[32]{0:T(128)} %seq_ref.1) | copy-start | bytes 388
  42.9 24.2 %all-to-all-start.1 = ((bf16[8,256,128]{2,1,0:T(8,128)(2,1)}), bf16[8,256,128]{2,1,0:T(8,128)(2,1)S(1)}, u32[]{:S(2)}, u32[]{:S(2)}) async-start(bf16[8,256,128]{2,1,0:T(8,128)(2,1)} %shard_map.76), calls=%async_computation.1 | async-start | bytes 1048576 | tf_op jit(solution)/shard_map/all_to_all | solution.py:316
  46.4 11.0 %collective-permute-start.1 = (bf16[128,512]{1,0:T(8,128)(2,1)S(1)}, bf16[128,512]{1,0:T(8,128)(2,1)S(1)}, u32[]{:S(2)}, u32[]{:S(2)}) collective-permute-start(bf16[128,512]{1,0:T(8,128)(2,1)S(1)} %bitcast.6), channel_id=1, source_target_pairs={{0,256},{8,264},{16,272},{24,280},{32,288},{40,296},{48,304},{56,3... | collective-permute-start | bytes 393224 | tf_op jit(solution)/shard_map/ppermute | solution.py:251
  57.4 8.9 %collective-permute-start.2 = (bf16[256,512]{1,0:T(8,128)(2,1)S(1)}, bf16[256,512]{1,0:T(8,128)(2,1)S(1)}, u32[]{:S(2)}, u32[]{:S(2)}) collective-permute-start(bf16[256,512]{1,0:T(8,128)(2,1)S(1)} %shard_map.77.half_ref), channel_id=1, source_target_pairs={{0,8},{8,0},{16,24},{24,16},{32,40},{40,32},{48,56},{56,48},{64,72... | collective-permute-start | bytes 786440 | tf_op jit(solution)/shard_map/ppermute | solution.py:259

commit v15 on v14

--- a/solution.py
+++ b/solution.py
@@ -162,18 +162,11 @@
         store.wait()
 
 
-def join_kernel(near_ref, far_ref, out_ref):
-    rows = near_ref.shape[0]
-    out_ref[:rows] = near_ref[...]
-    out_ref[rows:] = far_ref[...]
-
-
 def valid_kernel(own_ref, half_ref, other_ref, out_ref, squares_ref):
     count = half_ref.shape[0]
     place = lax.broadcasted_iota(jnp.int32, (8, 2 * count), 1)
-    core = ((place >> 8) ^ own_ref[0]) & 1
-    far = ((place >> 7) ^ (own_ref[0] >> 5)) & 1
-    index = (far << 7) | (((place >> 3) & 15) << 3) | (core << 2) | ((place >> 1) & 3)
+    far = ((place >> 8) ^ (own_ref[0] >> 5)) & 1
+    index = (far << 7) | (((place >> 3) & 31) << 2) | ((place >> 1) & 3)
     row = lax.broadcasted_iota(jnp.int32, (count, 2 * count), 0)
     squares = jnp.zeros((count, 128), F32)
     for h in range(2):
@@ -242,21 +235,13 @@
     valid_count = valid_grads.shape[0] * groups
     scaling = math.sqrt(kl * proj)
 
+    far_bit = groups // 2
     own_valid = valid_grads.reshape(-1, owned, 2, 8).transpose(0, 3, 2, 1).reshape(1, -1, owned * proj // 2)
-    own_valid = jnp.broadcast_to(own_valid, (groups // 4,) + own_valid.shape[1:])
-    far_bit = groups // 2
-    members = [[y * far_bit + i * 2 + c for i in range(far_bit // 2)] for y in range(2) for c in range(2)]
+    own_valid = jnp.broadcast_to(own_valid, (far_bit,) + own_valid.shape[1:])
+    members = [[y * far_bit + i for i in range(far_bit)] for y in range(2)]
     near = lax.all_to_all(own_valid, "ex", 0, 0, tiled=True, axis_index_groups=members)
-    near = near.reshape(valid_count // 2, owned * proj // 2)
+    near = near.reshape(valid_count, owned * proj // 2)
     far = lax.ppermute(near, "ex", [(i, i ^ far_bit) for i in range(groups)])
-    half = call(
-        join_kernel,
-        jax.ShapeDtypeStruct((valid_count, owned * proj // 2), BF16),
-        0,
-        2 * valid_count * owned * proj,
-        args=(on_chip(near), on_chip(far)),
-    )
-    other = lax.ppermute(half, "ex", [(i, i ^ 1) for i in range(groups)])
     own_group = jnp.full((1,), lax.axis_index("ex"), jnp.int32)
     valid, valid_squares = call(
         valid_kernel,
@@ -267,7 +252,7 @@
         2 * valid_count * valid_count * owned * proj,
         2 * valid_count * owned * proj * 2,
         smem=1,
-        args=(own_group, on_chip(half), on_chip(other)),
+        args=(own_group, on_chip(near), on_chip(far)),
     )
 
     right_in = (proj_inputs.reshape(layers, tokens, inputs), frozen_adapter, right_factor.swapaxes(1, 2))

time: 81.2 us -> 86.8 us (1.069)
  waiting for transfers between devices: 20.4 us -> 31.1 us
  starting transfers between devices: 37.4 us -> 33.2 us
  blocking collectives: 12.6 us -> 11.5 us
    ppermute x1, waiting for transfers between devices: 6.26 us -> 14.8 us  [scores_of(): far = lax.ppermute(near, 'ex', [(i, i ^ far_bit) for i in range(groups)])]
    ppermute x1 -> x0, starting transfers between devices: 7.74 us -> none  [scores_of(): other = lax.ppermute(half, 'ex', [(i, i ^ 1) for i in range(groups)])]
    all_to_all x1, starting transfers between devices: 12 us -> 15.6 us  [scores_of(): lax.all_to_all(own_valid, 'ex', 0, 0, tiled=True, axis_index_groups=members)]
    all_to_all x1, waiting for transfers between devices: 5.12 us -> 8.5 us  [scores_of(): lax.all_to_all(own_valid, 'ex', 0, 0, tiled=True, axis_index_groups=members)]
    ppermute x1 -> x0, waiting for transfers between devices: 1.14 us -> none  [scores_of(): other = lax.ppermute(half, 'ex', [(i, i ^ 1) for i in range(groups)])]
    all_to_all x1, blocking collectives: 12.6 us -> 11.5 us  [scores_of(): products = lax.all_to_all(products, 'feat', 0, 0, tiled=True)]
    pallas_call x8 -> x7, Pallas kernels: 9.34 us -> 9.32 us  [call(): pl.pallas_call(kernel, out_shape=out_shape, in_specs=specs, out_specs=out...]
  transfers between devices with their start and end apart: 6 -> 5, of which waited for: 5 -> 4; matrix products, arithmetic and copies ran while one was open for 0% -> 0% of each run, Pallas kernels for 7% -> 7%
where the time goes in v15:
time: 86.8 us; the launch traced here: 86.3 us
  starting transfers between devices  33.2 us (38%)
  waiting for transfers between devices  31.1 us (36%)
  blocking collectives  11.5 us (13%)
  Pallas kernels  9.32 us (11%)
  local copies, waits for them, and re-layouts  1.1 us (1%)
    all_to_all x1, starting transfers between devices, scores_of(): lax.all_to_all(own_valid, 'ex', 0, 0, tiled=True, axis_index_groups=members)  15.6 us
    ppermute x1, waiting for transfers between devices, scores_of(): far = lax.ppermute(near, 'ex', [(i, i ^ far_bit) for i in range(groups)])  14.8 us
    all_to_all x1, blocking collectives, scores_of(): products = lax.all_to_all(products, 'feat', 0, 0, tiled=True)  11.5 us
    pallas_call x7, Pallas kernels, call(): pl.pallas_call(kernel, out_shape=out_shape, in_specs=specs, out_specs=out...  9.32 us
    all_to_all x1, waiting for transfers between devices, scores_of(): lax.all_to_all(own_valid, 'ex', 0, 0, tiled=True, axis_index_groups=members)  8.5 us
    all_to_all x1, waiting for transfers between devices, scores_of(): lax.all_to_all(right_parts, 'feat', 0, 0, tiled=True, axis_index_groups=a...  5.84 us
    ppermute x1, starting transfers between devices, scores_of(): lax.ppermute(right_parts, 'feat', [(i, i ^ 1) for i in range(peers)])  4.82 us
    ppermute x1, starting transfers between devices, scores_of(): far = lax.ppermute(near, 'ex', [(i, i ^ far_bit) for i in range(groups)])  4.76 us
  transfers between devices with their start and end apart: 5, of which 4 were waited for; matrix products, arithmetic and copies ran while one was open for 0% of the time, Pallas kernels for 7%

profile of v15, /device:TPU:1, one launch (start us, length us, event | category | flops | bytes accessed | tf_op | source)
XLA Modules:
  0.0 86.3 jit_solution(5484942908874260142)
XLA Ops:
  0.0 0.0 copy-start.1
  0.0 1.7 %shard_map.73.own_ref = f32[32,768]{1,0:T(8,128)S(1)} custom-call(bf16[2,768,256]{2,1,0:T(8,128)(2,1)} %bitcast.9, bf16[2,128,256]{2,1,0:T(8,128)(2,1)} %a_hbm.1, bf16[2,16,128]{2,1,0:T(8,128)(2,1)} %bitcast.11), custom_call_target="tpu_custom_call" | custom-call | flops 201326592 | bytes 786432 | tf_op jit(solution)/shard_map/pallas_call | solution.py:50
  1.7 4.8 %collective-permute-start = (f32[32,768]{1,0:T(8,128)S(1)}, f32[32,768]{1,0:T(8,128)S(1)}, u32[]{:S(2)}, u32[]{:S(2)}) collective-permute-start(f32[32,768]{1,0:T(8,128)S(1)} %shard_map.73.own_ref), channel_id=1, source_target_pairs={{0,1},{1,0},{2,3},{3,2},{4,5},{5,4},{6,7},{7,6},{8,9},{9,8},{10,11... | collective-permute-start | bytes 294920 | tf_op jit(solution)/shard_map/ppermute | solution.py:268
  6.5 2.0 %collective-permute-done.other_ref = f32[32,768]{1,0:T(8,128)S(1)} collective-permute-done((f32[32,768]{1,0:T(8,128)S(1)}, f32[32,768]{1,0:T(8,128)S(1)}, u32[]{:S(2)}, u32[]{:S(2)}) %collective-permute-start) | collective-permute-done | bytes 98336 | tf_op jit(solution)/shard_map/ppermute | solution.py:268
  8.5 0.8 shard_map.74
  9.3 4.5 %all-to-all-start = ((f32[4,32,768]{2,1,0:T(8,128)}), f32[4,32,768]{2,1,0:T(8,128)S(1)}, u32[]{:S(2)}, u32[]{:S(2)}) async-start(f32[4,32,768]{2,1,0:T(8,128)} %shard_map.74), calls=%async_computation | async-start | bytes 786432 | tf_op jit(solution)/shard_map/all_to_all | solution.py:277
  13.8 0.0 copy-done.1
  13.8 0.2 reshape.16
  14.0 0.1 copy.8
  14.0 0.1 broadcast_in_dim.11
  14.2 5.8 %all-to-all-done.rr_ref = f32[4,32,768]{2,1,0:T(8,128)S(1)} async-done(((f32[4,32,768]{2,1,0:T(8,128)}), f32[4,32,768]{2,1,0:T(8,128)S(1)}, u32[]{:S(2)}, u32[]{:S(2)}) %all-to-all-start) | async-done | bytes 393248 | tf_op jit(solution)/shard_map/all_to_all | solution.py:277
  20.0 0.7 broadcast_in_dim.12
  20.7 15.6 %all-to-all-start.2 = ((bf16[32,8,512]{2,1,0:T(8,128)(2,1)}), bf16[32,8,512]{2,1,0:T(8,128)(2,1)S(1)}, u32[]{:S(2)}, u32[]{:S(2)}) async-start(bf16[32,8,512]{2,1,0:T(8,128)(2,1)} %broadcast_in_dim.12), calls=%async_computation.2 | async-start | bytes 524288 | tf_op jit(solution)/shard_map/all_to_all | solution.py:242
  36.3 0.0 copy-start
  36.3 3.2 %shard_map.75.left_ref = bf16[2,768,512]{2,1,0:T(8,128)(2,1)S(1)} custom-call(bf16[2,768,512]{2,1,0:T(8,128)(2,1)} %bitcast.8, bf16[2,512,512]{2,1,0:T(8,128)(2,1)} %l_hbm.1), custom_call_target="tpu_custom_call" | custom-call | flops 805306368 | bytes 4194304 | tf_op jit(solution)/shard_map/pallas_call | solution.py:50
  39.5 0.0 copy-done
  39.6 1.8 %shard_map.76 = bf16[8,256,128]{2,1,0:T(8,128)(2,1)} custom-call(s32[32]{0:T(128)S(1)} %copy-done, f32[4,32,768]{2,1,0:T(8,128)S(1)} %all-to-all-done.rr_ref, bf16[2,768,512]{2,1,0:T(8,128)(2,1)S(1)} %shard_map.75.left_ref), custom_call_target="tpu_custom_call" | custom-call | flops 402653184 | bytes 3145728 | tf_op jit(solution)/shard_map/pallas_call | solution.py:50
  41.4 8.5 %all-to-all-done.2 = bf16[32,8,512]{2,1,0:T(8,128)(2,1)S(1)} async-done(((bf16[32,8,512]{2,1,0:T(8,128)(2,1)}), bf16[32,8,512]{2,1,0:T(8,128)(2,1)S(1)}, u32[]{:S(2)}, u32[]{:S(2)}) %all-to-all-start.2) | async-done | bytes 262176 | tf_op jit(solution)/shard_map/all_to_all | solution.py:242
  49.9 3.5 %all-to-all-start.1 = ((bf16[8,256,128]{2,1,0:T(8,128)(2,1)}), bf16[8,256,128]{2,1,0:T(8,128)(2,1)S(1)}, u32[]{:S(2)}, u32[]{:S(2)}) async-start(bf16[8,256,128]{2,1,0:T(8,128)(2,1)} %shard_map.76), calls=%async_computation.1 | async-start | bytes 1048576 | tf_op jit(solution)/shard_map/all_to_all | solution.py:301
  53.4 4.8 %collective-permute-start.1 = (bf16[256,512]{1,0:T(8,128)(2,1)S(1)}, bf16[256,512]{1,0:T(8,128)(2,1)S(1)}, u32[]{:S(2)}, u32[]{:S(2)}) collective-permute-start(bf16[256,512]{1,0:T(8,128)(2,1)S(1)} %bitcast.6), channel_id=1, source_target_pairs={{0,256},{8,264},{16,272},{24,280},{32,288},{40,296},{48,304},{56,3... | collective-permute-start | bytes 786440 | tf_op jit(solution)/shard_map/ppermute | solution.py:244
  58.2 14.8 %collective-permute-done.1.other_ref = bf16[256,512]{1,0:T(8,128)(2,1)S(1)} collective-permute-done((bf16[256,512]{1,0:T(8,128)(2,1)S(1)}, bf16[256,512]{1,0:T(8,128)(2,1)S(1)}, u32[]{:S(2)}, u32[]{:S(2)}) %collective-permute-start.1) | collective-permute-done | bytes 262176 | tf_op jit(solution)/shard_map/ppermute | solution.py:244
  72.9 0.8 shard_map.77
  73.7 0.0 all-to-all-done.1.part_ref
  73.7 0.4 shard_map.78
  74.1 11.5 %all_to_all.20.part_ref = f32[8,40,256]{2,1,0:T(8,128)S(1)} all-to-all(f32[8,40,256]{2,1,0:T(8,128)S(1)} %shard_map.78), channel_id=1, replica_groups=mesh['ex'=64,'feat'=8] {'feat'}, dimensions={0} | all-to-all | bytes 655360 | tf_op jit(solution)/shard_map/all_to_all | solution.py:310
  85.6 0.7 shard_map.79
Async XLA Ops:
  0.0 13.8 %copy-start.1 = (bf16[4,1024]{1,0:T(4,128)(2,1)S(1)}, bf16[4,1024]{1,0:T(4,128)(2,1)}, u32[]{:S(2)}) copy-start(bf16[4,1024]{1,0:T(4,128)(2,1)} %param.13) | copy-start | bytes 24580
  1.7 6.8 %collective-permute-start = (f32[32,768]{1,0:T(8,128)S(1)}, f32[32,768]{1,0:T(8,128)S(1)}, u32[]{:S(2)}, u32[]{:S(2)}) collective-permute-start(f32[32,768]{1,0:T(8,128)S(1)} %shard_map.73.own_ref), channel_id=1, source_target_pairs={{0,1},{1,0},{2,3},{3,2},{4,5},{5,4},{6,7},{7,6},{8,9},{9,8},{10,11... | collective-permute-start | bytes 294920 | tf_op jit(solution)/shard_map/ppermute | solution.py:268
  9.3 10.7 %all-to-all-start = ((f32[4,32,768]{2,1,0:T(8,128)}), f32[4,32,768]{2,1,0:T(8,128)S(1)}, u32[]{:S(2)}, u32[]{:S(2)}) async-start(f32[4,32,768]{2,1,0:T(8,128)} %shard_map.74), calls=%async_computation | async-start | bytes 786432 | tf_op jit(solution)/shard_map/all_to_all | solution.py:277
  20.7 29.2 %all-to-all-start.2 = ((bf16[32,8,512]{2,1,0:T(8,128)(2,1)}), bf16[32,8,512]{2,1,0:T(8,128)(2,1)S(1)}, u32[]{:S(2)}, u32[]{:S(2)}) async-start(bf16[32,8,512]{2,1,0:T(8,128)(2,1)} %broadcast_in_dim.12), calls=%async_computation.2 | async-start | bytes 524288 | tf_op jit(solution)/shard_map/all_to_all | solution.py:242
  36.3 3.2 %copy-start = (s32[32]{0:T(128)S(1)}, s32[32]{0:T(128)}, u32[]{:S(2)}) copy-start(s32[32]{0:T(128)} %seq_ref.1) | copy-start | bytes 388
  49.9 23.8 %all-to-all-start.1 = ((bf16[8,256,128]{2,1,0:T(8,128)(2,1)}), bf16[8,256,128]{2,1,0:T(8,128)(2,1)S(1)}, u32[]{:S(2)}, u32[]{:S(2)}) async-start(bf16[8,256,128]{2,1,0:T(8,128)(2,1)} %shard_map.76), calls=%async_computation.1 | async-start | bytes 1048576 | tf_op jit(solution)/shard_map/all_to_all | solution.py:301
  53.4 19.5 %collective-permute-start.1 = (bf16[256,512]{1,0:T(8,128)(2,1)S(1)}, bf16[256,512]{1,0:T(8,128)(2,1)S(1)}, u32[]{:S(2)}, u32[]{:S(2)}) collective-permute-start(bf16[256,512]{1,0:T(8,128)(2,1)S(1)} %bitcast.6), channel_id=1, source_target_pairs={{0,256},{8,264},{16,272},{24,280},{32,288},{40,296},{48,304},{56,3... | collective-permute-start | bytes 786440 | tf_op jit(solution)/shard_map/ppermute | solution.py:244

commit v16 on v14

--- a/solution.py
+++ b/solution.py
@@ -162,6 +162,14 @@
         store.wait()
 
 
+def spread_kernel(own_ref, out_hbm, sems):
+    copies = [pltpu.make_async_copy(own_ref, out_hbm.at[n], sems.at[n]) for n in range(out_hbm.shape[0])]
+    for copy in copies:
+        copy.start()
+    for copy in copies:
+        copy.wait()
+
+
 def join_kernel(near_ref, far_ref, out_ref):
     rows = near_ref.shape[0]
     out_ref[:rows] = near_ref[...]
@@ -242,8 +250,17 @@
     valid_count = valid_grads.shape[0] * groups
     scaling = math.sqrt(kl * proj)
 
-    own_valid = valid_grads.reshape(-1, owned, 2, 8).transpose(0, 3, 2, 1).reshape(1, -1, owned * proj // 2)
-    own_valid = jnp.broadcast_to(own_valid, (groups // 4,) + own_valid.shape[1:])
+    own_valid = valid_grads.reshape(-1, owned, 2, 8).transpose(0, 3, 2, 1).reshape(-1, owned * proj // 2)
+    count = groups // 4
+    (own_valid,) = call(
+        spread_kernel,
+        (pltpu.HBM((count,) + own_valid.shape, BF16),),
+        0,
+        valid_grads.size * 2 * count,
+        scratch=(pltpu.SemaphoreType.DMA((count,)),),
+        args=(on_chip(own_valid),),
+        hbm_out=(0,),
+    )
     far_bit = groups // 2
     members = [[y * far_bit + i * 2 + c for i in range(far_bit // 2)] for y in range(2) for c in range(2)]
     near = lax.all_to_all(own_valid, "ex", 0, 0, tiled=True, axis_index_groups=members)

time: 81.2 us -> 80.6 us (level)
  waiting for transfers between devices: 20.4 us -> 19.5 us
    pallas_call x8 -> x9, Pallas kernels: 9.34 us -> 10.1 us  [call(): pl.pallas_call(kernel, out_shape=out_shape, in_specs=specs, out_specs=out...]
  transfers between devices with their start and end apart: 6 -> 6, of which waited for: 5 -> 5; matrix products, arithmetic and copies ran while one was open for 0% -> 0% of each run, Pallas kernels for 7% -> 8%
where the time goes in v16:
time: 80.6 us; the launch traced here: 80.1 us
  starting transfers between devices  37.4 us (46%)
  waiting for transfers between devices  19.5 us (24%)
  blocking collectives  12.6 us (16%)
  Pallas kernels  10.1 us (13%)
    all_to_all x1, blocking collectives, scores_of(): products = lax.all_to_all(products, 'feat', 0, 0, tiled=True)  12.6 us
    all_to_all x1, starting transfers between devices, scores_of(): lax.all_to_all(own_valid, 'ex', 0, 0, tiled=True, axis_index_groups=members)  12 us
    pallas_call x9, Pallas kernels, call(): pl.pallas_call(kernel, out_shape=out_shape, in_specs=specs, out_specs=out...  10.1 us
    ppermute x1, starting transfers between devices, scores_of(): other = lax.ppermute(half, 'ex', [(i, i ^ 1) for i in range(groups)])  7.74 us
    ppermute x1, waiting for transfers between devices, scores_of(): far = lax.ppermute(near, 'ex', [(i, i ^ far_bit) for i in range(groups)])  6.26 us
    all_to_all x1, waiting for transfers between devices, scores_of(): lax.all_to_all(own_valid, 'ex', 0, 0, tiled=True, axis_index_groups=members)  5.13 us
    all_to_all x1, waiting for transfers between devices, scores_of(): lax.all_to_all(right_parts, 'feat', 0, 0, tiled=True, axis_index_groups=a...  5.03 us
    ppermute x1, starting transfers between devices, scores_of(): lax.ppermute(right_parts, 'feat', [(i, i ^ 1) for i in range(peers)])  4.82 us
  transfers between devices with their start and end apart: 6, of which 5 were waited for; matrix products, arithmetic and copies ran while one was open for 0% of the time, Pallas kernels for 8%

profile of v16, /device:TPU:1, one launch (start us, length us, event | category | flops | bytes accessed | tf_op | source)
XLA Modules:
  0.0 80.1 jit_solution(3654201506515193735)
XLA Ops:
  0.0 0.0 copy-start.1
  0.0 1.7 %shard_map.73.own_ref = f32[32,768]{1,0:T(8,128)S(1)} custom-call(bf16[2,768,256]{2,1,0:T(8,128)(2,1)} %bitcast.9, bf16[2,128,256]{2,1,0:T(8,128)(2,1)} %a_hbm.1, bf16[2,16,128]{2,1,0:T(8,128)(2,1)} %bitcast.11), custom_call_target="tpu_custom_call" | custom-call | flops 201326592 | bytes 786432 | tf_op jit(solution)/shard_map/pallas_call | solution.py:50
  1.7 4.8 %collective-permute-start = (f32[32,768]{1,0:T(8,128)S(1)}, f32[32,768]{1,0:T(8,128)S(1)}, u32[]{:S(2)}, u32[]{:S(2)}) collective-permute-start(f32[32,768]{1,0:T(8,128)S(1)} %shard_map.73.own_ref), channel_id=1, source_target_pairs={{0,1},{1,0},{2,3},{3,2},{4,5},{5,4},{6,7},{7,6},{8,9},{9,8},{10,11... | collective-permute-start | bytes 294920 | tf_op jit(solution)/shard_map/ppermute | solution.py:300
  6.5 2.0 %collective-permute-done.other_ref = f32[32,768]{1,0:T(8,128)S(1)} collective-permute-done((f32[32,768]{1,0:T(8,128)S(1)}, f32[32,768]{1,0:T(8,128)S(1)}, u32[]{:S(2)}, u32[]{:S(2)}) %collective-permute-start) | collective-permute-done | bytes 98336 | tf_op jit(solution)/shard_map/ppermute | solution.py:300
  8.5 0.8 shard_map.74
  9.3 4.5 %all-to-all-start = ((f32[4,32,768]{2,1,0:T(8,128)}), f32[4,32,768]{2,1,0:T(8,128)S(1)}, u32[]{:S(2)}, u32[]{:S(2)}) async-start(f32[4,32,768]{2,1,0:T(8,128)} %shard_map.74), calls=%async_computation | async-start | bytes 786432 | tf_op jit(solution)/shard_map/all_to_all | solution.py:309
  13.8 0.0 copy-done.1
  13.8 0.2 reshape.17
  14.0 0.1 copy.9
  14.0 0.1 reshape.18.own_ref
  14.1 0.8 %shard_map.77 = bf16[16,8,512]{2,1,0:T(8,128)(2,1)} custom-call(bf16[8,512]{1,0:T(8,128)(2,1)S(1)} %reshape.18.own_ref), custom_call_target="tpu_custom_call" | custom-call | bytes 131072 | tf_op jit(solution)/shard_map/pallas_call | solution.py:50
  15.0 5.0 %all-to-all-done.rr_ref = f32[4,32,768]{2,1,0:T(8,128)S(1)} async-done(((f32[4,32,768]{2,1,0:T(8,128)}), f32[4,32,768]{2,1,0:T(8,128)S(1)}, u32[]{:S(2)}, u32[]{:S(2)}) %all-to-all-start) | async-done | bytes 393248 | tf_op jit(solution)/shard_map/all_to_all | solution.py:309
  20.0 12.0 %all-to-all-start.2 = ((bf16[16,8,512]{2,1,0:T(8,128)(2,1)}), bf16[16,8,512]{2,1,0:T(8,128)(2,1)S(1)}, u32[]{:S(2)}, u32[]{:S(2)}) async-start(bf16[16,8,512]{2,1,0:T(8,128)(2,1)} %shard_map.77), calls=%async_computation.2 | async-start | bytes 262144 | tf_op jit(solution)/shard_map/all_to_all | solution.py:266
  32.0 0.0 copy-start
  32.0 3.2 %shard_map.75.left_ref = bf16[2,768,512]{2,1,0:T(8,128)(2,1)S(1)} custom-call(bf16[2,768,512]{2,1,0:T(8,128)(2,1)} %bitcast.8, bf16[2,512,512]{2,1,0:T(8,128)(2,1)} %l_hbm.1), custom_call_target="tpu_custom_call" | custom-call | flops 805306368 | bytes 4194304 | tf_op jit(solution)/shard_map/pallas_call | solution.py:50
  35.3 0.0 copy-done
  35.3 1.8 %shard_map.76 = bf16[8,256,128]{2,1,0:T(8,128)(2,1)} custom-call(s32[32]{0:T(128)S(1)} %copy-done, f32[4,32,768]{2,1,0:T(8,128)S(1)} %all-to-all-done.rr_ref, bf16[2,768,512]{2,1,0:T(8,128)(2,1)S(1)} %shard_map.75.left_ref), custom_call_target="tpu_custom_call" | custom-call | flops 402653184 | bytes 3145728 | tf_op jit(solution)/shard_map/pallas_call | solution.py:50
  37.1 5.1 %all-to-all-done.2 = bf16[16,8,512]{2,1,0:T(8,128)(2,1)S(1)} async-done(((bf16[16,8,512]{2,1,0:T(8,128)(2,1)}), bf16[16,8,512]{2,1,0:T(8,128)(2,1)S(1)}, u32[]{:S(2)}, u32[]{:S(2)}) %all-to-all-start.2) | async-done | bytes 131104 | tf_op jit(solution)/shard_map/all_to_all | solution.py:266
  42.2 3.5 %all-to-all-start.1 = ((bf16[8,256,128]{2,1,0:T(8,128)(2,1)}), bf16[8,256,128]{2,1,0:T(8,128)(2,1)S(1)}, u32[]{:S(2)}, u32[]{:S(2)}) async-start(bf16[8,256,128]{2,1,0:T(8,128)(2,1)} %shard_map.76), calls=%async_computation.1 | async-start | bytes 1048576 | tf_op jit(solution)/shard_map/all_to_all | solution.py:333
  45.7 4.8 %collective-permute-start.1 = (bf16[128,512]{1,0:T(8,128)(2,1)S(1)}, bf16[128,512]{1,0:T(8,128)(2,1)S(1)}, u32[]{:S(2)}, u32[]{:S(2)}) collective-permute-start(bf16[128,512]{1,0:T(8,128)(2,1)S(1)} %bitcast.6), channel_id=1, source_target_pairs={{0,256},{8,264},{16,272},{24,280},{32,288},{40,296},{48,304},{56,3... | collective-permute-start | bytes 393224 | tf_op jit(solution)/shard_map/ppermute | solution.py:268
  50.5 6.3 %collective-permute-done.1.far_ref = bf16[128,512]{1,0:T(8,128)(2,1)S(1)} collective-permute-done((bf16[128,512]{1,0:T(8,128)(2,1)S(1)}, bf16[128,512]{1,0:T(8,128)(2,1)S(1)}, u32[]{:S(2)}, u32[]{:S(2)}) %collective-permute-start.1) | collective-permute-done | bytes 131104 | tf_op jit(solution)/shard_map/ppermute | solution.py:268
  56.8 7.7 %collective-permute-start.2 = (bf16[256,512]{1,0:T(8,128)(2,1)S(1)}, bf16[256,512]{1,0:T(8,128)(2,1)S(1)}, u32[]{:S(2)}, u32[]{:S(2)}) collective-permute-start(bf16[256,512]{1,0:T(8,128)(2,1)S(1)} %shard_map.78.half_ref), channel_id=1, source_target_pairs={{0,8},{8,0},{16,24},{24,16},{32,40},{40,32},{48,56},{56,48},{64,72... | collective-permute-start | bytes 786440 | tf_op jit(solution)/shard_map/ppermute | solution.py:276
  64.5 1.1 %collective-permute-done.2.other_ref = bf16[256,512]{1,0:T(8,128)(2,1)S(1)} collective-permute-done((bf16[256,512]{1,0:T(8,128)(2,1)S(1)}, bf16[256,512]{1,0:T(8,128)(2,1)S(1)}, u32[]{:S(2)}, u32[]{:S(2)}) %collective-permute-start.2) | collective-permute-done | bytes 262176 | tf_op jit(solution)/shard_map/ppermute | solution.py:276
  65.7 0.8 shard_map.79
  66.4 0.0 all-to-all-done.1.part_ref
  66.4 0.4 shard_map.80
  66.8 12.6 %all_to_all.20.part_ref = f32[8,40,256]{2,1,0:T(8,128)S(1)} all-to-all(f32[8,40,256]{2,1,0:T(8,128)S(1)} %shard_map.80), channel_id=1, replica_groups=mesh['ex'=64,'feat'=8] {'feat'}, dimensions={0} | all-to-all | bytes 655360 | tf_op jit(solution)/shard_map/all_to_all | solution.py:342
  79.4 0.7 shard_map.81
  (1 shorter events, 0.0 us)
Async XLA Ops:
  0.0 13.8 %copy-start.1 = (bf16[4,1024]{1,0:T(4,128)(2,1)S(1)}, bf16[4,1024]{1,0:T(4,128)(2,1)}, u32[]{:S(2)}) copy-start(bf16[4,1024]{1,0:T(4,128)(2,1)} %param.13) | copy-start | bytes 24580
  1.7 6.8 %collective-permute-start = (f32[32,768]{1,0:T(8,128)S(1)}, f32[32,768]{1,0:T(8,128)S(1)}, u32[]{:S(2)}, u32[]{:S(2)}) collective-permute-start(f32[32,768]{1,0:T(8,128)S(1)} %shard_map.73.own_ref), channel_id=1, source_target_pairs={{0,1},{1,0},{2,3},{3,2},{4,5},{5,4},{6,7},{7,6},{8,9},{9,8},{10,11... | collective-permute-start | bytes 294920 | tf_op jit(solution)/shard_map/ppermute | solution.py:300
  9.3 10.7 %all-to-all-start = ((f32[4,32,768]{2,1,0:T(8,128)}), f32[4,32,768]{2,1,0:T(8,128)S(1)}, u32[]{:S(2)}, u32[]{:S(2)}) async-start(f32[4,32,768]{2,1,0:T(8,128)} %shard_map.74), calls=%async_computation | async-start | bytes 786432 | tf_op jit(solution)/shard_map/all_to_all | solution.py:309
  20.0 22.2 %all-to-all-start.2 = ((bf16[16,8,512]{2,1,0:T(8,128)(2,1)}), bf16[16,8,512]{2,1,0:T(8,128)(2,1)S(1)}, u32[]{:S(2)}, u32[]{:S(2)}) async-start(bf16[16,8,512]{2,1,0:T(8,128)(2,1)} %shard_map.77), calls=%async_computation.2 | async-start | bytes 262144 | tf_op jit(solution)/shard_map/all_to_all | solution.py:266
  32.0 3.2 %copy-start = (s32[32]{0:T(128)S(1)}, s32[32]{0:T(128)}, u32[]{:S(2)}) copy-start(s32[32]{0:T(128)} %seq_ref.1) | copy-start | bytes 388
  42.2 24.2 %all-to-all-start.1 = ((bf16[8,256,128]{2,1,0:T(8,128)(2,1)}), bf16[8,256,128]{2,1,0:T(8,128)(2,1)S(1)}, u32[]{:S(2)}, u32[]{:S(2)}) async-start(bf16[8,256,128]{2,1,0:T(8,128)(2,1)} %shard_map.76), calls=%async_computation.1 | async-start | bytes 1048576 | tf_op jit(solution)/shard_map/all_to_all | solution.py:333
  45.7 11.0 %collective-permute-start.1 = (bf16[128,512]{1,0:T(8,128)(2,1)S(1)}, bf16[128,512]{1,0:T(8,128)(2,1)S(1)}, u32[]{:S(2)}, u32[]{:S(2)}) collective-permute-start(bf16[128,512]{1,0:T(8,128)(2,1)S(1)} %bitcast.6), channel_id=1, source_target_pairs={{0,256},{8,264},{16,272},{24,280},{32,288},{40,296},{48,304},{56,3... | collective-permute-start | bytes 393224 | tf_op jit(solution)/shard_map/ppermute | solution.py:268
  56.8 8.9 %collective-permute-start.2 = (bf16[256,512]{1,0:T(8,128)(2,1)S(1)}, bf16[256,512]{1,0:T(8,128)(2,1)S(1)}, u32[]{:S(2)}, u32[]{:S(2)}) collective-permute-start(bf16[256,512]{1,0:T(8,128)(2,1)S(1)} %shard_map.78.half_ref), channel_id=1, source_target_pairs={{0,8},{8,0},{16,24},{24,16},{32,40},{40,32},{48,56},{56,48},{64,72... | collective-permute-start | bytes 786440 | tf_op jit(solution)/shard_map/ppermute | solution.py:276
